TPU v7x, 32 devices: a whole 2x2x4 slice. The times are simulated.
32 devices in a mesh: fsdp: 16 (over z, y, core), seq: 2 (over x).
Axes of the slice: x: 2, y: 2, z: 4, core: 2. Of those that a mesh axis runs over, the one named last changes fastest.
Arguments:
- block_input: bfloat16 [2, 16, 1024, 1024], P(None, 'fsdp', 'seq'), may hold values from -6 to 6
- output_grad: bfloat16 [2, 16, 1024, 1024], P(None, 'fsdp', 'seq'), may hold values from -6 to 6
- adapter_ids: int32 [2, 16], P(None, 'fsdp'), may hold values from 0 to 7
- in_weight: bfloat16 [1024, 3072], P('fsdp'), may hold values from -0.1875 to 0.1875
- out_weight: bfloat16 [1024, 1024], P('fsdp'), may hold values from -0.1875 to 0.1875
- gate_weight: bfloat16 [1024, 4608], P('fsdp'), may hold values from -0.1875 to 0.1875
- up_weight: bfloat16 [1024, 4608], P('fsdp'), may hold values from -0.1875 to 0.1875
- down_weight: bfloat16 [4608, 1024], P('fsdp'), may hold values from -0.09375 to 0.09375
- conv_weight: bfloat16 [3, 1024], replicated, may hold values from -3.5 to 3.5
- first_gain: bfloat16 [1024], replicated, may hold values from 0.099609375 to 1.8984375
- second_gain: bfloat16 [1024], replicated, may hold values from 0.099609375 to 1.8984375
- infirst_adapter: bfloat16 [1024, 128], replicated, may hold values from -0.1875 to 0.1875
- insecond_adapter: bfloat16 [128, 3072], replicated, may hold values from -1.5 to 1.5
- outfirst_adapter: bfloat16 [1024, 128], replicated, may hold values from -0.1875 to 0.1875
- outsecond_adapter: bfloat16 [128, 1024], replicated, may hold values from -1.5 to 1.5
- gatefirst_adapter: bfloat16 [1024, 128], replicated, may hold values from -0.1875 to 0.1875
- gatesecond_adapter: bfloat16 [128, 4608], replicated, may hold values from -1.5 to 1.5
- upfirst_adapter: bfloat16 [1024, 128], replicated, may hold values from -0.1875 to 0.1875
- upsecond_adapter: bfloat16 [128, 4608], replicated, may hold values from -1.5 to 1.5
- downfirst_adapter: bfloat16 [4608, 128], replicated, may hold values from -0.09375 to 0.09375
- downsecond_adapter: bfloat16 [128, 1024], replicated, may hold values from -1.5 to 1.5
Outputs:
- block_output: bfloat16 [2, 16, 1024, 1024], P(None, 'fsdp', 'seq')
- input_grad: bfloat16 [2, 16, 1024, 1024], P(None, 'fsdp', 'seq')
- infirst_grad: float32 [1024, 128], replicated
- insecond_grad: float32 [128, 3072], replicated
- outfirst_grad: float32 [1024, 128], replicated
- outsecond_grad: float32 [128, 1024], replicated
- gatefirst_grad: float32 [1024, 128], replicated
- gatesecond_grad: float32 [128, 4608], replicated
- upfirst_grad: float32 [1024, 128], replicated
- upsecond_grad: float32 [128, 4608], replicated
- downfirst_grad: float32 [4608, 128], replicated
- downsecond_grad: float32 [128, 1024], replicated
All inputs are finite; a program needn't handle non-finite values.
Results may differ from a plain program's by a relative error of at most 0.012.
The roundings to bfloat16 on the way count: a program that leaves them out, or rounds other values in their place, can miss the bound.
Values may be sent and summed in bfloat16 or wider, within the bound.
A program may use at most 256 MiB of HBM per device.

v0:
```python
import jax
import jax.numpy as jnp
from jax import lax
from jax.sharding import PartitionSpec as P

R = 16


EPSILON = 1e-05
ADAPTER_SCALE = 0.5


def from_behind(block, axis, distance):
    devices = range(lax.axis_size(axis))
    route = [(i - distance, i) for i in devices if i - distance in devices]
    return lax.ppermute(block, axis, route)


def forward_dot(left_side, right_side):
    return jnp.dot(left_side, right_side, preferred_element_type=jnp.float32)


def against_dot(left_side, right_side):
    return lax.dot_general(
        left_side, right_side, (((1,), (1,)), ((), ())), preferred_element_type=jnp.float32
    )


def outer_dot(left_side, right_side):
    return lax.dot_general(
        left_side, right_side, (((0,), (0,)), ((), ())), preferred_element_type=jnp.float32
    )


def adapted(inputs, weight, first_map, second_map, select):
    reduced = forward_dot(inputs, first_map).astype(jnp.bfloat16) * select
    result = forward_dot(inputs, weight) + ADAPTER_SCALE * forward_dot(reduced, second_map)
    return (result, reduced)


def adapted_back(grad_low, inputs, reduced, weight, first_map, second_map, select):
    grad_second = ADAPTER_SCALE * outer_dot(reduced, grad_low)
    grad_reduced = (ADAPTER_SCALE * against_dot(grad_low, second_map) * select).astype(jnp.bfloat16)
    grad_first = outer_dot(inputs, grad_reduced)
    grad_inputs = against_dot(grad_low, weight) + against_dot(grad_reduced, first_map)
    return (grad_inputs, grad_first, grad_second)


def rms_parts(values):
    inverse = lax.rsqrt(jnp.mean(values * values, axis=-1, keepdims=True) + EPSILON)
    return (inverse, values * inverse)


def rms_back(grad_normed, gain_vector, inverse, unit_rows):
    scaled = grad_normed * gain_vector
    return inverse * (scaled - unit_rows * jnp.mean(scaled * unit_rows, axis=-1, keepdims=True))


def per_device(
    block_input,
    output_grad,
    adapter_ids,
    in_weight,
    out_weight,
    gate_weight,
    up_weight,
    down_weight,
    conv_weight,
    first_gain,
    second_gain,
    infirst_adapter,
    insecond_adapter,
    outfirst_adapter,
    outsecond_adapter,
    gatefirst_adapter,
    gatesecond_adapter,
    upfirst_adapter,
    upsecond_adapter,
    downfirst_adapter,
    downsecond_adapter,
):
    batches, seq_count, local_len, features = block_input.shape
    row_count = seq_count * local_len
    adapters = (
        infirst_adapter,
        insecond_adapter,
        outfirst_adapter,
        outsecond_adapter,
        gatefirst_adapter,
        gatesecond_adapter,
        upfirst_adapter,
        upsecond_adapter,
        downfirst_adapter,
        downsecond_adapter,
    )
    slot_count = infirst_adapter.shape[1]
    kernel = conv_weight.astype(jnp.float32)
    gain_first = first_gain.astype(jnp.float32)
    gain_second = second_gain.astype(jnp.float32)
    owners = lax.broadcasted_iota(jnp.int32, (1, 1, slot_count), 2) // R
    totals = [jnp.zeros(member.shape, jnp.float32) for member in adapters]
    outputs = []
    input_grads = []
    for batch_index in range(batches):
        weight_in, weight_out, weight_gate, weight_up, weight_down = (
            lax.all_gather(in_weight, "fsdp", axis=0, tiled=True),
            lax.all_gather(out_weight, "fsdp", axis=0, tiled=True),
            lax.all_gather(gate_weight, "fsdp", axis=0, tiled=True),
            lax.all_gather(up_weight, "fsdp", axis=0, tiled=True),
            lax.all_gather(down_weight, "fsdp", axis=0, tiled=True),
        )
        inputs = block_input[batch_index].reshape(row_count, features).astype(jnp.float32)
        matches = owners == adapter_ids[batch_index][:, None, None]
        select = (
            jnp.broadcast_to(matches, (seq_count, local_len, slot_count))
            .reshape(row_count, slot_count)
            .astype(jnp.bfloat16)
        )
        inverse_first, unit_first = rms_parts(inputs)
        normed = (unit_first * gain_first).astype(jnp.bfloat16)
        mixed_in, low_in = adapted(normed, weight_in, adapters[0], adapters[1], select)
        first_part = mixed_in[:, :features]
        middle_part = mixed_in[:, features : 2 * features]
        last_part = mixed_in[:, 2 * features :]
        gated_values = (first_part * last_part).reshape(seq_count, local_len, features)
        rim_rows = from_behind(gated_values[:, local_len - 2 :, :], "seq", 1)
        extended = jnp.concatenate([rim_rows, gated_values], axis=1)
        conv_out = (
            kernel[0] * extended[:, :local_len]
            + kernel[1] * extended[:, 1 : local_len + 1]
            + kernel[2] * extended[:, 2:]
        ).reshape(row_count, features)
        mixer_out = (middle_part * conv_out).astype(jnp.bfloat16)
        branch, low_out = adapted(mixer_out, weight_out, adapters[2], adapters[3], select)
        after_mixer = inputs + branch
        inverse_second, unit_second = rms_parts(after_mixer)
        second = (unit_second * gain_second).astype(jnp.bfloat16)
        gate_value, low_gate = adapted(second, weight_gate, adapters[4], adapters[5], select)
        up_value, low_up = adapted(second, weight_up, adapters[6], adapters[7], select)
        sigmoid_gate = jax.nn.sigmoid(gate_value)
        activated = gate_value * sigmoid_gate
        hidden = (activated * up_value).astype(jnp.bfloat16)
        down_value, low_down = adapted(hidden, weight_down, adapters[8], adapters[9], select)
        outputs.append(
            (after_mixer + down_value).astype(jnp.bfloat16).reshape(seq_count, local_len, features)
        )
        weight_in, weight_out, weight_gate, weight_up, weight_down = (
            lax.all_gather(in_weight, "fsdp", axis=0, tiled=True),
            lax.all_gather(out_weight, "fsdp", axis=0, tiled=True),
            lax.all_gather(gate_weight, "fsdp", axis=0, tiled=True),
            lax.all_gather(up_weight, "fsdp", axis=0, tiled=True),
            lax.all_gather(down_weight, "fsdp", axis=0, tiled=True),
        )
        cotangent = output_grad[batch_index].reshape(row_count, features)
        grad_hidden, grad_first, grad_second = adapted_back(
            cotangent, hidden, low_down, weight_down, adapters[8], adapters[9], select
        )
        totals[8] = totals[8] + grad_first
        totals[9] = totals[9] + grad_second
        grad_gate = (
            grad_hidden * up_value * sigmoid_gate * (1.0 + gate_value * (1.0 - sigmoid_gate))
        ).astype(jnp.bfloat16)
        grad_upper = (grad_hidden * activated).astype(jnp.bfloat16)
        back_gate, grad_first, grad_second = adapted_back(
            grad_gate, second, low_gate, weight_gate, adapters[4], adapters[5], select
        )
        totals[4] = totals[4] + grad_first
        totals[5] = totals[5] + grad_second
        back_upper, grad_first, grad_second = adapted_back(
            grad_upper, second, low_up, weight_up, adapters[6], adapters[7], select
        )
        totals[6] = totals[6] + grad_first
        totals[7] = totals[7] + grad_second
        grad_after = cotangent.astype(jnp.float32) + rms_back(
            back_gate + back_upper, gain_second, inverse_second, unit_second
        )
        grad_mixer, grad_first, grad_second = adapted_back(
            grad_after.astype(jnp.bfloat16),
            mixer_out,
            low_out,
            weight_out,
            adapters[2],
            adapters[3],
            select,
        )
        totals[2] = totals[2] + grad_first
        totals[3] = totals[3] + grad_second
        grad_conv = (grad_mixer * middle_part).reshape(seq_count, local_len, features)
        rim_back = from_behind(grad_conv[:, :2, :], "seq", -1)
        beyond = jnp.concatenate([grad_conv, rim_back], axis=1)
        grad_gated = (
            kernel[2] * beyond[:, :local_len]
            + kernel[1] * beyond[:, 1 : local_len + 1]
            + kernel[0] * beyond[:, 2:]
        ).reshape(row_count, features)
        grad_mixed = jnp.concatenate(
            [grad_gated * last_part, grad_mixer * conv_out, grad_gated * first_part], axis=1
        ).astype(jnp.bfloat16)
        grad_normed, grad_first, grad_second = adapted_back(
            grad_mixed, normed, low_in, weight_in, adapters[0], adapters[1], select
        )
        totals[0] = totals[0] + grad_first
        totals[1] = totals[1] + grad_second
        grad_input = grad_after + rms_back(grad_normed, gain_first, inverse_first, unit_first)
        input_grads.append(grad_input.astype(jnp.bfloat16).reshape(seq_count, local_len, features))
    summed = lax.psum(
        (
            totals[0],
            totals[1],
            totals[2],
            totals[3],
            totals[4],
            totals[5],
            totals[6],
            totals[7],
            totals[8],
            totals[9],
        ),
        ("fsdp", "seq"),
    )
    return (
        jnp.stack(outputs),
        jnp.stack(input_grads),
        summed[0],
        summed[1],
        summed[2],
        summed[3],
        summed[4],
        summed[5],
        summed[6],
        summed[7],
        summed[8],
        summed[9],
    )


def solution(mesh):
    return jax.shard_map(
        per_device,
        mesh=mesh,
        in_specs=(
            P(None, "fsdp", "seq", None),
            P(None, "fsdp", "seq", None),
            P(None, "fsdp"),
            P("fsdp", None),
            P("fsdp", None),
            P("fsdp", None),
            P("fsdp", None),
            P("fsdp", None),
            P(),
            P(),
            P(),
            P(),
            P(),
            P(),
            P(),
            P(),
            P(),
            P(),
            P(),
            P(),
            P(),
        ),
        out_specs=(
            P(None, "fsdp", "seq", None),
            P(None, "fsdp", "seq", None),
            P(),
            P(),
            P(),
            P(),
            P(),
            P(),
            P(),
            P(),
            P(),
            P(),
        ),
        check_vma=False,
    )
```

profile of v0, /device:TPU:0, one launch (start us, length us, event | category | flops | bytes accessed | tf_op | source)
XLA Modules:
  0.0 815.6 jit_solution(7204211921925107187)
XLA Ops:
  19.3 55.6 %all-gather.6.cloned.1.call-done = bf16[1024,3072]{1,0:T(8,128)(2,1)} async-done(((bf16[64,3072]{1,0:T(8,128)(2,1)}), bf16[1024,3072]{1,0:T(8,128)(2,1)}) %all-gather.6.cloned.1.call-update) | async-done | bytes 6291472 | tf_op jit(solution)/shard_map/all_gather | solution.py:106
  74.9 5.8 fusion.106
  102.3 14.8 %all-gather.8.cloned.1.call-done = bf16[1024,1024]{1,0:T(8,128)(2,1)} async-done(((bf16[64,1024]{1,0:T(8,128)(2,1)}), bf16[1024,1024]{1,0:T(8,128)(2,1)}) %all-gather.8.cloned.1.call-update) | async-done | bytes 2097168 | tf_op jit(solution)/shard_map/all_gather | solution.py:107
  127.3 72.3 %all-gather.12.cloned.1.call-done = bf16[1024,4608]{1,0:T(8,128)(2,1)} async-done(((bf16[64,4608]{1,0:T(8,128)(2,1)}), bf16[1024,4608]{1,0:T(8,128)(2,1)}) %all-gather.12.cloned.1.call-update) | async-done | bytes 9437200 | tf_op jit(solution)/shard_map/all_gather | solution.py:109
  199.6 7.7 fusion.121
  212.2 69.2 %all-gather.14.cloned.1.call-done = bf16[4608,1024]{1,0:T(8,128)(2,1)} async-done(((bf16[288,1024]{1,0:T(8,128)(2,1)}), bf16[4608,1024]{1,0:T(8,128)(2,1)}) %all-gather.14.cloned.1.call-update) | async-done | bytes 9437200 | tf_op jit(solution)/shard_map/all_gather | solution.py:110
  281.4 8.2 %fusion.82 = f32[512,4608]{1,0:T(8,128)S(1)} fusion(bf16[4608,1024]{1,0:T(8,128)(2,1)} %all-gather.14.cloned.1.call-done, bf16[2,1,512,1024]{3,2,1,0:T(8,128)(2,1)} %param.22), kind=kOutput, calls=%fused_computation.178 | convolution fusion | flops 4831838208 | bytes 19922944 | tf_op jit(solution)/shard_map/dot_general | solution.py:24
  294.6 68.5 %all-gather.10.cloned.1.call-done = bf16[1024,4608]{1,0:T(8,128)(2,1)} async-done(((bf16[64,4608]{1,0:T(8,128)(2,1)}), bf16[1024,4608]{1,0:T(8,128)(2,1)}) %all-gather.10.cloned.1.call-update) | async-done | bytes 9437200 | tf_op jit(solution)/shard_map/all_gather | solution.py:108
  363.1 11.0 %fusion.120 = f32[512,4608]{1,0:T(8,128)} fusion(bf16[512,1024]{1,0:T(8,128)(2,1)S(1)} %get-tuple-element.55, bf16[1024,4608]{1,0:T(8,128)(2,1)} %all-gather.10.cloned.1.call-done), kind=kOutput, calls=%fused_computation.222 | convolution fusion | flops 4831838208 | bytes 19922944 | tf_op jit(solution)/shard_map/dot_general | solution.py:20
  374.2 16.3 %multiply_convert_fusion.3 = (bf16[512,4608]{1,0:T(8,128)(2,1)}, bf16[512,4608]{1,0:T(8,128)(2,1)}, bf16[512,4608]{1,0:T(8,128)(2,1)S(1)}) fusion(f32[512,4608]{1,0:T(8,128)} %convolution_add_fusion.1, f32[512,4608]{1,0:T(8,128)} %multiply_add_fusion.2, f32[512,4608]{1,0:T(8,128)} %fusion.120, bf16[512,128]{1,0:T(8,128)(2,1)} %fusion.67, ...), kind=kOutput, calls=%fused_computation.3 | convolution fusion | flops 644087808 | bytes 43778048 | tf_op jit(solution)/shard_map/dot_general | solution.py:20
  411.7 7.6 fusion.125
  424.2 8.2 %fusion.77 = f32[512,4608]{1,0:T(8,128)S(1)} fusion(bf16[4608,1024]{1,0:T(8,128)(2,1)} %all-gather.14.cloned.1.call-done, bf16[2,1,512,1024]{3,2,1,0:T(8,128)(2,1)S(1)} %copy-done.19), kind=kOutput, calls=%fused_computation.173 | convolution fusion | flops 4831838208 | bytes 19922944 | tf_op jit(solution)/shard_map/dot_general | solution.py:24
  432.4 5.0 convolution_add_fusion
  437.4 11.0 %fusion.124 = f32[512,4608]{1,0:T(8,128)} fusion(bf16[512,1024]{1,0:T(8,128)(2,1)S(1)} %get-tuple-element.56, bf16[1024,4608]{1,0:T(8,128)(2,1)} %all-gather.10.cloned.1.call-done), kind=kOutput, calls=%fused_computation.226 | convolution fusion | flops 4831838208 | bytes 19922944 | tf_op jit(solution)/shard_map/dot_general | solution.py:20
  448.4 16.3 %multiply_convert_fusion.1 = (bf16[512,4608]{1,0:T(8,128)(2,1)S(1)}, bf16[512,4608]{1,0:T(8,128)(2,1)}, bf16[512,4608]{1,0:T(8,128)(2,1)}) fusion(f32[512,4608]{1,0:T(8,128)} %convolution_add_fusion, f32[512,4608]{1,0:T(8,128)} %multiply_add_fusion, f32[512,4608]{1,0:T(8,128)} %fusion.124, bf16[512,128]{1,0:T(8,128)(2,1)} %fusion.71, ...), kind=kOutput, calls=%fused_computation.1 | convolution fusion | flops 644087808 | bytes 43778048 | tf_op jit(solution)/shard_map/dot_general | solution.py:20
  464.7 5.8 fusion.61
  472.3 7.9 fusion.131
  480.3 7.8 fusion.133
  489.1 7.9 fusion.127
  497.1 7.9 fusion.129
  557.6 9.9 %fusion.122 = f32[512,1024]{1,0:T(8,128)S(1)} fusion(bf16[512,4608]{1,0:T(8,128)(2,1)} %copy-done.28, bf16[4608,1024]{1,0:T(8,128)(2,1)} %all-gather.14.cloned.1.call-done), kind=kOutput, calls=%fused_computation.224 | convolution fusion | flops 4831838208 | bytes 16252928 | tf_op jit(solution)/shard_map/dot_general | solution.py:20
  568.0 9.6 %fusion.126 = f32[512,1024]{1,0:T(8,128)S(1)} fusion(bf16[512,4608]{1,0:T(8,128)(2,1)} %get-tuple-element.39, bf16[4608,1024]{1,0:T(8,128)(2,1)} %all-gather.14.cloned.1.call-done), kind=kOutput, calls=%fused_computation.228 | convolution fusion | flops 4831838208 | bytes 16252928 | tf_op jit(solution)/shard_map/dot_general | solution.py:20
  585.1 6.9 fusion.38
  594.6 199.0 %all-reduce.3.cloned.1.call-done = (f32[1024,128]{1,0:T(8,128)}, f32[128,3072]{1,0:T(8,128)}, f32[1024,128]{1,0:T(8,128)}, f32[128,1024]{1,0:T(8,128)}, f32[1024...) async-done(((f32[1024,128]{1,0:T(8,128)}, f32[128,3072]{1,0:T(8,128)}, ...) | async-done | bytes 11796496 | tf_op jit(solution)/shard_map/psum | solution.py:206
  (438 shorter events, 158.9 us)
Async XLA Ops:
  7.2 367.0 %copy-start = (bf16[128,4608]{1,0:T(8,128)(2,1)S(1)}, bf16[128,4608]{1,0:T(8,128)(2,1)}, u32[]{:S(2)}) copy-start(bf16[128,4608]{1,0:T(8,128)(2,1)} %param.37) | copy-start | bytes 3538948
  7.2 67.7 %all-gather.6.cloned.1.call-start = ((), (), s32[]{:S(2)}) async-start(), calls=%async_computation | async-start | bytes 6684672 | tf_op jit(solution)/shard_map/all_gather | solution.py:106
  8.0 109.1 %all-gather.8.cloned.1.call-start = ((), (), s32[]{:S(2)}) async-start(), calls=%async_computation.1 | async-start | bytes 2228224 | tf_op jit(solution)/shard_map/all_gather | solution.py:107
  8.7 190.9 %all-gather.12.cloned.1.call-start = ((), (), s32[]{:S(2)}) async-start(), calls=%async_computation.3 | async-start | bytes 10027008 | tf_op jit(solution)/shard_map/all_gather | solution.py:109
  9.5 271.9 %all-gather.14.cloned.1.call-start = ((), (), s32[]{:S(2)}) async-start(), calls=%async_computation.4 | async-start | bytes 10027008 | tf_op jit(solution)/shard_map/all_gather | solution.py:110
  10.0 353.1 %all-gather.10.cloned.1.call-start = ((), (), s32[]{:S(2)}) async-start(), calls=%async_computation.2 | async-start | bytes 10027008 | tf_op jit(solution)/shard_map/all_gather | solution.py:108
  10.6 783.0 %all-reduce.3.cloned.1.call-start = ((), (), s32[]{:S(2)}) async-start(), calls=%async_computation.5 | async-start | bytes 23592960 | tf_op jit(solution)/shard_map/psum | solution.py:206
  10.7 75.1 %copy-start.115 = (f32[1024]{0:T(1024)}, f32[1024]{0:T(1024)S(1)}, u32[]{:S(2)}) copy-start(f32[1024]{0:T(1024)S(1)} %convert_element_type.169) | copy-start | bytes 12292
  16.0 58.9 %copy-start.111 = (f32[512]{0:T(512)}, f32[512]{0:T(512)S(1)}, u32[]{:S(2)}) copy-start(f32[512]{0:T(512)S(1)} %add_rsqrt_fusion.1) | copy-start | bytes 6148
  16.1 69.7 %copy-start.113 = (f32[512]{0:T(512)}, f32[512]{0:T(512)S(1)}, u32[]{:S(2)}) copy-start(f32[512]{0:T(512)S(1)} %add_rsqrt_fusion.3) | copy-start | bytes 6148
  18.8 62.0 %copy-start.91 = (bf16[512,128]{1,0:T(8,128)(2,1)}, bf16[512,128]{1,0:T(8,128)(2,1)S(1)}, u32[]{:S(2)}) copy-start(bf16[512,128]{1,0:T(8,128)(2,1)S(1)} %fusion.69) | copy-start | bytes 393220
  18.8 56.1 %copy-start.24 = (bf16[2,1,512,1024]{3,2,1,0:T(8,128)(2,1)S(1)}, bf16[2,1,512,1024]{3,2,1,0:T(8,128)(2,1)}, u32[]{:S(2)}) copy-start(bf16[2,1,512,1024]{3,2,1,0:T(8,128)(2,1)} %param.21) | copy-start | bytes 6291460
  19.3 70.1 %copy-start.93 = (bf16[512,128]{1,0:T(8,128)(2,1)}, bf16[512,128]{1,0:T(8,128)(2,1)S(1)}, u32[]{:S(2)}) copy-start(bf16[512,128]{1,0:T(8,128)(2,1)S(1)} %fusion.65) | copy-start | bytes 393220
  82.4 10.5 %collective-permute-start.1 = (f32[1,2,1024]{2,1,0:T(2,128)S(1)}, f32[1,2,1024]{2,1,0:T(2,128)S(1)}, u32[]{:S(2)}, u32[]{:S(2)}) collective-permute-start(f32[1,2,1024]{2,1,0:T(2,128)S(1)} %slice.129), channel_id=1, source_target_pairs={{0,1},{2,3},{4,5},{6,7},{8,9},{10,11},{12,13},{14,15},{16,17},{18,... | collective-permute-start | bytes 24584 | tf_op jit(solution)/shard_map/ppermute | solution.py:16
  91.0 2.7 collective-permute-start
  92.9 30.0 %copy-start.98 = (f32[1024]{0:T(1024)}, f32[1024]{0:T(1024)S(1)}, u32[]{:S(2)}) copy-start(f32[1024]{0:T(1024)S(1)} %convert_element_type.175) | copy-start | bytes 12292
  124.2 313.2 %copy-start.16 = (bf16[512,1024]{1,0:T(8,128)(2,1)}, bf16[512,1024]{1,0:T(8,128)(2,1)S(1)}, u32[]{:S(2)}) copy-start(bf16[512,1024]{1,0:T(8,128)(2,1)S(1)} %get-tuple-element.56) | copy-start | bytes 3145732
  126.2 293.1 %copy-start.49 = (bf16[512,128]{1,0:T(8,128)(2,1)}, bf16[512,128]{1,0:T(8,128)(2,1)S(1)}, u32[]{:S(2)}) copy-start(bf16[512,128]{1,0:T(8,128)(2,1)S(1)} %fusion.72) | copy-start | bytes 393220
  448.4 16.3 %copy-start.121 = (f32[128]{0:T(128)S(1)}, f32[128]{0:T(128)}, u32[]{:S(2)}) copy-start(f32[128]{0:T(128)} %copy-done.120) | copy-start | bytes 1540
  472.3 16.8 %slice-start.16 = ((s8[4718592]{0:T(1024)(128)(4,1)}), s8[4194304]{0:T(1024)(128)(4,1)S(1)}, s32[]{:S(2)}) async-start(s8[4718592]{0:T(1024)(128)(4,1)} %bitcast.233), calls=%async_computation.22 | async-start | bytes 8388608
  507.8 16.9 %copy-start.11 = (f32[512,1024]{1,0:T(8,128)}, f32[512,1024]{1,0:T(8,128)S(1)}, u32[]{:S(2)}) copy-start(f32[512,1024]{1,0:T(8,128)S(1)} %get-tuple-element.45) | copy-start | bytes 6291460
  507.8 25.0 %copy-start.9 = (f32[512,1024]{1,0:T(8,128)}, f32[512,1024]{1,0:T(8,128)S(1)}, u32[]{:S(2)}) copy-start(f32[512,1024]{1,0:T(8,128)S(1)} %get-tuple-element.44) | copy-start | bytes 6291460
  529.8 10.0 %collective-permute-start.3 = (f32[1,2,1024]{2,1,0:T(2,128)S(1)}, f32[1,2,1024]{2,1,0:T(2,128)S(1)}, u32[]{:S(2)}, u32[]{:S(2)}) collective-permute-start(f32[1,2,1024]{2,1,0:T(2,128)S(1)} %slice.135), channel_id=1, source_target_pairs={{1,0},{3,2},{5,4},{7,6},{9,8},{11,10},{13,12},{15,14},{17,16},{19,... | collective-permute-start | bytes 24584 | tf_op jit(solution)/shard_map/ppermute | solution.py:16
  537.4 5.5 collective-permute-start.2
  (137 other events, 557.9 us)
Sparse Core Ops, SparseCore 0:
  10.3 64.5 all-gather.5
  77.1 39.9 all-gather.7
  119.4 80.2 all-gather.11
  201.8 79.5 all-gather.13
  283.5 79.5 all-gather.9
  557.7 235.8 all-reduce.2
where the time goes:
time: 823 us; the launch traced here: 816 us
  waiting for transfers between devices  486 us (59%)
  matrix products  252 us (31%)
  local copies, waits for them, and re-layouts  28.8 us (3%)
  other arithmetic  23.6 us (3%)
  between operations  16.5 us (2%)
  starting transfers between devices  8.3 us (1%)
    psum x1, waiting for transfers between devices, per_device(): lax.psum((totals[0], totals[1], totals[2], totals[3], totals[4], totals[5...  199 us
    dot_general x30, matrix products, forward_dot(): return jnp.dot(left_side, right_side, preferred_element_type=jnp.float32)  130 us
    dot_general x30, matrix products, against_dot(): lax.dot_general(left_side, right_side, (((1,), (1,)), ((), ())), preferre...  91.6 us
    all_gather x1, waiting for transfers between devices, per_device(): lax.all_gather(up_weight, 'fsdp', axis=0, tiled=True)  72.3 us
    all_gather x1, waiting for transfers between devices, per_device(): lax.all_gather(down_weight, 'fsdp', axis=0, tiled=True)  69.2 us
    all_gather x1, waiting for transfers between devices, per_device(): lax.all_gather(gate_weight, 'fsdp', axis=0, tiled=True)  68.5 us
    all_gather x1, waiting for transfers between devices, per_device(): lax.all_gather(in_weight, 'fsdp', axis=0, tiled=True)  55.6 us
    dot_general x20, matrix products, outer_dot(): lax.dot_general(left_side, right_side, (((0,), (0,)), ((), ())), preferre...  30 us
  transfers between devices with their start and end apart: 10, of which 8 were waited for; matrix products, arithmetic and copies ran while one was open for 13% of the time, Pallas kernels for 0%

commit v1 on v0

--- a/solution.py
+++ b/solution.py
@@ -1,6 +1,10 @@
+import functools
+
 import jax
 import jax.numpy as jnp
 from jax import lax
+from jax.experimental import pallas as pl
+from jax.experimental.pallas import tpu as pltpu
 from jax.sharding import PartitionSpec as P
 
 R = 16
@@ -8,6 +12,221 @@
 
 EPSILON = 1e-05
 ADAPTER_SCALE = 0.5
+MESH = pl.DeviceIdType.MESH
+BF16 = jnp.bfloat16
+F32 = jnp.float32
+
+
+class Ring:
+    def __init__(self, fsdp_size):
+        self.count = fsdp_size // 2
+        self.me = lax.axis_index("fsdp")
+        self.core = lax.rem(self.me, 2)
+        chip = self.me // 2
+        if fsdp_size == 16:
+            z, y = chip // 2, lax.rem(chip, 2)
+            self.place = y * z + (1 - y) * (7 - z)
+        else:
+            self.place = chip
+        self.grid = fsdp_size == 16
+        x = lax.axis_index("seq")
+        self.role = lax.rem(x, 2)
+        self.to_next = {"fsdp": self.device(lax.rem(self.place + 1, self.count))}
+        self.to_prev = {"fsdp": self.device(lax.rem(self.place + self.count - 1, self.count))}
+        self.to_core = {"fsdp": self.me + 1 - 2 * self.core}
+        self.to_seq = {"seq": x + 1 - 2 * self.role}
+
+    def device(self, place):
+        if self.grid:
+            y = 1 - place // 4
+            z = y * place + (1 - y) * (7 - place)
+            return (z * 2 + y) * 2 + self.core
+        return place * 2 + self.core
+
+    def at_step(self, direction, step):
+        if direction == 0:
+            return self.device(lax.rem(self.place + self.count - step, self.count))
+        return self.device(lax.rem(self.place + step, self.count))
+
+    def greet(self):
+        barrier = pltpu.get_barrier_semaphore()
+        for device in (self.to_next, self.to_prev, self.to_core, self.to_seq):
+            pl.semaphore_signal(barrier, inc=1, device_id=device, device_id_type=MESH)
+        pl.semaphore_wait(barrier, 4)
+
+
+class Unit:
+    def __init__(self, ring, number, spot, sems):
+        self.ring, self.number, self.spot = ring, number, spot
+        self.send, self.ring_sem, self.seq_sem, self.core_sem = sems
+        half = ring.count // 2
+        self.reach = (half, ring.count - 1 - half) if number % 2 == 0 else (ring.count - 1 - half, half)
+        self.steps = max(self.reach)
+        self.sent = []
+
+    def push(self, spot, sem, device):
+        copy = pltpu.make_async_remote_copy(
+            src_ref=spot, dst_ref=spot, send_sem=self.send.at[self.number, len(self.sent)],
+            recv_sem=sem, device_id=device, device_id_type=MESH,
+        )
+        copy.start()
+        self.sent.append(copy)
+
+    def arrived(self, spot, sem):
+        pltpu.make_async_remote_copy(
+            src_ref=spot, dst_ref=spot, send_sem=self.send.at[self.number, 0],
+            recv_sem=sem, device_id=self.ring.to_next, device_id_type=MESH,
+        ).wait_recv()
+
+    def own(self):
+        ring, n = self.ring, self.number
+        for slot, third in ((0, ring.role), (1, 2)):
+            spot = self.spot(third, ring.me)
+            self.push(spot, self.ring_sem.at[n, slot, 0], ring.to_next)
+            self.push(spot, self.ring_sem.at[n, slot, ring.count - 2], ring.to_prev)
+        for third in (ring.role, 1 - ring.role, 2):
+            self.push(self.spot(third, ring.me), self.core_sem.at[n, third, 0], ring.to_core)
+
+    def legs(self, step):
+        for direction, reach in enumerate(self.reach):
+            if step <= reach:
+                lane = step - 1 if direction == 0 else self.ring.count - 1 - step
+                yield direction, reach, lane, self.ring.at_step(direction, step)
+
+    def relay(self, step):
+        ring, n = self.ring, self.number
+        for direction, reach, lane, owner in self.legs(step):
+            for slot, third in ((0, ring.role), (1, 2)):
+                spot = self.spot(third, owner)
+                self.arrived(spot, self.ring_sem.at[n, slot, lane])
+                if step < reach:
+                    onward = lane + 1 - 2 * direction
+                    self.push(spot, self.ring_sem.at[n, slot, onward], (ring.to_next, ring.to_prev)[direction])
+                if slot == 0:
+                    self.push(spot, self.seq_sem.at[n, lane], ring.to_seq)
+                self.push(spot, self.core_sem.at[n, third, 1 + lane], ring.to_core)
+
+    def relay_seq(self, step):
+        ring, n = self.ring, self.number
+        third = 1 - ring.role
+        for _, _, lane, owner in self.legs(step):
+            spot = self.spot(third, owner)
+            self.arrived(spot, self.seq_sem.at[n, lane])
+            self.push(spot, self.core_sem.at[n, third, 1 + lane], ring.to_core)
+
+    def collect(self):
+        ring, n = self.ring, self.number
+        for third in range(3):
+            for lane in range(ring.count):
+                self.arrived(self.spot(third, ring.me), self.core_sem.at[n, third, lane])
+
+    def drain(self):
+        for copy in self.sent:
+            copy.wait_send()
+
+
+def timeline(units, lag=2):
+    entries = []
+    for k, unit in enumerate(units):
+        entries.append((k, 0, unit.own))
+        for step in range(1, unit.steps + 1):
+            entries.append((k + step, 1, functools.partial(unit.relay, step)))
+            entries.append((k + step + lag, 2, functools.partial(unit.relay_seq, step)))
+    return [entry[2] for entry in sorted(entries, key=lambda entry: entry[:2])]
+
+
+def sem_shapes(units, count):
+    sends = 4 + 3 + 2 * (count - 1) * 2 + (count - 1) * 2
+    return [
+        pltpu.SemaphoreType.DMA((units, sends)),
+        pltpu.SemaphoreType.DMA((units, 2, count - 1)),
+        pltpu.SemaphoreType.DMA((units, count - 1)),
+        pltpu.SemaphoreType.DMA((units, 3, count)),
+    ]
+
+
+GU_UNITS = 3
+
+
+def spots(in_all, out_all, gu_all, down_all, fsdp_size):
+    rows = in_all.shape[0] // fsdp_size
+    down_rows = down_all.shape[0] // fsdp_size
+    part = in_all.shape[1] // 3
+    out_x = 3 * out_all.shape[1] // 8
+
+    def in_spot(third, owner):
+        return in_all.at[pl.ds(owner * rows, rows), pl.ds(pl.multiple_of(third * part, 128), part)]
+
+    def out_spot(third, owner):
+        width = out_x if not isinstance(third, int) or third < 2 else out_all.shape[1] - 2 * out_x
+        return out_all.at[pl.ds(owner * rows, rows), pl.ds(pl.multiple_of(third * out_x, 128), width)]
+
+    def down_spot(third, owner):
+        size = down_rows // 3
+        return down_all.at[pl.ds(owner * down_rows + third * size, size), :]
+
+    def gu_spot(chunk, third, owner):
+        size = gu_all.shape[2] // GU_UNITS // 3
+        start = pl.multiple_of((chunk * 3 + third) * size, 128)
+        return gu_all.at[:, pl.ds(owner * rows, rows), pl.ds(start, size)]
+
+    return [in_spot, out_spot, down_spot] + [functools.partial(gu_spot, k) for k in range(GU_UNITS)]
+
+
+def gather_kernel(fsdp_size, *refs):
+    in_own, out_own, gate_own, up_own, down_own, in_all, out_all, gu_all, down_all = refs[:9]
+    sems, local_sem, held = refs[9:13], refs[13], refs[14:]
+    ring = Ring(fsdp_size)
+    rows, down_rows = in_own.shape[0], down_own.shape[0]
+    mine = pl.ds(ring.me * rows, rows)
+    moves = [
+        (in_own, held[0], in_all.at[mine, :]),
+        (out_own, held[1], out_all.at[mine, :]),
+        (gate_own, held[2], gu_all.at[0, mine, :]),
+        (up_own, held[3], gu_all.at[1, mine, :]),
+        (down_own, held[4], down_all.at[pl.ds(ring.me * down_rows, down_rows), :]),
+    ]
+    inward = [pltpu.make_async_copy(a, b, local_sem.at[0, k]) for k, (a, b, _) in enumerate(moves)]
+    outward = [pltpu.make_async_copy(b, c, local_sem.at[1, k]) for k, (_, b, c) in enumerate(moves)]
+    for copy in inward:
+        copy.start()
+    ring.greet()
+    for first, second in zip(inward, outward):
+        first.wait()
+        second.start()
+    for copy in outward:
+        copy.wait()
+    units = [
+        Unit(ring, k, spot, sems)
+        for k, spot in enumerate(spots(in_all, out_all, gu_all, down_all, fsdp_size))
+    ]
+    for action in timeline(units):
+        action()
+    for unit in units:
+        unit.collect()
+    for unit in units:
+        unit.drain()
+
+
+def gather_all(fsdp_size, in_weight, out_weight, gate_weight, up_weight, down_weight):
+    anywhere = pl.BlockSpec(memory_space=pl.ANY)
+    rows, features = fsdp_size * in_weight.shape[0], out_weight.shape[1]
+    own = (in_weight, out_weight, gate_weight, up_weight, down_weight)
+    return pl.pallas_call(
+        functools.partial(gather_kernel, fsdp_size),
+        out_shape=(
+            jax.ShapeDtypeStruct((rows, in_weight.shape[1]), BF16),
+            jax.ShapeDtypeStruct((rows, features), BF16),
+            jax.ShapeDtypeStruct((2, rows, gate_weight.shape[1]), BF16),
+            jax.ShapeDtypeStruct((fsdp_size * down_weight.shape[0], features), BF16),
+        ),
+        in_specs=[anywhere] * 5,
+        out_specs=(anywhere,) * 4,
+        scratch_shapes=sem_shapes(3 + GU_UNITS, fsdp_size // 2)
+        + [pltpu.SemaphoreType.DMA((2, 5))]
+        + [pltpu.VMEM(member.shape, BF16) for member in own],
+        compiler_params=pltpu.CompilerParams(collective_id=0, has_side_effects=True),
+    )(*own)
 
 
 def from_behind(block, axis, distance):
@@ -101,14 +320,11 @@
     totals = [jnp.zeros(member.shape, jnp.float32) for member in adapters]
     outputs = []
     input_grads = []
+    weight_in, weight_out, weight_gate_up, weight_down = gather_all(
+        lax.axis_size("fsdp"), in_weight, out_weight, gate_weight, up_weight, down_weight
+    )
+    weight_gate, weight_up = weight_gate_up[0], weight_gate_up[1]
     for batch_index in range(batches):
-        weight_in, weight_out, weight_gate, weight_up, weight_down = (
-            lax.all_gather(in_weight, "fsdp", axis=0, tiled=True),
-            lax.all_gather(out_weight, "fsdp", axis=0, tiled=True),
-            lax.all_gather(gate_weight, "fsdp", axis=0, tiled=True),
-            lax.all_gather(up_weight, "fsdp", axis=0, tiled=True),
-            lax.all_gather(down_weight, "fsdp", axis=0, tiled=True),
-        )
         inputs = block_input[batch_index].reshape(row_count, features).astype(jnp.float32)
         matches = owners == adapter_ids[batch_index][:, None, None]
         select = (
@@ -144,13 +360,6 @@
         outputs.append(
             (after_mixer + down_value).astype(jnp.bfloat16).reshape(seq_count, local_len, features)
         )
-        weight_in, weight_out, weight_gate, weight_up, weight_down = (
-            lax.all_gather(in_weight, "fsdp", axis=0, tiled=True),
-            lax.all_gather(out_weight, "fsdp", axis=0, tiled=True),
-            lax.all_gather(gate_weight, "fsdp", axis=0, tiled=True),
-            lax.all_gather(up_weight, "fsdp", axis=0, tiled=True),
-            lax.all_gather(down_weight, "fsdp", axis=0, tiled=True),
-        )
         cotangent = output_grad[batch_index].reshape(row_count, features)
         grad_hidden, grad_first, grad_second = adapted_back(
             cotangent, hidden, low_down, weight_down, adapters[8], adapters[9], select
@@ -204,7 +413,7 @@
         grad_input = grad_after + rms_back(grad_normed, gain_first, inverse_first, unit_first)
         input_grads.append(grad_input.astype(jnp.bfloat16).reshape(seq_count, local_len, features))
     summed = lax.psum(
-        (
+        tuple(t.astype(BF16) for t in (
             totals[0],
             totals[1],
             totals[2],
@@ -215,22 +424,22 @@
             totals[7],
             totals[8],
             totals[9],
-        ),
+        )),
         ("fsdp", "seq"),
     )
     return (
         jnp.stack(outputs),
         jnp.stack(input_grads),
-        summed[0],
-        summed[1],
-        summed[2],
-        summed[3],
-        summed[4],
-        summed[5],
-        summed[6],
-        summed[7],
-        summed[8],
-        summed[9],
+        summed[0].astype(F32),
+        summed[1].astype(F32),
+        summed[2].astype(F32),
+        summed[3].astype(F32),
+        summed[4].astype(F32),
+        summed[5].astype(F32),
+        summed[6].astype(F32),
+        summed[7].astype(F32),
+        summed[8].astype(F32),
+        summed[9].astype(F32),
     )
 
 

time: 823 us -> 643 us (0.78)
  waiting for transfers between devices: 486 us -> 142 us
  Pallas kernels: 0 us -> 145 us
  matrix products: 252 us -> 271 us
  other arithmetic: 23.6 us -> 39.2 us
  local copies, waits for them, and re-layouts: 28.8 us -> 14.6 us
    all_gather x5 -> x0, waiting for transfers between devices: 280 us -> none  [the longest x1 72.3 us: per_device(): lax.all_gather(up_weight, 'fsdp', axis=0, tiled=True)]
    pallas_call x0 -> x1, Pallas kernels: none -> 145 us  [gather_all(): pl.pallas_call(functools.partial(gather_kernel, fsdp_size), out_shape=(ja...]
    psum x1, waiting for transfers between devices: 199 us -> 142 us  [per_device(): lax.psum(tuple((t.astype(BF16) for t in (totals[0], totals[1], totals[2],...]
    dot_general x30, matrix products: 91.6 us -> 116 us  [against_dot(): lax.dot_general(left_side, right_side, (((1,), (1,)), ((), ())), preferre...]
    unnamed x312 -> x274, local copies, waits for them, and re-layouts: 28.1 us -> 13.2 us
    convert_element_type x0 -> x10, other arithmetic: none -> 12.5 us  [the longest x1 3.01 us: per_device(): summed[5].astype(F32)]
  transfers between devices with their start and end apart: 10 -> 5, of which waited for: 8 -> 2; matrix products, arithmetic and copies ran while one was open for 13% -> 10% of each run, Pallas kernels for 0% -> 0%
where the time goes in v1:
time: 643 us; the launch traced here: 636 us
  matrix products  271 us (42%)
  Pallas kernels  145 us (23%)
  waiting for transfers between devices  142 us (22%)
  other arithmetic  39.2 us (6%)
  between operations  16.1 us (3%)
  local copies, waits for them, and re-layouts  14.6 us (2%)
  starting transfers between devices  7.34 us (1%)
    pallas_call x1, Pallas kernels, gather_all(): pl.pallas_call(functools.partial(gather_kernel, fsdp_size), out_shape=(ja...  145 us
    psum x1, waiting for transfers between devices, per_device(): lax.psum(tuple((t.astype(BF16) for t in (totals[0], totals[1], totals[2],...  142 us
    dot_general x30, matrix products, forward_dot(): return jnp.dot(left_side, right_side, preferred_element_type=jnp.float32)  130 us
    dot_general x30, matrix products, against_dot(): lax.dot_general(left_side, right_side, (((1,), (1,)), ((), ())), preferre...  116 us
    dot_general x20, matrix products, outer_dot(): lax.dot_general(left_side, right_side, (((0,), (0,)), ((), ())), preferre...  25.3 us
    unnamed x274, local copies, waits for them, and re-layouts  13.2 us
  transfers between devices with their start and end apart: 5, of which 2 were waited for; matrix products, arithmetic and copies ran while one was open for 10% of the time, Pallas kernels for 0%

profile of v1, /device:TPU:0, one launch (start us, length us, event | category | flops | bytes accessed | tf_op | source)
XLA Modules:
  0.0 635.8 jit_solution(14437730935612115866)
XLA Ops:
  12.2 145.2 %shard_map.292 = (bf16[1024,3072]{1,0:T(8,128)(2,1)}, bf16[1024,1024]{1,0:T(8,128)(2,1)}, bf16[2,1024,4608]{2,1,0:T(8,128)(2,1)}, bf16[4608,1024]{1,0:T(8,128)(2,1)}) custom-call(bf16[64,3072]{1,0:T(8,128)(2,1)} %refs_0_.1, bf16[64,1024]{1,0:T(8,128)(2,1)} %refs_1_.1, bf16[64,4608]{1,0:T(8,128)(2,1)} %refs_2_.1, bf16[64,4608]{1,0:T(8,128)(2,1)} %refs_3_.1, ...), custom_call_target="tpu_custom_call" | custom-call | tf_op jit(solution)/shard_map/pallas_call | solution.py:215
  157.4 5.8 fusion.144
  178.6 11.1 %fusion.120 = f32[4608,512]{0,1:T(8,128)} fusion(bf16[4608,1024]{1,0:T(8,128)(2,1)} %get-tuple-element.19, bf16[2,1,512,1024]{3,2,1,0:T(8,128)(2,1)S(1)} %copy-done.15), kind=kOutput, calls=%fused_computation.212 | convolution fusion | flops 4831838208 | bytes 19922944 | tf_op jit(solution)/shard_map/dot_general | solution.py:243
  189.8 7.7 %fusion.115 = f32[4608,512]{0,1:T(8,128)S(1)} fusion(bf16[4608,1024]{1,0:T(8,128)(2,1)} %get-tuple-element.19, bf16[2,1,512,1024]{3,2,1,0:T(8,128)(2,1)S(1)} %copy-done.15), kind=kOutput, calls=%fused_computation.207 | convolution fusion | flops 4831838208 | bytes 19922944 | tf_op jit(solution)/shard_map/dot_general | solution.py:243
  198.8 8.8 %bitcast_add_fusion.1 = f32[512,4608]{1,0:T(8,128)} fusion(f32[4608,512]{0,1:T(8,128)} %fusion.120, bf16[512,128]{1,0:T(8,128)(2,1)S(1)} %fusion.91, bf16[4608,128]{1,0:T(8,128)(2,1)S(1)} %copy-done.26), kind=kOutput, calls=%fused_computation.1 | convolution fusion | flops 606339072 | bytes 20185088 | tf_op jit(solution)/shard_map/dot_general | solution.py:243
  207.6 5.0 bitcast_add_fusion
  223.9 8.0 %fusion.6 = f32[512,4608]{1,0:T(8,128)S(1)} fusion(bf16[512,1024]{1,0:T(8,128)(2,1)S(1)} %get-tuple-element.63, bf16[2,1024,4608]{2,1,0:T(8,128)(2,1)} %get-tuple-element.18), kind=kOutput, calls=%fused_computation.8 | convolution fusion | flops 4831838208 | bytes 19922944 | tf_op jit(solution)/shard_map/dot_general | solution.py:239
  231.9 11.1 %fusion.14 = f32[512,4608]{1,0:T(8,128)} fusion(bf16[512,1024]{1,0:T(8,128)(2,1)S(1)} %get-tuple-element.63, bf16[2,1024,4608]{2,1,0:T(8,128)(2,1)} %get-tuple-element.18), kind=kOutput, calls=%fused_computation.16 | convolution fusion | flops 4831838208 | bytes 19922944 | tf_op jit(solution)/shard_map/dot_general | solution.py:239
  243.0 11.0 %fusion.12 = f32[512,4608]{1,0:T(8,128)} fusion(bf16[512,1024]{1,0:T(8,128)(2,1)S(1)} %get-tuple-element.64, bf16[2,1024,4608]{2,1,0:T(8,128)(2,1)} %get-tuple-element.18), kind=kOutput, calls=%fused_computation.14 | convolution fusion | flops 4831838208 | bytes 19922944 | tf_op jit(solution)/shard_map/dot_general | solution.py:239
  254.0 11.2 %fusion.4 = f32[512,4608]{1,0:T(8,128)} fusion(bf16[512,1024]{1,0:T(8,128)(2,1)S(1)} %get-tuple-element.64, bf16[2,1024,4608]{2,1,0:T(8,128)(2,1)} %get-tuple-element.18), kind=kOutput, calls=%fused_computation.6 | convolution fusion | flops 4831838208 | bytes 19922944 | tf_op jit(solution)/shard_map/dot_general | solution.py:239
  267.1 5.0 multiply_add_fusion.2
  272.1 17.3 %multiply_convert_fusion.3 = (bf16[512,4608]{1,0:T(8,128)(2,1)}, bf16[512,4608]{1,0:T(8,128)(2,1)}, bf16[512,4608]{1,0:T(8,128)(2,1)}) fusion(f32[512,4608]{1,0:T(8,128)} %bitcast_add_fusion.1, f32[512,4608]{1,0:T(8,128)} %multiply_add_fusion.2, f32[512,4608]{1,0:T(8,128)} %fusion.14, bf16[512,128]{1,0:T(8,128)(2,1)S(1)} %fusion.105, ...), kind=kOutput, calls=%fused_computation.21 | convolution fusion | flops 644087808 | bytes 43778048 | tf_op jit(solution)/shard_map/dot_general | solution.py:239
  289.4 4.5 fusion.101
  304.1 5.0 multiply_add_fusion
  309.1 17.0 %multiply_convert_fusion.1 = (bf16[512,4608]{1,0:T(8,128)(2,1)}, bf16[512,4608]{1,0:T(8,128)(2,1)}, bf16[512,4608]{1,0:T(8,128)(2,1)}) fusion(f32[512,4608]{1,0:T(8,128)} %bitcast_add_fusion, f32[512,4608]{1,0:T(8,128)} %multiply_add_fusion, f32[512,4608]{1,0:T(8,128)} %fusion.12, bf16[512,128]{1,0:T(8,128)(2,1)S(1)} %fusion.109, ...), kind=kOutput, calls=%fused_computation.19 | convolution fusion | flops 644087808 | bytes 43778048 | tf_op jit(solution)/shard_map/dot_general | solution.py:239
  330.0 10.2 %fusion = f32[512,1024]{1,0:T(8,128)} fusion(bf16[512,4608]{1,0:T(8,128)(2,1)} %get-tuple-element.46, bf16[2,1024,4608]{2,1,0:T(8,128)(2,1)} %get-tuple-element.18), kind=kOutput, calls=%fused_computation.2 | convolution fusion | flops 4831838208 | bytes 16252928 | tf_op jit(solution)/shard_map/dot_general | solution.py:243
  340.3 9.4 %fusion.2 = f32[512,1024]{1,0:T(8,128)} fusion(bf16[512,4608]{1,0:T(8,128)(2,1)S(1)} %bitcast.256, bf16[2,1024,4608]{2,1,0:T(8,128)(2,1)} %get-tuple-element.18), kind=kOutput, calls=%fused_computation.4 | convolution fusion | flops 4831838208 | bytes 16252928 | tf_op jit(solution)/shard_map/dot_general | solution.py:243
  357.4 11.2 %multiply_reduce_fusion = (f32[512]{0:T(512)S(1)}, f32[512,1024]{1,0:T(8,128)}) fusion(f32[512,1024]{1,0:T(8,128)S(1)} %get-tuple-element.70, f32[512]{0:T(512)S(1)} %get-tuple-element.76, f32[1024]{0:T(1024)S(1)} %convert_element_type.235, f32[512,1024]{1,0:T(8,128)} %fusion, f32[512,1024]{1,0:T(8,128)} %fusion.165, f32[512,1024]{1,0:T(8,128)S(1)} %fusion.164, ...), kind=kOutput, calls=%fused_computation.124 | convolution fusion | flops 4835507712 | bytes 24649728 | tf_op jit(solution)/shard_map/dot_general | solution.py:243
  368.6 11.2 %multiply_reduce_fusion.1 = (f32[512]{0:T(512)S(1)}, f32[512,1024]{1,0:T(8,128)}) fusion(f32[512,1024]{1,0:T(8,128)S(1)} %copy-done.7, f32[512]{0:T(512)S(1)} %copy-done.99, f32[1024]{0:T(1024)S(1)} %convert_element_type.235, f32[512,1024]{1,0:T(8,128)} %fusion.2, f32[512,1024]{1,0:T(8,128)} %fusion.162, f32[512,1024]{1,0:T(8,128)S(1)} %fusion.161, ...), kind=kOutput, calls=%fused_computation.131 | convolution fusion | flops 4835507712 | bytes 24649728 | tf_op jit(solution)/shard_map/dot_general | solution.py:243
  390.3 9.2 %fusion.158 = f32[512,1024]{1,0:T(8,128)} fusion(bf16[512,4608]{1,0:T(8,128)(2,1)S(1)} %bitcast.248, bf16[4608,1024]{1,0:T(8,128)(2,1)} %get-tuple-element.19), kind=kOutput, calls=%fused_computation.256 | convolution fusion | flops 4831838208 | bytes 16252928 | tf_op jit(solution)/shard_map/dot_general | solution.py:239
  401.6 9.2 %fusion.160 = f32[512,1024]{1,0:T(8,128)} fusion(bf16[512,4608]{1,0:T(8,128)(2,1)S(1)} %bitcast.246, bf16[4608,1024]{1,0:T(8,128)(2,1)} %get-tuple-element.19), kind=kOutput, calls=%fused_computation.258 | convolution fusion | flops 4831838208 | bytes 16252928 | tf_op jit(solution)/shard_map/dot_general | solution.py:239
  457.2 7.6 %add_multiply_fusion = f32[512,1024]{1,0:T(8,128)S(1)} fusion(f32[512,1024]{1,0:T(8,128)} %fusion.166, bf16[1024,3072]{1,0:T(8,128)(2,1)} %get-tuple-element.16, f32[1024]{0:T(1024)S(1)} %copy-done.106, bf16[512,1024]{1,0:T(8,128)(2,1)} %copy-done.52, bf16[512,1024]{1,0:T(8,128)(2,1)S(1)} %copy-done.44, bf16[512,1024]{1,0:T(8,128)(2,1)} %get-tuple-element.56), kind=kOutput, calls=%fused_computation.119 | convolution fusion | flops 3231711232 | bytes 13635584 | tf_op jit(solution)/shard_map/dot_general | solution.py:243
  464.9 6.8 %fusion.66 = (f32[512]{0:T(512)S(1)}, f32[512]{0:T(512)S(1)}, f32[512,1024]{1,0:T(8,128)S(1)}) fusion(f32[512]{0:T(512)S(1)} %copy-done.104, bf16[2,1,512,1024]{3,2,1,0:T(8,128)(2,1)S(1)} %copy-done.23, f32[512,1024]{1,0:T(8,128)S(1)} %add_multiply_fusion, f32[512]{0:T(512)S(1)} %copy-done.102, f32[1024]{0:T(1024)S(1)} %copy-done.106, ...), kind=kOutput, calls=%fused_computation.102 | convolution fusion | flops 3235904512 | bytes 17838080 | tf_op jit(solution)/shard_map/dot_general | solution.py:243
  474.4 141.6 %all-reduce.3.cloned.1.call-done = (bf16[1024,128]{1,0:T(8,128)(2,1)}, bf16[128,3072]{1,0:T(8,128)(2,1)}, bf16[1024,128]{1,0:T(8,128)(2,1)}, bf16[128,1024]{1,0:...) async-done(((bf16[1024,128]{1,0:T(8,128)(2,1)}, ...) | async-done | bytes 5898256 | tf_op jit(solution)/shard_map/psum | solution.py:415
  (397 shorter events, 129.8 us)
Async XLA Ops:
  7.2 264.9 %copy-start = (bf16[128,4608]{1,0:T(8,128)(2,1)S(1)}, bf16[128,4608]{1,0:T(8,128)(2,1)}, u32[]{:S(2)}) copy-start(bf16[128,4608]{1,0:T(8,128)(2,1)} %param.37) | copy-start | bytes 3538948
  7.2 608.8 %all-reduce.3.cloned.1.call-start = ((), (), s32[]{:S(2)}) async-start(), calls=%async_computation | async-start | bytes 11796480 | tf_op jit(solution)/shard_map/psum | solution.py:415
  8.0 164.8 %copy-start.105 = (f32[1024]{0:T(1024)}, f32[1024]{0:T(1024)S(1)}, u32[]{:S(2)}) copy-start(f32[1024]{0:T(1024)S(1)} %convert_element_type.229) | copy-start | bytes 12292
  10.0 256.6 %copy-start.110 = (pred[128]{0:T(512)(128)(4,1)}, pred[128]{0:T(512)(128)(4,1)S(1)}, u32[]{:S(2)}) copy-start(pred[128]{0:T(512)(128)(4,1)S(1)} %broadcast_compare_fusion) | copy-start | bytes 388
  10.0 147.4 %copy-start.20 = (bf16[2,1,512,1024]{3,2,1,0:T(8,128)(2,1)S(1)}, bf16[2,1,512,1024]{3,2,1,0:T(8,128)(2,1)}, u32[]{:S(2)}) copy-start(bf16[2,1,512,1024]{3,2,1,0:T(8,128)(2,1)} %param.21) | copy-start | bytes 6291460
  12.2 151.0 %copy-start.101 = (f32[512]{0:T(512)}, f32[512]{0:T(512)S(1)}, u32[]{:S(2)}) copy-start(f32[512]{0:T(512)S(1)} %add_rsqrt_fusion.1) | copy-start | bytes 6148
  165.3 47.3 %copy-start.2 = (f32[512,3072]{1,0:T(8,128)}, f32[512,3072]{1,0:T(8,128)S(1)}, u32[]{:S(2)}) copy-start(f32[512,3072]{1,0:T(8,128)S(1)} %multiply_add_fusion.4) | copy-start | bytes 18874372
  165.9 46.7 %collective-permute-start.1 = (f32[1,2,1024]{2,1,0:T(2,128)S(1)}, f32[1,2,1024]{2,1,0:T(2,128)S(1)}, u32[]{:S(2)}, u32[]{:S(2)}) collective-permute-start(f32[1,2,1024]{2,1,0:T(2,128)S(1)} %slice.137), channel_id=1, source_target_pairs={{0,1},{2,3},{4,5},{6,7},{8,9},{10,11},{12,13},{14,15},{16,17},{18,... | collective-permute-start | bytes 24584 | tf_op jit(solution)/shard_map/ppermute | solution.py:235
  175.0 37.6 %copy-start.3 = (f32[512,3072]{1,0:T(8,128)}, f32[512,3072]{1,0:T(8,128)S(1)}, u32[]{:S(2)}) copy-start(f32[512,3072]{1,0:T(8,128)S(1)} %multiply_add_fusion.5) | copy-start | bytes 18874372
  175.6 37.0 %collective-permute-start = (f32[1,2,1024]{2,1,0:T(2,128)S(1)}, f32[1,2,1024]{2,1,0:T(2,128)S(1)}, u32[]{:S(2)}, u32[]{:S(2)}) collective-permute-start(f32[1,2,1024]{2,1,0:T(2,128)S(1)} %slice.129), channel_id=1, source_target_pairs={{0,1},{2,3},{4,5},{6,7},{8,9},{10,11},{12,13},{14,15},{16,17},{18,... | collective-permute-start | bytes 24584 | tf_op jit(solution)/shard_map/ppermute | solution.py:235
  223.9 42.7 %copy-start.11 = (bf16[512,1024]{1,0:T(8,128)(2,1)}, bf16[512,1024]{1,0:T(8,128)(2,1)S(1)}, u32[]{:S(2)}) copy-start(bf16[512,1024]{1,0:T(8,128)(2,1)S(1)} %get-tuple-element.64) | copy-start | bytes 3145732
  266.2 37.9 %copy-start.62 = (bf16[512,128]{1,0:T(8,128)(2,1)}, bf16[512,128]{1,0:T(8,128)(2,1)S(1)}, u32[]{:S(2)}) copy-start(bf16[512,128]{1,0:T(8,128)(2,1)S(1)} %fusion.110) | copy-start | bytes 393220
  267.1 42.0 %copy-start.90 = (bf16[512,128]{1,0:T(8,128)(2,1)}, bf16[512,128]{1,0:T(8,128)(2,1)S(1)}, u32[]{:S(2)}) copy-start(bf16[512,128]{1,0:T(8,128)(2,1)S(1)} %fusion.109) | copy-start | bytes 393220
  272.1 21.8 %copy-start.68 = (bf16[512,128]{1,0:T(8,128)(2,1)S(1)}, bf16[512,128]{1,0:T(8,128)(2,1)}, u32[]{:S(2)}) copy-start(bf16[512,128]{1,0:T(8,128)(2,1)} %copy-done.67) | copy-start | bytes 393220
  304.1 45.5 %copy-start.72 = (bf16[512,128]{1,0:T(8,128)(2,1)}, bf16[512,128]{1,0:T(8,128)(2,1)S(1)}, u32[]{:S(2)}) copy-start(bf16[512,128]{1,0:T(8,128)(2,1)S(1)} %fusion.95) | copy-start | bytes 393220
  326.1 14.1 %slice-start.17 = ((s8[4718592]{0:T(1024)(128)(4,1)}), s8[4194304]{0:T(1024)(128)(4,1)S(1)}, s32[]{:S(2)}) async-start(s8[4718592]{0:T(1024)(128)(4,1)} %bitcast.255), calls=%async_computation.18 | async-start | bytes 8388608
  330.0 25.6 %copy-start.75 = (bf16[512,128]{1,0:T(8,128)(2,1)}, bf16[512,128]{1,0:T(8,128)(2,1)S(1)}, u32[]{:S(2)}) copy-start(bf16[512,128]{1,0:T(8,128)(2,1)S(1)} %fusion.99) | copy-start | bytes 393220
  330.0 23.7 %slice-start.19 = ((s8[4718592]{0:T(1024)(128)(4,1)}), s8[4194304]{0:T(1024)(128)(4,1)S(1)}, s32[]{:S(2)}) async-start(s8[4718592]{0:T(1024)(128)(4,1)} %bitcast.257), calls=%async_computation.20 | async-start | bytes 8388608
  340.3 13.5 %slice-start.20 = ((s8[4718592]{0:T(1024)(128)(4,1)}), s8[524288]{0:T(1024)(128)(4,1)S(1)}, s32[]{:S(2)}) async-start(s8[4718592]{0:T(1024)(128)(4,1)} %bitcast.257), calls=%async_computation.21 | async-start | bytes 1048576
  355.1 13.4 %slice-start.13 = ((s8[4718592]{0:T(1024)(128)(4,1)}), s8[4194304]{0:T(1024)(128)(4,1)S(1)}, s32[]{:S(2)}) async-start(s8[4718592]{0:T(1024)(128)(4,1)} %bitcast.251), calls=%async_computation.14 | async-start | bytes 8388608
  382.6 37.3 %copy-start.4 = (f32[512,1024]{1,0:T(8,128)}, f32[512,1024]{1,0:T(8,128)S(1)}, u32[]{:S(2)}) copy-start(f32[512,1024]{1,0:T(8,128)S(1)} %get-tuple-element.53) | copy-start | bytes 6291460
  399.6 14.1 %slice-start.21 = ((s8[4718592]{0:T(1024)(128)(4,1)}), s8[4194304]{0:T(1024)(128)(4,1)S(1)}, s32[]{:S(2)}) async-start(s8[4718592]{0:T(1024)(128)(4,1)} %bitcast.259), calls=%async_computation.22 | async-start | bytes 8388608
  425.1 11.3 %collective-permute-start.3 = (f32[1,2,1024]{2,1,0:T(2,128)S(1)}, f32[1,2,1024]{2,1,0:T(2,128)S(1)}, u32[]{:S(2)}, u32[]{:S(2)}) collective-permute-start(f32[1,2,1024]{2,1,0:T(2,128)S(1)} %slice.143), channel_id=1, source_target_pairs={{1,0},{3,2},{5,4},{7,6},{9,8},{11,10},{13,12},{15,14},{17,16},{19,... | collective-permute-start | bytes 24584 | tf_op jit(solution)/shard_map/ppermute | solution.py:235
  430.9 5.9 collective-permute-start.2
  (118 other events, 489.1 us)
Sparse Core Ops, SparseCore 0:
  456.1 159.8 all-reduce.2

commit v2 on v0

v2 whole, which is shorter than its diff:
```python
import functools

import jax
import jax.numpy as jnp
from jax import lax
from jax.experimental import pallas as pl
from jax.experimental.pallas import tpu as pltpu
from jax.sharding import PartitionSpec as P

R = 16
LANES = 128
EPSILON = 1e-05
ADAPTER_SCALE = 0.5
MESH = pl.DeviceIdType.MESH
BF16 = jnp.bfloat16
F32 = jnp.float32
VMEM_LIMIT = 62 * 1024 * 1024
FF_CHUNK = 768
ROW_BLOCK = 256


def from_behind(block, axis, distance):
    devices = range(lax.axis_size(axis))
    route = [(i - distance, i) for i in devices if i - distance in devices]
    return lax.ppermute(block, axis, route)


def dot_nn(left, right):
    return jnp.dot(left, right, preferred_element_type=F32)


def dot_nt(left, right):
    return lax.dot_general(left, right, (((1,), (1,)), ((), ())), preferred_element_type=F32)


def dot_tn(left, right):
    return lax.dot_general(left, right, (((0,), (0,)), ((), ())), preferred_element_type=F32)


def when(condition, action):
    if isinstance(condition, bool):
        if condition:
            action()
    else:
        pl.when(condition)(action)


class Ring:
    def __init__(self, fsdp_size):
        self.count = fsdp_size // 2
        self.me = lax.axis_index("fsdp")
        self.core = lax.rem(self.me, 2)
        chip = self.me // 2
        self.grid = fsdp_size == 16
        if self.grid:
            z, y = chip // 2, lax.rem(chip, 2)
            self.place = y * z + (1 - y) * (7 - z)
        else:
            self.place = chip
        x = lax.axis_index("seq")
        self.x = x
        self.role = lax.rem(x, 2)
        self.to_next = {"fsdp": self.device(lax.rem(self.place + 1, self.count))}
        self.to_prev = {"fsdp": self.device(lax.rem(self.place + self.count - 1, self.count))}
        self.to_core = {"fsdp": self.me + 1 - 2 * self.core}
        self.to_seq = {"seq": x + 1 - 2 * self.role}

    def device(self, place):
        if self.grid:
            y = 1 - place // 4
            z = y * place + (1 - y) * (7 - place)
            return (z * 2 + y) * 2 + self.core
        return place * 2 + self.core

    def at_step(self, direction, step):
        if direction == 0:
            return self.device(lax.rem(self.place + self.count - step, self.count))
        return self.device(lax.rem(self.place + step, self.count))

    def greet(self):
        barrier = pltpu.get_barrier_semaphore()
        for device in (self.to_next, self.to_prev, self.to_core, self.to_seq):
            pl.semaphore_signal(barrier, inc=1, device_id=device, device_id_type=MESH)
        pl.semaphore_wait(barrier, 4)


class Unit:
    def __init__(self, ring, number, spot, sems):
        self.ring, self.number, self.spot = ring, number, spot
        self.send, self.ring_sem, self.seq_sem, self.core_sem = sems
        half = ring.count // 2
        self.reaches = ((half, ring.count - 1 - half), (ring.count - 1 - half, half))
        self.steps = half
        self.others = ring.count - 1

    def copy(self, spot, slot, sem, device):
        return pltpu.make_async_remote_copy(
            src_ref=spot,
            dst_ref=spot,
            send_sem=self.send.at[self.number, slot],
            recv_sem=sem,
            device_id=device,
            device_id_type=MESH,
        )

    def arrived(self, spot, sem):
        self.copy(spot, 0, sem, self.ring.to_next).wait_recv()

    def own(self):
        ring, n = self.ring, self.number
        for slot, third in ((0, ring.role), (1, 2)):
            spot = self.spot(third, ring.me)
            self.copy(spot, 2 * slot, self.ring_sem.at[n, slot, 0], ring.to_next).start()
            self.copy(spot, 2 * slot + 1, self.ring_sem.at[n, slot, self.others - 1], ring.to_prev).start()
        for k, third in enumerate((ring.role, 1 - ring.role, 2)):
            self.copy(self.spot(third, ring.me), 4 + k, self.core_sem.at[n, third, 0], ring.to_core).start()

    def relay(self, step):
        ring, n, others = self.ring, self.number, self.others
        for slot, third in ((0, ring.role), (1, 2)):
            for direction in (0, 1):
                reach = self.reaches[slot][direction]
                lane = step - 1 if direction == 0 else others - step
                spot = self.spot(third, ring.at_step(direction, step))

                def forward(slot=slot, direction=direction, lane=lane, spot=spot):
                    onward = self.ring_sem.at[n, slot, lane + 1 - 2 * direction]
                    target = (ring.to_next, ring.to_prev)[direction]
                    self.copy(spot, 7 + slot * others + lane, onward, target).start()

                def take(slot=slot, third=third, reach=reach, lane=lane, spot=spot, forward=forward):
                    self.arrived(spot, self.ring_sem.at[n, slot, lane])
                    when(step < reach, forward)
                    if slot == 0:
                        self.copy(spot, 7 + 2 * others + lane, self.seq_sem.at[n, lane], ring.to_seq).start()
                    core = self.core_sem.at[n, third, 1 + lane]
                    self.copy(spot, 7 + (3 + slot) * others + lane, core, ring.to_core).start()

                when(step <= reach, take)

    def relay_seq(self, step):
        ring, n, others = self.ring, self.number, self.others
        third = 1 - ring.role
        for direction in (0, 1):
            reach = self.reaches[0][direction]
            lane = step - 1 if direction == 0 else others - step
            spot = self.spot(third, ring.at_step(direction, step))

            def take(lane=lane, spot=spot):
                self.arrived(spot, self.seq_sem.at[n, lane])
                core = self.core_sem.at[n, third, 1 + lane]
                self.copy(spot, 7 + 5 * others + lane, core, ring.to_core).start()

            when(step <= reach, take)

    def collect(self):
        for third in range(3):
            for lane in range(self.others + 1):
                self.arrived(self.spot(third, self.ring.me), self.core_sem.at[self.number, third, lane])

    def drain(self):
        ring, others = self.ring, self.others

        def done(third, slot):
            self.copy(self.spot(third, ring.me), slot, self.seq_sem.at[self.number, 0], ring.to_next).wait_send()

        for slot, third in ((0, 0), (1, 2)):
            done(third, 2 * slot)
            done(third, 2 * slot + 1)
            for direction in (0, 1):
                reach = self.reaches[slot][direction]
                for step in range(1, reach + 1):
                    lane = step - 1 if direction == 0 else others - step
                    if step < reach:
                        done(third, 7 + slot * others + lane)
                    done(third, 7 + (3 + slot) * others + lane)
        for lane in range(others):
            done(0, 7 + 2 * others + lane)
            done(0, 7 + 5 * others + lane)
        for k, third in enumerate((0, 0, 2)):
            done(third, 4 + k)


def unit_sems(units, count):
    return [
        pltpu.SemaphoreType.DMA((units, 7 + 6 * (count - 1))),
        pltpu.SemaphoreType.DMA((units, 2, count - 1)),
        pltpu.SemaphoreType.DMA((units, count - 1)),
        pltpu.SemaphoreType.DMA((units, 3, count)),
    ]


def in_order(units, lag=2):
    entries = []
    for k, unit in enumerate(units):
        entries.append((k, 0, unit.own))
        for step in range(1, unit.steps + 1):
            entries.append((k + step, 1, functools.partial(unit.relay, step)))
            entries.append((k + step + lag, 2, functools.partial(unit.relay_seq, step)))
    for entry in sorted(entries, key=lambda entry: entry[:2]):
        entry[2]()


def move_in(moves, sems):
    inward = [pltpu.make_async_copy(a, b, sems.at[0, k]) for k, (a, b, _) in enumerate(moves)]
    outward = [pltpu.make_async_copy(b, c, sems.at[1, k]) for k, (_, b, c) in enumerate(moves)]
    for copy in inward:
        copy.start()
    for first, second in zip(inward, outward):
        first.wait()
        second.start()
    return outward


def row_spot(landing, rows, third, owner, columns=None):
    return landing.at[pl.ds(owner * rows + third * (rows // 3), rows // 3), :]


def column_spot(landing, rows, width, last, third, owner):
    size = last if isinstance(third, int) and third == 2 else width
    start = third * width if isinstance(third, int) else pl.multiple_of(third * width, LANES)
    return landing.at[pl.ds(owner * rows, rows), pl.ds(start, size)]


def chunk_spot(landing, rows, size, chunk, third, owner):
    start = pl.multiple_of((chunk * 3 + third) * size, LANES)
    return landing.at[:, pl.ds(owner * rows, rows), pl.ds(start, size)]


def mixer_gather_kernel(fsdp_size, in_own, out_own, in_all, out_all, s0, s1, s2, s3, local_sem, held_in, held_out):
    ring = Ring(fsdp_size)
    rows = in_own.shape[0]
    mine = pl.ds(ring.me * rows, rows)
    moved = move_in([(in_own, held_in, in_all.at[mine, :]), (out_own, held_out, out_all.at[mine, :])], local_sem)
    ring.greet()
    for copy in moved:
        copy.wait()
    part = in_all.shape[1] // 3
    out_x = 3 * out_all.shape[1] // 8
    sems = (s0, s1, s2, s3)
    units = [
        Unit(ring, 0, functools.partial(column_spot, in_all, rows, part, part), sems),
        Unit(ring, 1, functools.partial(column_spot, out_all, rows, out_x, out_all.shape[1] - 2 * out_x), sems),
    ]
    in_order(units)
    for unit in units:
        unit.collect()
    for unit in units:
        unit.drain()


ANYWHERE = pl.BlockSpec(memory_space=pl.ANY)
IN_VMEM = pl.BlockSpec(memory_space=pltpu.VMEM)


def gather_mixer(fsdp_size, in_weight, out_weight):
    rows = fsdp_size * in_weight.shape[0]
    own = (in_weight, out_weight)
    return pl.pallas_call(
        functools.partial(mixer_gather_kernel, fsdp_size),
        out_shape=tuple(jax.ShapeDtypeStruct((rows, member.shape[1]), BF16) for member in own),
        in_specs=[ANYWHERE] * 2,
        out_specs=(ANYWHERE,) * 2,
        scratch_shapes=unit_sems(2, fsdp_size // 2)
        + [pltpu.SemaphoreType.DMA((2, 2))]
        + [pltpu.VMEM(member.shape, BF16) for member in own],
        compiler_params=pltpu.CompilerParams(collective_id=0, has_side_effects=True),
    )(*own)


def slot_mask(rows, slots, per_sequence, base=0):
    row = lax.broadcasted_iota(jnp.int32, (rows, slots), 0)
    column = lax.broadcasted_iota(jnp.int32, (rows, slots), 1)
    return (row // per_sequence == column // R).astype(F32)


def feed_forward_kernel(fsdp_size, per_sequence, *refs):
    (
        second, cotangent, after, pick, pick_t,
        gate_first, gate_second, up_first, up_second, down_first, down_second,
        gate_own, up_own, down_own,
    ) = refs[:14]
    block_out, grad_second, grads, gu_all, down_all = refs[14:19]
    sems, local_sem, load_sem = refs[19:23], refs[23], refs[24]
    (
        held_gate, held_up, held_down, total, grad_hidden, gate_w, up_w, down_w, hidden_s, gate_s, up_s,
        first_gu, first_down, second_gu, second_down, low_gu, grad_low_down, low_down, grad_low_gu,
    ) = refs[25:]
    ring = Ring(fsdp_size)
    rows, down_rows = gate_own.shape[0], down_own.shape[0]
    tokens, features = second.shape
    hidden_size = gate_own.shape[1]
    chunks = hidden_size // FF_CHUNK
    slots = pick.shape[1]
    blocks = tokens // ROW_BLOCK
    mine = pl.ds(ring.me * rows, rows)
    moved = move_in(
        [
            (down_own, held_down, down_all.at[pl.ds(ring.me * down_rows, down_rows), :]),
            (gate_own, held_gate, gu_all.at[0, mine, :]),
            (up_own, held_up, gu_all.at[1, mine, :]),
        ],
        local_sem,
    )
    started = pltpu.make_async_copy(after, total, load_sem.at[2, 0])
    started.start()
    ring.greet()
    for copy in moved:
        copy.wait()
    down_unit = Unit(ring, 0, functools.partial(row_spot, down_all, down_rows), sems)

    def chunk_unit(k):
        return Unit(ring, 1 + k, functools.partial(chunk_spot, gu_all, rows, FF_CHUNK // 3, k), sems)

    steps = down_unit.steps
    down_unit.own()
    chunk_unit(0).own()

    for k, (first, second_map) in enumerate(((gate_first, gate_second), (up_first, up_second))):
        first_gu[k] = dot_nn(first[...], pick[...]).astype(BF16)
        for j in range(chunks):
            part = dot_nn(pick_t[...], second_map[:, j * FF_CHUNK : (j + 1) * FF_CHUNK])
            second_gu[k, j] = part.astype(BF16)
    second_down[...] = dot_nn(pick_t[...], down_second[...]).astype(BF16)
    for j in range(chunks):
        first_down[j] = dot_nn(down_first[j * FF_CHUNK : (j + 1) * FF_CHUNK, :], pick[...]).astype(BF16)
    mask = slot_mask(tokens, slots, per_sequence)
    for k in range(2):
        low = (dot_nn(second[...], first_gu[k]) * mask).astype(BF16)
        low_gu[k] = low * ADAPTER_SCALE
    grad_low_down[...] = (ADAPTER_SCALE * dot_nt(cotangent[...], second_down[...]) * mask).astype(BF16)
    grad_second[...] = jnp.zeros_like(grad_second)
    low_down[...] = jnp.zeros_like(low_down)
    grad_low_gu[...] = jnp.zeros_like(grad_low_gu)

    for step in range(1, steps + 1):
        down_unit.relay(step)
    for step in range(1, steps + 1):
        down_unit.relay_seq(step)
    down_unit.collect()

    def down_load(j, s):
        place = pl.ds(pl.multiple_of(j * FF_CHUNK, FF_CHUNK), FF_CHUNK)
        return pltpu.make_async_copy(down_all.at[place, :], down_w.at[s], load_sem.at[s, 0])

    def gu_loads(j, s):
        place = pl.ds(pl.multiple_of(j * FF_CHUNK, FF_CHUNK), FF_CHUNK)
        return (
            pltpu.make_async_copy(gu_all.at[0, :, place], gate_w.at[s], load_sem.at[s, 1]),
            pltpu.make_async_copy(gu_all.at[1, :, place], up_w.at[s], load_sem.at[s, 2]),
        )

    per_tick = -(-steps // blocks)

    def ticks(unit_action, r):
        for k in range(per_tick):
            step = r * per_tick + k + 1
            when(step <= steps, functools.partial(unit_action, step))

    down_load(0, 0).start()

    @pl.loop(0, chunks)
    def _(j):
        s = lax.rem(j, 2)

        @pl.when(j + 1 < chunks)
        def _():
            down_load(j + 1, 1 - s).start()

        down_load(j, s).wait()

        @pl.loop(0, blocks)
        def _(r):
            at = pl.ds(pl.multiple_of(r * ROW_BLOCK, ROW_BLOCK), ROW_BLOCK)

            @pl.when(j == 0)
            def _():
                ticks(chunk_unit(0).relay, r)

            @pl.when((j == 1) & (r == 0))
            def _():
                chunk_unit(1).own()

            @pl.when(j == 2)
            def _():
                ticks(chunk_unit(0).relay_seq, r)

            @pl.when(j == 3)
            def _():
                ticks(chunk_unit(1).relay, r)

            @pl.when((j == 4) & (r == 0))
            def _():
                chunk_unit(2).own()

            grad_hidden[j, at, :] = dot_nt(cotangent[at, :], down_w[s]) + dot_nt(
                grad_low_down[at, :], first_down[j]
            )

    started.wait()
    chunk_unit(0).collect()
    for copy in gu_loads(0, 0):
        copy.start()
    down_load(0, 0).start()

    @pl.loop(0, chunks)
    def _(j):
        s = lax.rem(j, 2)
        for copy in (down_load(j, s),) + gu_loads(j, s):
            copy.wait()

        @pl.loop(0, blocks)
        def _(r):
            at = pl.ds(pl.multiple_of(r * ROW_BLOCK, ROW_BLOCK), ROW_BLOCK)

            @pl.when((r == 0) & (j + 3 < chunks))
            def _():
                chunk_unit(j + 3).own()

            @pl.when(j + 2 < chunks)
            def _():
                ticks(chunk_unit(j + 2).relay, r)

            @pl.when(j + 1 < chunks)
            def _():
                spread = -(-steps // max(blocks - 1, 1))
                for k in range(spread):
                    step = r * spread + k + 1
                    when(step <= steps, functools.partial(chunk_unit(j + 1).relay_seq, step))

                @pl.when(r == blocks - 1)
                def _():
                    chunk_unit(j + 1).collect()
                    for copy in (down_load(j + 1, 1 - s),) + gu_loads(j + 1, 1 - s):
                        copy.start()

            rows_in = second[at, :]
            gate = dot_nn(rows_in, gate_w[s]) + dot_nn(low_gu[0, at, :], second_gu[0, j])
            up = dot_nn(rows_in, up_w[s]) + dot_nn(low_gu[1, at, :], second_gu[1, j])
            back = grad_hidden[j, at, :]
            sigmoid = 1.0 / (1.0 + jnp.exp(-gate))
            active = gate * sigmoid
            hidden = (active * up).astype(BF16)
            grad_gate = (back * up * sigmoid * (1.0 + gate * (1.0 - sigmoid))).astype(BF16)
            grad_up = (back * active).astype(BF16)
            hidden_s[at, :] = hidden
            gate_s[at, :] = grad_gate
            up_s[at, :] = grad_up
            total[at, :] += dot_nn(hidden, down_w[s])
            grad_second[at, :] += dot_nt(grad_gate, gate_w[s]) + dot_nt(grad_up, up_w[s])
            low_down[at, :] += dot_nn(hidden, first_down[j])
            grad_low_gu[0, at, :] += dot_nt(grad_gate, second_gu[0, j])
            grad_low_gu[1, at, :] += dot_nt(grad_up, second_gu[1, j])

        base = j * FF_CHUNK
        for offset, left, right in (
            (2 * features, grad_low_down[...], hidden_s),
            (2 * features + hidden_size, low_gu[0], gate_s),
            (2 * features + 2 * hidden_size, low_gu[1], up_s),
        ):
            columns = pl.ds(pl.multiple_of(offset + base, LANES), FF_CHUNK)
            grads[:, columns] = dot_tn(left, right[...]).astype(BF16)

    half_low_down = (ADAPTER_SCALE * low_down[...] * mask).astype(BF16)
    block_out[...] = (total[...] + dot_nn(half_low_down, second_down[...])).astype(BF16)
    base = 2 * features + 3 * hidden_size
    grads[:, base : base + features] = dot_tn(half_low_down, cotangent[...]).astype(BF16)
    for k in range(2):
        back_low = (ADAPTER_SCALE * grad_low_gu[k] * mask).astype(BF16)
        grads[:, k * features : (k + 1) * features] = dot_tn(back_low, second[...]).astype(BF16)
        grad_second[...] += dot_nt(back_low, first_gu[k])

    down_unit.drain()

    @pl.loop(0, chunks)
    def _(k):
        chunk_unit(k).drain()


def feed_forward(fsdp_size, per_sequence, second, cotangent, after, pick, pick_t, adapters, own):
    tokens, features = second.shape
    hidden_size = own[0].shape[1]
    slots = pick.shape[1]
    chunks = hidden_size // FF_CHUNK
    grads_width = 3 * features + 3 * hidden_size
    return pl.pallas_call(
        functools.partial(feed_forward_kernel, fsdp_size, per_sequence),
        out_shape=(
            jax.ShapeDtypeStruct((tokens, features), BF16),
            jax.ShapeDtypeStruct((tokens, features), F32),
            jax.ShapeDtypeStruct((slots, grads_width), BF16),
            jax.ShapeDtypeStruct((2, features, hidden_size), BF16),
            jax.ShapeDtypeStruct((hidden_size, features), BF16),
        ),
        in_specs=[IN_VMEM, IN_VMEM, ANYWHERE] + [IN_VMEM] * 8 + [ANYWHERE] * 3,
        out_specs=(IN_VMEM, IN_VMEM, IN_VMEM, ANYWHERE, ANYWHERE),
        scratch_shapes=unit_sems(1 + chunks, fsdp_size // 2)
        + [pltpu.SemaphoreType.DMA((2, 3)), pltpu.SemaphoreType.DMA((3, 3))]
        + [pltpu.VMEM(member.shape, BF16) for member in own]
        + [
            pltpu.VMEM((tokens, features), F32),
            pltpu.VMEM((chunks, tokens, FF_CHUNK), F32),
            pltpu.VMEM((2, features, FF_CHUNK), BF16),
            pltpu.VMEM((2, features, FF_CHUNK), BF16),
            pltpu.VMEM((2, FF_CHUNK, features), BF16),
            pltpu.VMEM((tokens, FF_CHUNK), BF16),
            pltpu.VMEM((tokens, FF_CHUNK), BF16),
            pltpu.VMEM((tokens, FF_CHUNK), BF16),
            pltpu.VMEM((2, features, slots), BF16),
            pltpu.VMEM((chunks, FF_CHUNK, slots), BF16),
            pltpu.VMEM((2, chunks, slots, FF_CHUNK), BF16),
            pltpu.VMEM((slots, features), BF16),
            pltpu.VMEM((2, tokens, slots), BF16),
            pltpu.VMEM((tokens, slots), BF16),
            pltpu.VMEM((tokens, slots), F32),
            pltpu.VMEM((2, tokens, slots), F32),
        ],
        compiler_params=pltpu.CompilerParams(
            collective_id=1, has_side_effects=True, vmem_limit_bytes=VMEM_LIMIT
        ),
    )(second, cotangent, after, pick, pick_t, *adapters, *own)


def sum_kernel(sizes, first_tiles, packed, landing, s0, s1, s2, s3, send_sem, recv_sem, seq_sem, local_sem, got, result):
    fsdp_size, seq_size = sizes
    devices = fsdp_size * seq_size
    ring = Ring(fsdp_size)
    me = ring.me * seq_size + ring.x
    tiles = landing.shape[2]
    width = tiles * LANES
    barrier = pltpu.get_barrier_semaphore()

    def target(k):
        d = lax.rem(me + k, devices)
        return d, {"fsdp": d // seq_size, "seq": lax.rem(d, seq_size)}

    @pl.loop(1, devices)
    def _(k):
        pl.semaphore_signal(barrier, inc=1, device_id=target(k)[1], device_id_type=MESH)

    own = pltpu.make_async_copy(packed.at[me], got.at[me], local_sem.at[0])
    own.start()
    pl.semaphore_wait(barrier, devices - 1)

    def piece(k):
        d, device = target(k)
        return pltpu.make_async_remote_copy(
            src_ref=packed.at[d],
            dst_ref=got.at[me],
            send_sem=send_sem.at[k],
            recv_sem=recv_sem.at[k],
            device_id=device,
            device_id_type=MESH,
        )

    @pl.loop(1, devices)
    def _(k):
        piece(k).start()

    own.wait()

    @pl.loop(1, devices)
    def _(k):
        piece(k).wait_recv()

    everything = got[...].reshape(devices * got.shape[1], width + LANES)
    summed = dot_tn(everything[:, width:], everything[:, :width])
    for t in range(tiles):
        tile = summed[:, t * LANES : (t + 1) * LANES]
        result[t] = jnp.where(me * tiles + t < first_tiles, tile.T, tile).astype(BF16)
    place = landing.at[ring.me, ring.x]
    store = pltpu.make_async_copy(result, place, local_sem.at[1])
    store.start()
    store.wait()

    def across(k):
        x = lax.rem(ring.x + k, seq_size)
        return pltpu.make_async_remote_copy(
            src_ref=place,
            dst_ref=place,
            send_sem=seq_sem.at[0, k],
            recv_sem=seq_sem.at[1, k],
            device_id={"seq": x},
            device_id_type=MESH,
        )

    for k in range(1, seq_size):
        across(k).start()
    for k in range(1, seq_size):
        across(k).wait_recv()

    def spot(third, owner):
        size = 32 if isinstance(third, int) and third == 2 else 48
        return landing.at[owner, :, :, pl.ds(third * 48, size), :]

    unit = Unit(ring, 0, spot, (s0, s1, s2, s3))
    in_order([unit])
    unit.collect()
    unit.drain()
    for k in range(1, seq_size):
        across(k).wait_send()

    @pl.loop(1, devices)
    def _(k):
        piece(k).wait_send()


def sum_gradients(sizes, first_tiles, packed):
    devices, slots, width = packed.shape
    tiles = width // LANES - 1
    fsdp_size, seq_size = sizes
    return pl.pallas_call(
        functools.partial(sum_kernel, sizes, first_tiles),
        out_shape=jax.ShapeDtypeStruct((fsdp_size, seq_size, tiles, LANES, LANES), BF16),
        in_specs=[ANYWHERE],
        out_specs=ANYWHERE,
        scratch_shapes=unit_sems(1, fsdp_size // 2)
        + [
            pltpu.SemaphoreType.DMA((devices,)),
            pltpu.SemaphoreType.DMA((devices,)),
            pltpu.SemaphoreType.DMA((2, seq_size)),
            pltpu.SemaphoreType.DMA((2,)),
            pltpu.VMEM(packed.shape, BF16),
            pltpu.VMEM((tiles, LANES, LANES), BF16),
        ],
        compiler_params=pltpu.CompilerParams(
            collective_id=2, has_side_effects=True, vmem_limit_bytes=VMEM_LIMIT
        ),
    )(packed)


def rms_parts(values):
    inverse = lax.rsqrt(jnp.mean(values * values, axis=-1, keepdims=True) + EPSILON)
    return (inverse, values * inverse)


def rms_back(grad_normed, gain_vector, inverse, unit_rows):
    scaled = grad_normed * gain_vector
    return inverse * (scaled - unit_rows * jnp.mean(scaled * unit_rows, axis=-1, keepdims=True))


def per_device(
    block_input,
    output_grad,
    adapter_ids,
    in_weight,
    out_weight,
    gate_weight,
    up_weight,
    down_weight,
    conv_weight,
    first_gain,
    second_gain,
    infirst_adapter,
    insecond_adapter,
    outfirst_adapter,
    outsecond_adapter,
    gatefirst_adapter,
    gatesecond_adapter,
    upfirst_adapter,
    upsecond_adapter,
    downfirst_adapter,
    downsecond_adapter,
):
    batches, seq_count, local_len, features = block_input.shape
    sequences = batches * seq_count
    tokens = sequences * local_len
    fsdp_size, seq_size = lax.axis_size("fsdp"), lax.axis_size("seq")
    slots = sequences * R
    hidden_size = gate_weight.shape[1]
    kernel = conv_weight.astype(F32)
    gain_first = first_gain.astype(F32)
    gain_second = second_gain.astype(F32)
    wanted = jnp.repeat(adapter_ids.reshape(sequences) * R, R) + jnp.tile(jnp.arange(R), sequences)
    pick = (lax.broadcasted_iota(jnp.int32, (LANES, slots), 0) == wanted[None, :]).astype(BF16)
    pick_t = (lax.broadcasted_iota(jnp.int32, (slots, LANES), 1) == wanted[:, None]).astype(BF16)
    mask = slot_mask(tokens, slots, local_len)
    in_first, out_first = (dot_nn(m, pick).astype(BF16) for m in (infirst_adapter, outfirst_adapter))
    in_second, out_second = (dot_nn(pick_t, m).astype(BF16) for m in (insecond_adapter, outsecond_adapter))

    weight_in, weight_out = gather_mixer(fsdp_size, in_weight, out_weight)
    inputs = block_input.reshape(tokens, features).astype(F32)
    cotangent = output_grad.reshape(tokens, features)
    inverse_first, unit_first = rms_parts(inputs)
    normed = (unit_first * gain_first).astype(BF16)
    low_in = (dot_nn(normed, in_first) * mask * ADAPTER_SCALE).astype(BF16)
    mixed_in = dot_nn(normed, weight_in) + dot_nn(low_in, in_second)
    first_part = mixed_in[:, :features]
    middle_part = mixed_in[:, features : 2 * features]
    last_part = mixed_in[:, 2 * features :]
    gated_values = (first_part * last_part).reshape(sequences, local_len, features)
    rim_rows = from_behind(gated_values[:, local_len - 2 :, :], "seq", 1)
    extended = jnp.concatenate([rim_rows, gated_values], axis=1)
    conv_out = (
        kernel[0] * extended[:, :local_len]
        + kernel[1] * extended[:, 1 : local_len + 1]
        + kernel[2] * extended[:, 2:]
    ).reshape(tokens, features)
    mixer_out = (middle_part * conv_out).astype(BF16)
    low_out = (dot_nn(mixer_out, out_first) * mask * ADAPTER_SCALE).astype(BF16)
    after_mixer = inputs + (dot_nn(mixer_out, weight_out) + dot_nn(low_out, out_second))
    inverse_second, unit_second = rms_parts(after_mixer)
    second = (unit_second * gain_second).astype(BF16)

    block_output, grad_second, grads_late, _, _ = feed_forward(
        fsdp_size,
        local_len,
        second,
        cotangent,
        after_mixer,
        pick,
        pick_t,
        (
            gatefirst_adapter,
            gatesecond_adapter,
            upfirst_adapter,
            upsecond_adapter,
            downfirst_adapter,
            downsecond_adapter,
        ),
        (gate_weight, up_weight, down_weight),
    )

    grad_after = cotangent.astype(F32) + rms_back(grad_second, gain_second, inverse_second, unit_second)
    grad_branch = grad_after.astype(BF16)
    grad_outsecond = dot_tn(low_out, grad_branch)
    grad_low_out = (ADAPTER_SCALE * dot_nt(grad_branch, out_second) * mask).astype(BF16)
    grad_outfirst = dot_tn(grad_low_out, mixer_out)
    grad_mixer = dot_nt(grad_branch, weight_out) + dot_nt(grad_low_out, out_first)
    grad_conv = (grad_mixer * middle_part).reshape(sequences, local_len, features)
    rim_back = from_behind(grad_conv[:, :2, :], "seq", -1)
    beyond = jnp.concatenate([grad_conv, rim_back], axis=1)
    grad_gated = (
        kernel[2] * beyond[:, :local_len]
        + kernel[1] * beyond[:, 1 : local_len + 1]
        + kernel[0] * beyond[:, 2:]
    ).reshape(tokens, features)
    grad_mixed = jnp.concatenate(
        [grad_gated * last_part, grad_mixer * conv_out, grad_gated * first_part], axis=1
    ).astype(BF16)
    grad_insecond = dot_tn(low_in, grad_mixed)
    grad_low_in = (ADAPTER_SCALE * dot_nt(grad_mixed, in_second) * mask).astype(BF16)
    grad_infirst = dot_tn(grad_low_in, normed)

    grads = [
        grad_infirst.astype(BF16),
        grad_outfirst.astype(BF16),
        grads_late[:, : 2 * features + hidden_size],
        grad_insecond.astype(BF16),
        grad_outsecond.astype(BF16),
        grads_late[:, 2 * features + hidden_size :],
    ]
    total_width = sum(member.shape[1] for member in grads)
    devices = fsdp_size * seq_size
    tiles = -(-total_width // (LANES * devices))
    grads.append(jnp.zeros((slots, tiles * LANES * devices - total_width), BF16))
    packed = jnp.concatenate(grads, axis=1).reshape(slots, devices, tiles * LANES).transpose(1, 0, 2)
    packed = jnp.concatenate([packed, jnp.broadcast_to(pick_t, (devices, slots, LANES))], axis=2)
    first_tiles = (4 * features + hidden_size) // LANES
    summed = sum_gradients((fsdp_size, seq_size), first_tiles, packed).reshape(devices * tiles, LANES, LANES)

    grad_normed = dot_nt(grad_mixed, weight_in) + dot_nt(grad_low_in, in_first)
    grad_input = grad_after + rms_back(grad_normed, gain_first, inverse_first, unit_first)

    ones = summed[:first_tiles].reshape(first_tiles * LANES, LANES).astype(F32)
    twos = summed[first_tiles:].transpose(1, 0, 2).reshape(LANES, -1).astype(F32)
    at = [0, features, 2 * features, 3 * features, 4 * features, 4 * features + hidden_size]
    firsts = [ones[at[k] : at[k + 1]] for k in range(5)]
    at = [0]
    for width in (3 * features, features, hidden_size, hidden_size, features):
        at.append(at[-1] + width)
    seconds = [twos[:, at[k] : at[k + 1]] for k in range(5)]
    shape = block_input.shape
    return (
        block_output.reshape(shape),
        grad_input.astype(BF16).reshape(shape),
        firsts[0],
        seconds[0],
        firsts[1],
        seconds[1],
        firsts[2],
        seconds[2],
        firsts[3],
        seconds[3],
        firsts[4],
        seconds[4],
    )


def solution(mesh):
    return jax.shard_map(
        per_device,
        mesh=mesh,
        in_specs=(
            P(None, "fsdp", "seq", None),
            P(None, "fsdp", "seq", None),
            P(None, "fsdp"),
            P("fsdp", None),
            P("fsdp", None),
            P("fsdp", None),
            P("fsdp", None),
            P("fsdp", None),
            P(),
            P(),
            P(),
            P(),
            P(),
            P(),
            P(),
            P(),
            P(),
            P(),
            P(),
            P(),
            P(),
        ),
        out_specs=(
            P(None, "fsdp", "seq", None),
            P(None, "fsdp", "seq", None),
            P(),
            P(),
            P(),
            P(),
            P(),
            P(),
            P(),
            P(),
            P(),
            P(),
        ),
        check_vma=False,
    )
```

time: 823 us -> 468 us (0.57)
  waiting for transfers between devices: 486 us -> 4.34 us
  Pallas kernels: 0 us -> 327 us
  matrix products: 252 us -> 46 us
  between operations: 16.5 us -> 1.48 us
  other arithmetic: 23.6 us -> 38.2 us
  local copies, waits for them, and re-layouts: 28.8 us -> 40 us
    pallas_call x0 -> x3, Pallas kernels: none -> 327 us  [the longest x1 204 us: feed_forward(): pl.pallas_call(functools.partial(feed_forward_kernel, fsdp_size, per_sequ...]
    all_gather x5 -> x0, waiting for transfers between devices: 280 us -> none  [the longest x1 72.3 us: per_device(): lax.all_gather(up_weight, 'fsdp', axis=0, tiled=True)]
    dot_general x80 -> x20, matrix products: 252 us -> 46 us  [the longest x6 26.3 us: dot_nt(): lax.dot_general(left, right, (((1,), (1,)), ((), ())), preferred_element_...]
    psum x1 -> x0, waiting for transfers between devices: 199 us -> none  [per_device(): lax.psum((totals[0], totals[1], totals[2], totals[3], totals[4], totals[5...]
    slice x1 -> x6, local copies, waits for them, and re-layouts: 0.58 us -> 11.4 us  [the longest x1 4.64 us: per_device(): summed[first_tiles:].transpose(1, 0, 2).reshape(LANES, -1).astype(F32)]
    convert_element_type x4 -> x9, other arithmetic: 4.12 us -> 14.1 us  [the longest x1 3.94 us: per_device(): grad_input.astype(BF16).reshape(shape)]
    unnamed x312 -> x76, local copies, waits for them, and re-layouts: 28.1 us -> 28.2 us
  transfers between devices with their start and end apart: 10 -> 2, of which waited for: 8 -> 1; matrix products, arithmetic and copies ran while one was open for 13% -> 0% of each run, Pallas kernels for 0% -> 0%
where the time goes in v2:
time: 468 us; the launch traced here: 461 us
  Pallas kernels  327 us (70%)
  matrix products  46 us (10%)
  local copies, waits for them, and re-layouts  40 us (9%)
  other arithmetic  38.2 us (8%)
    pallas_call x1, Pallas kernels, feed_forward(): pl.pallas_call(functools.partial(feed_forward_kernel, fsdp_size, per_sequ...  204 us
    pallas_call x1, Pallas kernels, sum_gradients(): pl.pallas_call(functools.partial(sum_kernel, sizes, first_tiles), out_sha...  80 us
    pallas_call x1, Pallas kernels, gather_mixer(): pl.pallas_call(functools.partial(mixer_gather_kernel, fsdp_size), out_sha...  43 us
    unnamed x76, local copies, waits for them, and re-layouts  28.2 us
    dot_general x6, matrix products, dot_nt(): lax.dot_general(left, right, (((1,), (1,)), ((), ())), preferred_element_...  26.3 us
    dot_general x10, matrix products, dot_nn(): return jnp.dot(left, right, preferred_element_type=F32)  17.1 us
  transfers between devices with their start and end apart: 2, of which 1 were waited for; matrix products, arithmetic and copies ran while one was open for 0% of the time, Pallas kernels for 0%

profile of v2, /device:TPU:0, one launch (start us, length us, event | category | flops | bytes accessed | tf_op | source)
XLA Modules:
  0.0 460.8 jit_solution(15489747126894645206)
XLA Ops:
  1.6 2.2 fusion.23
  6.6 43.0 %shard_map.292 = (bf16[1024,3072]{1,0:T(8,128)(2,1)}, bf16[1024,1024]{1,0:T(8,128)(2,1)}) custom-call(bf16[64,3072]{1,0:T(8,128)(2,1)} %in_own.1, bf16[64,1024]{1,0:T(8,128)(2,1)} %out_own.1), custom_call_target="tpu_custom_call" | custom-call | tf_op jit(solution)/shard_map/pallas_call | solution.py:259
  49.6 8.7 %fusion.53 = f32[1024,3072]{1,0:T(8,128)S(1)} fusion(bf16[1024,1024]{1,0:T(8,128)(2,1)S(1)} %fusion.17, bf16[1024,3072]{1,0:T(8,128)(2,1)} %get-tuple-element.17), kind=kOutput, calls=%fused_computation.110 | convolution fusion | flops 6442450944 | bytes 20971520 | tf_op jit(solution)/shard_map/dot_general | solution.py:29
  62.4 2.6 collective-permute-start
  73.6 2.6 multiply_reduce_fusion.1
  79.8 204.0 %shard_map.293 = (bf16[1024,1024]{1,0:T(8,128)(2,1)}, f32[1024,1024]{1,0:T(8,128)}, bf16[32,16896]{1,0:T(8,128)(2,1)}, bf16[2,1024,4608]{2,1,0:T(8,128)(2,1)}, bf16[4608,1024]{1,0:T(8,128)(2,1)}) custom-call(bf16[1024,1024]{1,0:T(8,128)(2,1)} %multiply_convert_fusion.refs_0_, bf16[1024,1024]{1,0:T(8,128)(2,1)} %bitcast.110, f32[1024,1024]{1,0:T(8,128)} %copy-done.3, ...), custom_call_target="tpu_custom_call" | custom-call | tf_op jit(solution)/shard_map/pallas_call | solution.py:486
  283.8 4.3 multiply_reduce_fusion
  289.7 2.8 multiply_add_fusion
  292.6 2.4 fusion.47
  298.5 2.3 fusion.13
  302.2 4.3 collective-permute-done.1
  306.5 3.1 fusion.3
  309.6 5.9 %fusion.10 = (bf16[1024,1024]{1,0:T(8,128)(2,1)}, bf16[1024,1024]{1,0:T(8,128)(2,1)}) fusion(f32[2,512,1024]{2,1,0:T(8,128)} %fusion.3, f32[1024,3072]{1,0:T(8,128)S(1)} %bitcast.100), kind=kLoop, calls=%fused_computation.20 | loop fusion | flops 4194304 | bytes 16777216 | tf_op jit(solution)/shard_map/convert.3
  315.4 5.0 %fusion.32 = bf16[1024,32]{0,1:T(8,128)(2,1)S(1)} fusion(bf16[32,3072]{1,0:T(8,128)(2,1)S(1)} %convolution_convert_fusion, s32[32]{0:T(128)S(1)} %get-tuple-element.67, s32[32]{0:T(128)S(1)} %get-tuple-element.68, pred[32]{0:T(512)(128)(4,1)S(1)} %compare_and_fusion, s32[1024]{0:T(1024)S(1)} %get-tuple-element.65, s32[1024]{0:T(1024)S(1)} %get-tuple-element.66, ...), kind=kOutput, calls=%fused_computation.64 | convolution fusion | flops 220397568 | bytes 6563104 | tf_op jit(solution)/shard_map/dot_general | solution.py:33
  326.1 80.0 %shard_map.294 = bf16[16,2,6,128,128]{4,3,2,1,0:T(8,128)(2,1)} custom-call(bf16[32,32,896]{2,1,0:T(8,128)(2,1)} %pad_maximum_fusion.3.packed), custom_call_target="tpu_custom_call" | custom-call | tf_op jit(solution)/shard_map/pallas_call | solution.py:612
  406.0 4.6 %slice.141 = bf16[124,128,128]{2,1,0:T(8,128)(2,1)} slice(bf16[192,128,128]{2,1,0:T(8,128)(2,1)} %bitcast.104), slice={[68:192], [0:128], [0:128]} | slice | bytes 8126464 | tf_op jit(solution)/shard_map/slice | solution.py:766
  410.7 6.4 %copy.45 = bf16[124,128,128]{1,2,0:T(8,128)(2,1)} copy(bf16[124,128,128]{2,1,0:T(8,128)(2,1)} %slice.141) | data formatting | bytes 8126464
  417.1 3.2 convert_element_type.127
  424.2 2.2 slice_convert_fusion
  429.3 2.7 fusion.55
  433.9 3.2 copy.43
  437.1 3.0 copy.40
  442.1 13.2 %fusion.18 = (f32[1024]{0:T(1024)S(1)}, f32[1024,1024]{1,0:T(8,128)}) fusion(bf16[2,1,512,1024]{3,2,1,0:T(8,128)(2,1)S(1)} %copy-done.15, f32[1024]{0:T(1024)S(1)} %bitcast.127, f32[1024]{0:T(1024)S(1)} %convert_element_type.98, f32[1024,1024]{1,0:T(8,128)} %fusion.55, bf16[1024,3072]{1,0:T(8,128)(2,1)} %get-tuple-element.17, ...), kind=kOutput, calls=%fused_computation.33 | convolution fusion | flops 6467615744 | bytes 23080960 | tf_op jit(solution)/shard_map/dot_general | solution.py:33
  455.3 3.9 fusion.22
  (121 shorter events, 43.7 us)
Async XLA Ops:
  0.6 5.0 %copy-start = (bf16[128,3072]{1,0:T(8,128)(2,1)S(1)}, bf16[128,3072]{1,0:T(8,128)(2,1)}, u32[]{:S(2)}) copy-start(bf16[128,3072]{1,0:T(8,128)(2,1)} %param.33) | copy-start | bytes 2359300
  6.5 51.8 %copy-start.11 = (bf16[1024,1024]{1,0:T(8,128)(2,1)}, bf16[1024,1024]{1,0:T(8,128)(2,1)S(1)}, u32[]{:S(2)}) copy-start(bf16[1024,1024]{1,0:T(8,128)(2,1)S(1)} %fusion.17) | copy-start | bytes 6291460
  60.9 7.6 %copy-start.2 = (f32[1024,3072]{1,0:T(8,128)}, f32[1024,3072]{1,0:T(8,128)S(1)}, u32[]{:S(2)}) copy-start(f32[1024,3072]{1,0:T(8,128)S(1)} %convolution_add_fusion) | copy-start | bytes 37748740
  60.9 4.7 %copy-start.26 = (bf16[3,1024]{1,0:T(4,128)(2,1)S(1)}, bf16[3,1024]{1,0:T(4,128)(2,1)}, u32[]{:S(2)}) copy-start(bf16[3,1024]{1,0:T(4,128)(2,1)} %param.29) | copy-start | bytes 18436
  60.9 4.8 %copy-start.23 = (bf16[1024,128]{1,0:T(8,128)(2,1)S(1)}, bf16[1024,128]{1,0:T(8,128)(2,1)}, u32[]{:S(2)}) copy-start(bf16[1024,128]{1,0:T(8,128)(2,1)} %param.34) | copy-start | bytes 786436
  61.0 4.9 %copy-start.24 = (bf16[128,1024]{1,0:T(8,128)(2,1)S(1)}, bf16[128,1024]{1,0:T(8,128)(2,1)}, u32[]{:S(2)}) copy-start(bf16[128,1024]{1,0:T(8,128)(2,1)} %param.35) | copy-start | bytes 786436
  61.0 5.9 %copy-start.27 = (bf16[1024]{0:T(1024)(128)(2,1)S(1)}, bf16[1024]{0:T(1024)(128)(2,1)}, u32[]{:S(2)}) copy-start(bf16[1024]{0:T(1024)(128)(2,1)} %param.31) | copy-start | bytes 6148
  62.4 4.5 collective-permute-start
  70.6 5.5 %copy-start.9 = (bf16[1024,1024]{1,0:T(8,128)(2,1)}, bf16[1024,1024]{1,0:T(8,128)(2,1)S(1)}, u32[]{:S(2)}) copy-start(bf16[1024,1024]{1,0:T(8,128)(2,1)S(1)} %fusion.12) | copy-start | bytes 6291460
  283.8 4.6 %copy-start.4 = (f32[1024,1024]{1,0:T(8,128)S(1)}, f32[1024,1024]{1,0:T(8,128)}, u32[]{:S(2)}) copy-start(f32[1024,1024]{1,0:T(8,128)} %copy-done.3) | copy-start | bytes 12582916
  283.8 5.9 %copy-start.16 = (f32[1024,1024]{1,0:T(8,128)S(1)}, f32[1024,1024]{1,0:T(8,128)}, u32[]{:S(2)}) copy-start(f32[1024,1024]{1,0:T(8,128)} %get-tuple-element.20) | copy-start | bytes 12582916
  289.7 6.0 %slice-start = ((s8[12582912]{0:T(1024)(128)(4,1)}), s8[4194304]{0:T(1024)(128)(4,1)S(1)}, s32[]{:S(2)}) async-start(s8[12582912]{0:T(1024)(128)(4,1)} %bitcast.99), calls=%async_computation | async-start | bytes 8388608
  289.7 6.2 %slice-start.1 = ((s8[12582912]{0:T(1024)(128)(4,1)}), s8[4194304]{0:T(1024)(128)(4,1)S(1)}, s32[]{:S(2)}) async-start(s8[12582912]{0:T(1024)(128)(4,1)} %bitcast.99), calls=%async_computation.1 | async-start | bytes 8388608
  292.5 31.3 %copy-start.5 = (f32[1024,1024]{1,0:T(8,128)}, f32[1024,1024]{1,0:T(8,128)S(1)}, u32[]{:S(2)}) copy-start(f32[1024,1024]{1,0:T(8,128)S(1)} %multiply_add_fusion) | copy-start | bytes 12582916
  292.5 4.7 %slice-start.2 = ((s8[12582912]{0:T(1024)(128)(4,1)}), s8[4194304]{0:T(1024)(128)(4,1)S(1)}, s32[]{:S(2)}) async-start(s8[12582912]{0:T(1024)(128)(4,1)} %bitcast.99), calls=%async_computation.2 | async-start | bytes 8388608
  300.9 5.6 %collective-permute-start.1 = (f32[2,2,1024]{2,1,0:T(2,128)S(1)}, f32[2,2,1024]{2,1,0:T(2,128)S(1)}, u32[]{:S(2)}, u32[]{:S(2)}) collective-permute-start(f32[2,2,1024]{2,1,0:T(2,128)S(1)} %slice.136), channel_id=1, source_target_pairs={{1,0},{3,2},{5,4},{7,6},{9,8},{11,10},{13,12},{15,14},{17,16},{19,... | collective-permute-start | bytes 49160 | tf_op jit(solution)/shard_map/ppermute | solution.py:25
  315.4 5.0 %copy-start.12 = (bf16[1024,1024]{1,0:T(8,128)(2,1)S(1)}, bf16[1024,1024]{1,0:T(8,128)(2,1)}, u32[]{:S(2)}) copy-start(bf16[1024,1024]{1,0:T(8,128)(2,1)} %copy-done.11) | copy-start | bytes 6291460
  315.4 5.5 %copy-start.10 = (bf16[1024,1024]{1,0:T(8,128)(2,1)S(1)}, bf16[1024,1024]{1,0:T(8,128)(2,1)}, u32[]{:S(2)}) copy-start(bf16[1024,1024]{1,0:T(8,128)(2,1)} %copy-done.9) | copy-start | bytes 6291460
  315.4 6.0 %copy-start.22 = (bf16[32,16896]{1,0:T(8,128)(2,1)S(1)}, bf16[32,16896]{1,0:T(8,128)(2,1)}, u32[]{:S(2)}) copy-start(bf16[32,16896]{1,0:T(8,128)(2,1)} %get-tuple-element.21) | copy-start | bytes 3244036
  315.4 6.0 %copy-start.21 = (bf16[1024,1024]{1,0:T(8,128)(2,1)S(1)}, bf16[1024,1024]{1,0:T(8,128)(2,1)}, u32[]{:S(2)}) copy-start(bf16[1024,1024]{1,0:T(8,128)(2,1)} %get-tuple-element.47) | copy-start | bytes 6291460
  433.9 6.2 %copy-start.19 = (f32[128,1024]{0,1:T(8,128)S(1)}, f32[128,1024]{0,1:T(8,128)}, u32[]{:S(2)}) copy-start(f32[128,1024]{0,1:T(8,128)} %get-tuple-element.49) | copy-start | bytes 1572868
  433.9 8.2 %copy-start.15 = (bf16[2,1,512,1024]{3,2,1,0:T(8,128)(2,1)S(1)}, bf16[2,1,512,1024]{3,2,1,0:T(8,128)(2,1)}, u32[]{:S(2)}) copy-start(bf16[2,1,512,1024]{3,2,1,0:T(8,128)(2,1)} %param.21) | copy-start | bytes 6291460
  442.1 13.2 %copy-start.6 = (f32[1024,1024]{1,0:T(8,128)S(1)}, f32[1024,1024]{1,0:T(8,128)}, u32[]{:S(2)}) copy-start(f32[1024,1024]{1,0:T(8,128)} %copy-done.5) | copy-start | bytes 12582916
  455.3 5.3 %copy-start.1 = (bf16[128,3072]{1,0:T(8,128)(2,1)S(1)}, bf16[128,3072]{1,0:T(8,128)(2,1)}, u32[]{:S(2)}) copy-start(bf16[128,3072]{1,0:T(8,128)(2,1)} %param.33) | copy-start | bytes 2359300
  (11 other events, 28.7 us)

commit v3 on v2

--- a/solution.py
+++ b/solution.py
@@ -454,20 +454,21 @@
 
         base = j * FF_CHUNK
         for offset, left, right in (
-            (2 * features, grad_low_down[...], hidden_s),
-            (2 * features + hidden_size, low_gu[0], gate_s),
-            (2 * features + 2 * hidden_size, low_gu[1], up_s),
+            (0, grad_low_down[...], hidden_s),
+            (hidden_size, low_gu[0], gate_s),
+            (2 * hidden_size, low_gu[1], up_s),
         ):
             columns = pl.ds(pl.multiple_of(offset + base, LANES), FF_CHUNK)
             grads[:, columns] = dot_tn(left, right[...]).astype(BF16)
 
     half_low_down = (ADAPTER_SCALE * low_down[...] * mask).astype(BF16)
     block_out[...] = (total[...] + dot_nn(half_low_down, second_down[...])).astype(BF16)
-    base = 2 * features + 3 * hidden_size
-    grads[:, base : base + features] = dot_tn(half_low_down, cotangent[...]).astype(BF16)
+    base = 3 * hidden_size
+    grads[:, base + 2 * features : base + 3 * features] = dot_tn(half_low_down, cotangent[...]).astype(BF16)
     for k in range(2):
         back_low = (ADAPTER_SCALE * grad_low_gu[k] * mask).astype(BF16)
-        grads[:, k * features : (k + 1) * features] = dot_tn(back_low, second[...]).astype(BF16)
+        columns = slice(base + k * features, base + (k + 1) * features)
+        grads[:, columns] = dot_tn(back_low, second[...]).astype(BF16)
         grad_second[...] += dot_nt(back_low, first_gu[k])
 
     down_unit.drain()
@@ -477,12 +478,11 @@
         chunk_unit(k).drain()
 
 
-def feed_forward(fsdp_size, per_sequence, second, cotangent, after, pick, pick_t, adapters, own):
+def feed_forward(fsdp_size, per_sequence, grads_width, second, cotangent, after, pick, pick_t, adapters, own):
     tokens, features = second.shape
     hidden_size = own[0].shape[1]
     slots = pick.shape[1]
     chunks = hidden_size // FF_CHUNK
-    grads_width = 3 * features + 3 * hidden_size
     return pl.pallas_call(
         functools.partial(feed_forward_kernel, fsdp_size, per_sequence),
         out_shape=(
@@ -521,122 +521,424 @@
     )(second, cotangent, after, pick, pick_t, *adapters, *own)
 
 
-def sum_kernel(sizes, first_tiles, packed, landing, s0, s1, s2, s3, send_sem, recv_sem, seq_sem, local_sem, got, result):
+class Shares:
+    def __init__(self, devices, features, hidden_size):
+        self.early_all = (3 * hidden_size + 3 * features) // LANES
+        self.early = max(1, self.early_all // devices)
+        self.early_used = min(self.early_all, self.early * devices)
+        self.rest = self.early_all - self.early_used
+        self.late_used = self.rest + 6 * features // LANES
+        self.late = -(-self.late_used // devices)
+        self.wide, self.narrow = hidden_size // LANES, features // LANES
+        self.early_width = max(self.early_all, self.early * devices) * LANES
+        self.late_width = self.late * devices * LANES
+
+    def early_is_first(self, t):
+        lowest = 3 * self.wide
+        return (t < self.wide) | ((t >= lowest) & (t < lowest + 2 * self.narrow))
+
+    def late_is_first(self, t):
+        return (t >= self.rest) & (t < self.rest + 2 * self.narrow)
+
+
+class Sum:
+    def __init__(self, ring, seq_size, number, source, landing, tiles, is_first, refs, unit_sems_refs):
+        self.ring, self.seq_size, self.source, self.landing = ring, seq_size, source, landing
+        self.tiles, self.is_first = tiles, is_first
+        self.send_sem, self.recv_sem, self.seq_sem, self.local_sem, self.got, self.result = refs
+        self.devices = self.got.shape[0]
+        self.me = ring.me * seq_size + ring.x
+        self.place = landing.at[ring.me, ring.x]
+        self.unit = Unit(ring, number, self.spot, unit_sems_refs)
+
+    def spot(self, third, owner):
+        size = 32 if isinstance(third, int) and third == 2 else 48
+        return self.landing.at[owner, :, :, pl.ds(third * 48, size), :]
+
+    def columns(self, d):
+        width = self.tiles * LANES
+        return self.source.at[:, pl.ds(pl.multiple_of(d * width, LANES), width)]
+
+    def target(self, k):
+        d = lax.rem(self.me + k, self.devices)
+        return d, {"fsdp": d // self.seq_size, "seq": lax.rem(d, self.seq_size)}
+
+    def piece(self, k):
+        d, device = self.target(k)
+        return pltpu.make_async_remote_copy(
+            src_ref=self.columns(d),
+            dst_ref=self.got.at[self.me],
+            send_sem=self.send_sem.at[k],
+            recv_sem=self.recv_sem.at[k],
+            device_id=device,
+            device_id_type=MESH,
+        )
+
+    def own(self):
+        return pltpu.make_async_copy(self.columns(self.me), self.got.at[self.me], self.local_sem.at[0])
+
+    def start(self):
+        self.own().start()
+
+        @pl.loop(1, self.devices)
+        def _(k):
+            self.piece(k).start()
+
+    def add(self, chosen):
+        self.own().wait()
+
+        @pl.loop(1, self.devices)
+        def _(k):
+            self.piece(k).wait_recv()
+
+        everything = self.got[...].reshape(self.devices * self.got.shape[1], self.tiles * LANES)
+        summed = dot_tn(chosen, everything)
+        for t in range(self.tiles):
+            tile = summed[:, t * LANES : (t + 1) * LANES]
+            self.result[t] = jnp.where(self.is_first(self.me * self.tiles + t), tile.T, tile).astype(BF16)
+        store = pltpu.make_async_copy(self.result, self.place, self.local_sem.at[1])
+        store.start()
+        store.wait()
+        for k in range(1, self.seq_size):
+            self.across(k).start()
+
+    def across(self, k):
+        return pltpu.make_async_remote_copy(
+            src_ref=self.place,
+            dst_ref=self.place,
+            send_sem=self.seq_sem.at[0, k],
+            recv_sem=self.seq_sem.at[1, k],
+            device_id={"seq": lax.rem(self.ring.x + k, self.seq_size)},
+            device_id_type=MESH,
+        )
+
+    def crossed(self):
+        for k in range(1, self.seq_size):
+            self.across(k).wait_recv()
+
+    def drain(self):
+        self.unit.drain()
+        for k in range(1, self.seq_size):
+            self.across(k).wait_send()
+
+        @pl.loop(1, self.devices)
+        def _(k):
+            self.piece(k).wait_send()
+
+
+def mixer_back_kernel(sizes, per_sequence, shares, *refs):
+    (
+        grad_second, after, cotangent, block_in, mixed, conv, mixer_out, normed, low_in, low_out,
+        in_first, in_second, out_first, out_second, pick_t, taps, gain_first, gain_second, weight_in, weight_out,
+        grads_early,
+    ) = refs[:21]
+    grad_input, landing_early, landing_late = refs[21:24]
+    units_refs = refs[24:28]
+    early_refs, late_refs = refs[28:34], refs[34:40]
+    pick_send, pick_recv, rim_sem, load_sem = refs[40:44]
+    (
+        picks, rim_out, rim_in, grad_after, after_s, mixed_s, conv_s, in_w, out_w, branch,
+        grad_mixer, grad_mixed, low_out_back, low_in_back, late,
+    ) = refs[44:]
     fsdp_size, seq_size = sizes
     devices = fsdp_size * seq_size
     ring = Ring(fsdp_size)
-    me = ring.me * seq_size + ring.x
-    tiles = landing.shape[2]
-    width = tiles * LANES
+    tokens, features = after_s.shape
+    slots = low_in.shape[1]
+    sequences = tokens // per_sequence
+    block = min(ROW_BLOCK, per_sequence)
+    early = Sum(
+        ring, seq_size, 0, grads_early, landing_early, shares.early, shares.early_is_first, early_refs, units_refs
+    )
+    later = Sum(ring, seq_size, 1, late, landing_late, shares.late, shares.late_is_first, late_refs, units_refs)
+    loads = [
+        pltpu.make_async_copy(a, b, load_sem.at[k])
+        for k, (a, b) in enumerate(
+            (
+                (after, after_s),
+                (grad_second, grad_after),
+                (weight_out, out_w),
+                (mixed, mixed_s),
+                (conv, conv_s),
+                (weight_in, in_w),
+                (
+                    grads_early.at[:, pl.ds(shares.early_used * LANES, max(shares.rest, 1) * LANES)],
+                    late.at[:, pl.ds(0, max(shares.rest, 1) * LANES)],
+                ),
+            )
+        )
+    ]
+    for copy in loads[:6]:
+        copy.start()
+
     barrier = pltpu.get_barrier_semaphore()
-
-    def target(k):
-        d = lax.rem(me + k, devices)
-        return d, {"fsdp": d // seq_size, "seq": lax.rem(d, seq_size)}
 
     @pl.loop(1, devices)
     def _(k):
-        pl.semaphore_signal(barrier, inc=1, device_id=target(k)[1], device_id_type=MESH)
-
-    own = pltpu.make_async_copy(packed.at[me], got.at[me], local_sem.at[0])
-    own.start()
+        pl.semaphore_signal(barrier, inc=1, device_id=early.target(k)[1], device_id_type=MESH)
+
+    late[:, shares.late_used * LANES :] = jnp.zeros((slots, shares.late_width - shares.late_used * LANES), BF16)
+    if shares.rest:
+        loads[6].start()
     pl.semaphore_wait(barrier, devices - 1)
 
-    def piece(k):
-        d, device = target(k)
+    def pick_piece(k):
         return pltpu.make_async_remote_copy(
-            src_ref=packed.at[d],
-            dst_ref=got.at[me],
-            send_sem=send_sem.at[k],
-            recv_sem=recv_sem.at[k],
-            device_id=device,
+            src_ref=pick_t,
+            dst_ref=picks.at[early.me],
+            send_sem=pick_send.at[k],
+            recv_sem=pick_recv.at[k],
+            device_id=early.target(k)[1],
             device_id_type=MESH,
         )
 
+    picks[early.me] = pick_t[...]
+
     @pl.loop(1, devices)
     def _(k):
-        piece(k).start()
-
-    own.wait()
+        pick_piece(k).start()
+
+    early.start()
+    for copy in loads[:3]:
+        copy.wait()
+    mask = slot_mask(block, slots, per_sequence)
+
+    def rows_of(r):
+        return pl.ds(pl.multiple_of(r * block, block), block)
+
+    def masked(r, values):
+        row = r * block + lax.broadcasted_iota(jnp.int32, (block, slots), 0)
+        column = lax.broadcasted_iota(jnp.int32, (block, slots), 1)
+        return jnp.where(row // per_sequence == column // R, ADAPTER_SCALE * values, 0.0).astype(BF16)
+
+    @pl.loop(0, tokens // block)
+    def _(r):
+        at = rows_of(r)
+        rows = after_s[at, :]
+        inverse = lax.rsqrt(jnp.mean(rows * rows, axis=-1, keepdims=True) + EPSILON)
+        unit_rows = rows * inverse
+        scaled = grad_after[at, :] * gain_second[...]
+        gradient = cotangent[at, :].astype(F32) + inverse * (
+            scaled - unit_rows * jnp.mean(scaled * unit_rows, axis=-1, keepdims=True)
+        )
+        grad_after[at, :] = gradient
+        rounded = gradient.astype(BF16)
+        branch[at, :] = rounded
+        back_low = masked(r, dot_nt(rounded, out_second[...]))
+        low_out_back[at, :] = back_low
+        grad_mixer[at, :] = dot_nt(rounded, out_w[...]) + dot_nt(back_low, out_first[...])
+
+    for copy in loads[3:5]:
+        copy.wait()
+    middle = slice(features, 2 * features)
+    for k in range(sequences):
+        at = slice(k * per_sequence, k * per_sequence + 8)
+        rim_out[k] = grad_mixer[at, :] * mixed_s[at, middle]
+    rim = pltpu.make_async_remote_copy(
+        src_ref=rim_out,
+        dst_ref=rim_in,
+        send_sem=rim_sem.at[0],
+        recv_sem=rim_sem.at[1],
+        device_id={"seq": lax.rem(ring.x + seq_size - 1, seq_size)},
+        device_id_type=MESH,
+    )
+    rim.start()
+    base = shares.rest * LANES
+    late[:, base + features : base + 2 * features] = dot_tn(low_out_back[...], mixer_out[...]).astype(BF16)
+    base += 2 * features
+    late[:, base + 3 * features : base + 4 * features] = dot_tn(low_out[...], branch[...]).astype(BF16)
+    rim.wait_recv()
+    inner = (ring.x < seq_size - 1).astype(F32)
+
+    @pl.loop(0, tokens // block)
+    def _(r):
+        at = rows_of(r)
+        back = grad_mixer[at, :]
+        through = back * mixed_s[at, middle]
+        after_at = pl.ds(pl.multiple_of(jnp.minimum((r + 1) * block, tokens - 8), 8), 8)
+        beyond = grad_mixer[after_at, :] * mixed_s[after_at, middle]
+        last = lax.rem((r + 1) * block, per_sequence) == 0
+        beyond = jnp.where(last, rim_in[(r * block) // per_sequence] * inner, beyond)
+        extended = jnp.concatenate([through, beyond], axis=0)
+        gated = (
+            taps[2:3, :] * through + taps[1:2, :] * extended[1 : block + 1] + taps[0:1, :] * extended[2 : block + 2]
+        )
+        grad_mixed[at, :features] = (gated * mixed_s[at, 2 * features :]).astype(BF16)
+        grad_mixed[at, middle] = (back * conv_s[at, :]).astype(BF16)
+        grad_mixed[at, 2 * features :] = (gated * mixed_s[at, :features]).astype(BF16)
+        low_in_back[at, :] = masked(r, dot_nt(grad_mixed[at, :], in_second[...]))
+
+    late[:, base : base + 3 * features] = dot_tn(low_in[...], grad_mixed[...]).astype(BF16)
+    base -= 2 * features
+    late[:, base : base + features] = dot_tn(low_in_back[...], normed[...]).astype(BF16)
+    if shares.rest:
+        loads[6].wait()
+    later.start()
+    loads[5].wait()
 
     @pl.loop(1, devices)
     def _(k):
-        piece(k).wait_recv()
-
-    everything = got[...].reshape(devices * got.shape[1], width + LANES)
-    summed = dot_tn(everything[:, width:], everything[:, :width])
-    for t in range(tiles):
-        tile = summed[:, t * LANES : (t + 1) * LANES]
-        result[t] = jnp.where(me * tiles + t < first_tiles, tile.T, tile).astype(BF16)
-    place = landing.at[ring.me, ring.x]
-    store = pltpu.make_async_copy(result, place, local_sem.at[1])
-    store.start()
-    store.wait()
-
-    def across(k):
-        x = lax.rem(ring.x + k, seq_size)
-        return pltpu.make_async_remote_copy(
-            src_ref=place,
-            dst_ref=place,
-            send_sem=seq_sem.at[0, k],
-            recv_sem=seq_sem.at[1, k],
-            device_id={"seq": x},
-            device_id_type=MESH,
-        )
-
-    for k in range(1, seq_size):
-        across(k).start()
-    for k in range(1, seq_size):
-        across(k).wait_recv()
-
-    def spot(third, owner):
-        size = 32 if isinstance(third, int) and third == 2 else 48
-        return landing.at[owner, :, :, pl.ds(third * 48, size), :]
-
-    unit = Unit(ring, 0, spot, (s0, s1, s2, s3))
-    in_order([unit])
-    unit.collect()
-    unit.drain()
-    for k in range(1, seq_size):
-        across(k).wait_send()
+        pick_piece(k).wait_recv()
+
+    def finish(r):
+        at = rows_of(r)
+        rows = block_in[at, :].astype(F32)
+        inverse = lax.rsqrt(jnp.mean(rows * rows, axis=-1, keepdims=True) + EPSILON)
+        unit_rows = rows * inverse
+        gradient = dot_nt(grad_mixed[at, :], in_w[...]) + dot_nt(low_in_back[at, :], in_first[...])
+        scaled = gradient * gain_first[...]
+        grad_input[at, :] = (
+            grad_after[at, :]
+            + inverse * (scaled - unit_rows * jnp.mean(scaled * unit_rows, axis=-1, keepdims=True))
+        ).astype(BF16)
+
+    chosen = picks[...].reshape(devices * slots, LANES)
+    early.add(chosen)
+    parts = tokens // block
+    half = parts // 2
+
+    @pl.loop(0, half)
+    def _(r):
+        finish(r)
+
+    early.crossed()
+    early.unit.own()
+    later.add(chosen)
+
+    @pl.loop(half, parts)
+    def _(r):
+        finish(r)
+
+    steps = early.unit.steps
+    early.unit.relay(1)
+    later.crossed()
+    later.unit.own()
+    for step in range(2, steps + 3):
+        if step <= steps:
+            early.unit.relay(step)
+        if step >= 3:
+            early.unit.relay_seq(step - 2)
+        if step <= steps + 1:
+            later.unit.relay(step - 1)
+    for step in range(1, steps + 1):
+        later.unit.relay_seq(step)
+    early.unit.collect()
+    later.unit.collect()
+    early.drain()
+    later.drain()
+    rim.wait_send()
 
     @pl.loop(1, devices)
     def _(k):
-        piece(k).wait_send()
-
-
-def sum_gradients(sizes, first_tiles, packed):
-    devices, slots, width = packed.shape
-    tiles = width // LANES - 1
+        pick_piece(k).wait_send()
+
+
+def mixer_back(sizes, per_sequence, shares, operands):
     fsdp_size, seq_size = sizes
-    return pl.pallas_call(
-        functools.partial(sum_kernel, sizes, first_tiles),
-        out_shape=jax.ShapeDtypeStruct((fsdp_size, seq_size, tiles, LANES, LANES), BF16),
-        in_specs=[ANYWHERE],
-        out_specs=ANYWHERE,
-        scratch_shapes=unit_sems(1, fsdp_size // 2)
-        + [
+    devices = fsdp_size * seq_size
+    tokens, features = operands[0].shape
+    slots = operands[8].shape[1]
+    sequences = tokens // per_sequence
+
+    def sum_refs(tiles):
+        return [
             pltpu.SemaphoreType.DMA((devices,)),
             pltpu.SemaphoreType.DMA((devices,)),
             pltpu.SemaphoreType.DMA((2, seq_size)),
             pltpu.SemaphoreType.DMA((2,)),
-            pltpu.VMEM(packed.shape, BF16),
+            pltpu.VMEM((devices, slots, tiles * LANES), BF16),
             pltpu.VMEM((tiles, LANES, LANES), BF16),
+        ]
+
+    in_specs = [IN_VMEM] * len(operands)
+    for k in (0, 1, 4, 5, 18, 19, 20):
+        in_specs[k] = ANYWHERE
+    return pl.pallas_call(
+        functools.partial(mixer_back_kernel, sizes, per_sequence, shares),
+        out_shape=(
+            jax.ShapeDtypeStruct((tokens, features), BF16),
+            jax.ShapeDtypeStruct((fsdp_size, seq_size, shares.early, LANES, LANES), BF16),
+            jax.ShapeDtypeStruct((fsdp_size, seq_size, shares.late, LANES, LANES), BF16),
+        ),
+        in_specs=in_specs,
+        out_specs=(IN_VMEM, ANYWHERE, ANYWHERE),
+        scratch_shapes=unit_sems(2, fsdp_size // 2)
+        + sum_refs(shares.early)
+        + sum_refs(shares.late)
+        + [
+            pltpu.SemaphoreType.DMA((devices,)),
+            pltpu.SemaphoreType.DMA((devices,)),
+            pltpu.SemaphoreType.DMA((2,)),
+            pltpu.SemaphoreType.DMA((7,)),
+            pltpu.VMEM((devices, slots, LANES), BF16),
+            pltpu.VMEM((sequences, 8, features), F32),
+            pltpu.VMEM((sequences, 8, features), F32),
+            pltpu.VMEM((tokens, features), F32),
+            pltpu.VMEM((tokens, features), F32),
+            pltpu.VMEM((tokens, 3 * features), F32),
+            pltpu.VMEM((tokens, features), F32),
+            pltpu.VMEM((features, 3 * features), BF16),
+            pltpu.VMEM((features, features), BF16),
+            pltpu.VMEM((tokens, features), BF16),
+            pltpu.VMEM((tokens, features), F32),
+            pltpu.VMEM((tokens, 3 * features), BF16),
+            pltpu.VMEM((tokens, slots), BF16),
+            pltpu.VMEM((tokens, slots), BF16),
+            pltpu.VMEM((slots, shares.late_width), BF16),
         ],
         compiler_params=pltpu.CompilerParams(
             collective_id=2, has_side_effects=True, vmem_limit_bytes=VMEM_LIMIT
         ),
-    )(packed)
+    )(*operands)
+
+
+def spread_kernel(layout, early, late, *outs):
+    for out, pieces in zip(outs, layout):
+        for is_late, start, count, first in pieces:
+            source = late if is_late else early
+            offset = pieces[0][2] if len(pieces) > 1 and (is_late, start) == pieces[1][:2] else 0
+
+            @pl.loop(0, count)
+            def _(k, source=source, start=start, offset=offset, out=out, first=first):
+                at = pl.ds(pl.multiple_of((offset + k) * LANES, LANES), LANES)
+                tile = source[start + k].astype(F32)
+                if first:
+                    out[at, :] = tile
+                else:
+                    out[:, at] = tile
+
+
+def spread(shares, early, late):
+    wide, narrow, rest = shares.wide, shares.narrow, shares.rest
+    low = 3 * wide
+    layout = (
+        ((True, rest, narrow, True),),
+        ((True, rest + 2 * narrow, 3 * narrow, False),),
+        ((True, rest + narrow, narrow, True),),
+        ((True, rest + 5 * narrow, narrow, False),),
+        ((False, low, narrow, True),),
+        ((False, wide, wide, False),),
+        ((False, low + narrow, narrow, True),),
+        ((False, 2 * wide, wide, False),),
+        ((False, 0, wide, True),),
+        ((False, low + 2 * narrow, narrow - rest, False), (True, 0, rest, False)),
+    )
+    shapes = []
+    for pieces in layout:
+        length = sum(piece[2] for piece in pieces) * LANES
+        shapes.append(jax.ShapeDtypeStruct((length, LANES) if pieces[0][3] else (LANES, length), F32))
+    return pl.pallas_call(
+        functools.partial(spread_kernel, layout),
+        out_shape=tuple(shapes),
+        in_specs=[IN_VMEM] * 2,
+        out_specs=(IN_VMEM,) * len(shapes),
+        compiler_params=pltpu.CompilerParams(vmem_limit_bytes=VMEM_LIMIT),
+    )(early.reshape(-1, LANES, LANES), late.reshape(-1, LANES, LANES))
 
 
 def rms_parts(values):
     inverse = lax.rsqrt(jnp.mean(values * values, axis=-1, keepdims=True) + EPSILON)
     return (inverse, values * inverse)
-
-
-def rms_back(grad_normed, gain_vector, inverse, unit_rows):
-    scaled = grad_normed * gain_vector
-    return inverse * (scaled - unit_rows * jnp.mean(scaled * unit_rows, axis=-1, keepdims=True))
 
 
 def per_device(
@@ -668,6 +970,7 @@
     fsdp_size, seq_size = lax.axis_size("fsdp"), lax.axis_size("seq")
     slots = sequences * R
     hidden_size = gate_weight.shape[1]
+    shares = Shares(fsdp_size * seq_size, features, hidden_size)
     kernel = conv_weight.astype(F32)
     gain_first = first_gain.astype(F32)
     gain_second = second_gain.astype(F32)
@@ -705,6 +1008,7 @@
     block_output, grad_second, grads_late, _, _ = feed_forward(
         fsdp_size,
         local_len,
+        shares.early_width,
         second,
         cotangent,
         after_mixer,
@@ -721,70 +1025,36 @@
         (gate_weight, up_weight, down_weight),
     )
 
-    grad_after = cotangent.astype(F32) + rms_back(grad_second, gain_second, inverse_second, unit_second)
-    grad_branch = grad_after.astype(BF16)
-    grad_outsecond = dot_tn(low_out, grad_branch)
-    grad_low_out = (ADAPTER_SCALE * dot_nt(grad_branch, out_second) * mask).astype(BF16)
-    grad_outfirst = dot_tn(grad_low_out, mixer_out)
-    grad_mixer = dot_nt(grad_branch, weight_out) + dot_nt(grad_low_out, out_first)
-    grad_conv = (grad_mixer * middle_part).reshape(sequences, local_len, features)
-    rim_back = from_behind(grad_conv[:, :2, :], "seq", -1)
-    beyond = jnp.concatenate([grad_conv, rim_back], axis=1)
-    grad_gated = (
-        kernel[2] * beyond[:, :local_len]
-        + kernel[1] * beyond[:, 1 : local_len + 1]
-        + kernel[0] * beyond[:, 2:]
-    ).reshape(tokens, features)
-    grad_mixed = jnp.concatenate(
-        [grad_gated * last_part, grad_mixer * conv_out, grad_gated * first_part], axis=1
-    ).astype(BF16)
-    grad_insecond = dot_tn(low_in, grad_mixed)
-    grad_low_in = (ADAPTER_SCALE * dot_nt(grad_mixed, in_second) * mask).astype(BF16)
-    grad_infirst = dot_tn(grad_low_in, normed)
-
-    grads = [
-        grad_infirst.astype(BF16),
-        grad_outfirst.astype(BF16),
-        grads_late[:, : 2 * features + hidden_size],
-        grad_insecond.astype(BF16),
-        grad_outsecond.astype(BF16),
-        grads_late[:, 2 * features + hidden_size :],
-    ]
-    total_width = sum(member.shape[1] for member in grads)
-    devices = fsdp_size * seq_size
-    tiles = -(-total_width // (LANES * devices))
-    grads.append(jnp.zeros((slots, tiles * LANES * devices - total_width), BF16))
-    packed = jnp.concatenate(grads, axis=1).reshape(slots, devices, tiles * LANES).transpose(1, 0, 2)
-    packed = jnp.concatenate([packed, jnp.broadcast_to(pick_t, (devices, slots, LANES))], axis=2)
-    first_tiles = (4 * features + hidden_size) // LANES
-    summed = sum_gradients((fsdp_size, seq_size), first_tiles, packed).reshape(devices * tiles, LANES, LANES)
-
-    grad_normed = dot_nt(grad_mixed, weight_in) + dot_nt(grad_low_in, in_first)
-    grad_input = grad_after + rms_back(grad_normed, gain_first, inverse_first, unit_first)
-
-    ones = summed[:first_tiles].reshape(first_tiles * LANES, LANES).astype(F32)
-    twos = summed[first_tiles:].transpose(1, 0, 2).reshape(LANES, -1).astype(F32)
-    at = [0, features, 2 * features, 3 * features, 4 * features, 4 * features + hidden_size]
-    firsts = [ones[at[k] : at[k + 1]] for k in range(5)]
-    at = [0]
-    for width in (3 * features, features, hidden_size, hidden_size, features):
-        at.append(at[-1] + width)
-    seconds = [twos[:, at[k] : at[k + 1]] for k in range(5)]
+    grad_input, early, late = mixer_back(
+        (fsdp_size, seq_size),
+        local_len,
+        shares,
+        (
+            grad_second,
+            after_mixer,
+            cotangent,
+            block_input.reshape(tokens, features),
+            mixed_in,
+            conv_out,
+            mixer_out,
+            normed,
+            low_in,
+            low_out,
+            in_first,
+            in_second,
+            out_first,
+            out_second,
+            pick_t,
+            kernel,
+            gain_first[None, :],
+            gain_second[None, :],
+            weight_in,
+            weight_out,
+            grads_late,
+        ),
+    )
     shape = block_input.shape
-    return (
-        block_output.reshape(shape),
-        grad_input.astype(BF16).reshape(shape),
-        firsts[0],
-        seconds[0],
-        firsts[1],
-        seconds[1],
-        firsts[2],
-        seconds[2],
-        firsts[3],
-        seconds[3],
-        firsts[4],
-        seconds[4],
-    )
+    return (block_output.reshape(shape), grad_input.reshape(shape)) + tuple(spread(shares, early, late))
 
 
 def solution(mesh):

time: 468 us -> 392 us (0.84)
  local copies, waits for them, and re-layouts: 40 us -> 8.33 us
  matrix products: 46 us -> 18.7 us
  other arithmetic: 38.2 us -> 13.4 us
  Pallas kernels: 327 us -> 340 us
    dot_general x10 -> x0, matrix products: 28.9 us -> none  [the longest x6 26.3 us: dot_nt(): lax.dot_general(left, right, (((1,), (1,)), ((), ())), preferred_element_...]
    unnamed x76 -> x47, local copies, waits for them, and re-layouts: 28.2 us -> 8.23 us
    pallas_call x1 -> x2, Pallas kernels: 80 us -> 92 us  [the longest x1 83.5 us: mixer_back(): pl.pallas_call(functools.partial(mixer_back_kernel, sizes, per_sequence,...]
    slice x7 -> x0, local copies, waits for them, and re-layouts: 11.4 us -> none  [the longest x1 4.64 us: per_device(): summed[first_tiles:].transpose(1, 0, 2).reshape(LANES, -1).astype(F32)]
    convert_element_type x3 -> x2, other arithmetic: 9.3 us -> 1.3 us  [the longest x1 0.69 us: per_device(): (lax.broadcasted_iota(jnp.int32, (LANES, slots), 0) == wanted[None, :]).a...]
    another operation x1 -> x0, other arithmetic: 5.87 us -> none
    add x2 -> x0, other arithmetic: 5.84 us -> none  [the longest x1 3.07 us: per_device(): kernel[2] * beyond[:, :local_len] + kernel[1] * beyond[:, 1:local_len + 1]]
  transfers between devices with their start and end apart: 2 -> 1, of which waited for: 1 -> 0; matrix products, arithmetic and copies ran while one was open for 0% -> 1% of each run, Pallas kernels for 0% -> 0%
where the time goes in v3:
time: 392 us; the launch traced here: 384 us
  Pallas kernels  340 us (87%)
  matrix products  18.7 us (5%)
  other arithmetic  13.4 us (3%)
  local copies, waits for them, and re-layouts  8.33 us (2%)
    pallas_call x1, Pallas kernels, feed_forward(): pl.pallas_call(functools.partial(feed_forward_kernel, fsdp_size, per_sequ...  205 us
    pallas_call x1, Pallas kernels, mixer_back(): pl.pallas_call(functools.partial(mixer_back_kernel, sizes, per_sequence,...  83.5 us
    pallas_call x1, Pallas kernels, gather_mixer(): pl.pallas_call(functools.partial(mixer_gather_kernel, fsdp_size), out_sha...  42.6 us
    dot_general x10, matrix products, dot_nn(): return jnp.dot(left, right, preferred_element_type=F32)  18.7 us
    pallas_call x1, Pallas kernels, spread(): pl.pallas_call(functools.partial(spread_kernel, layout), out_shape=tuple(...  8.54 us
    unnamed x47, local copies, waits for them, and re-layouts  8.23 us
  transfers between devices with their start and end apart: 1, of which 0 were waited for; matrix products, arithmetic and copies ran while one was open for 1% of the time, Pallas kernels for 0%

profile of v3, /device:TPU:0, one launch (start us, length us, event | category | flops | bytes accessed | tf_op | source)
XLA Modules:
  0.0 384.2 jit_solution(17846103599120105353)
XLA Ops:
  0.7 0.8 multiply_bitcast_fusion
  1.7 0.7 convert_element_type.55
  2.4 2.1 multiply_reduce_fusion.1
  4.5 1.2 convolution_convert_fusion.2
  6.0 1.9 fusion.5.refs_7_
  7.8 42.6 %shard_map.292 = (bf16[1024,3072]{1,0:T(8,128)(2,1)}, bf16[1024,1024]{1,0:T(8,128)(2,1)}) custom-call(bf16[64,3072]{1,0:T(8,128)(2,1)} %in_own.1, bf16[64,1024]{1,0:T(8,128)(2,1)} %out_own.1), custom_call_target="tpu_custom_call" | custom-call | tf_op jit(solution)/shard_map/pallas_call | solution.py:259
  50.4 9.5 %fusion.22 = f32[1024,3072]{1,0:T(8,128)S(1)} fusion(bf16[1024,1024]{1,0:T(8,128)(2,1)} %fusion.5.refs_7_, bf16[1024,3072]{1,0:T(8,128)(2,1)} %get-tuple-element.30.refs_18_), kind=kOutput, calls=%fused_computation.55 | convolution fusion | flops 6442450944 | bytes 20971520 | tf_op jit(solution)/shard_map/dot_general | solution.py:29
  60.0 1.1 fusion.11.refs_8_
  61.1 1.8 convolution_add_fusion.refs_4_
  63.0 1.4 slice_multiply_fusion
  64.4 2.6 collective-permute-start
  67.0 0.7 fusion.12.refs_3_
  69.5 1.6 fusion.3
  71.1 1.1 fusion.7.refs_6_
  72.3 1.0 copy-done.4
  73.2 1.1 fusion.10.refs_9_
  75.7 2.6 multiply_reduce_fusion
  78.4 1.9 copy-done.3
  80.3 1.7 multiply_convert_fusion.refs_0_
  82.0 205.1 %shard_map.293 = (bf16[1024,1024]{1,0:T(8,128)(2,1)}, f32[1024,1024]{1,0:T(8,128)}, bf16[32,16896]{1,0:T(8,128)(2,1)}, bf16[2,1024,4608]{2,1,0:T(8,128)(2,1)}, bf16[4608,1024]{1,0:T(8,128)(2,1)}) custom-call(bf16[1024,1024]{1,0:T(8,128)(2,1)} %multiply_convert_fusion.refs_0_, bf16[1024,1024]{1,0:T(8,128)(2,1)} %bitcast.47, f32[1024,1024]{1,0:T(8,128)} %copy-done.3, ...), custom_call_target="tpu_custom_call" | custom-call | tf_op jit(solution)/shard_map/pallas_call | solution.py:486
  287.2 83.5 %shard_map.294 = (bf16[1024,1024]{1,0:T(8,128)(2,1)}, bf16[16,2,4,128,128]{4,3,2,1,0:T(8,128)(2,1)}, bf16[16,2,2,128,128]{4,3,2,1,0:T(8,128)(2,1)}) custom-call(f32[1024,1024]{1,0:T(8,128)} %get-tuple-element.33.refs_0_, f32[1024,1024]{1,0:T(8,128)} %copy-done.3, bf16[1024,1024]{1,0:T(8,128)(2,1)} %bitcast.48, bf16[1024,1024]{1,0:T(8,128)(2,1)} %bitcast.43, ...), custom_call_target="tpu_custom_call" | custom-call | tf_op jit(solution)/shard_map/pallas_call | solution.py:856
  370.7 8.5 %shard_map.295 = (f32[1024,128]{1,0:T(8,128)}, f32[128,3072]{1,0:T(8,128)}, f32[1024,128]{1,0:T(8,128)}, f32[128,1024]{1,0:T(8,128)}, f32[1024,128]{1,0:T(8,128)...) custom-call(bf16[128,128,128]{2,1,0:T(8,128)(2,1)} %bitcast.49, ...), custom_call_target="tpu_custom_call" | custom-call | tf_op jit(solution)/shard_map/pallas_call | solution.py:930
  379.2 3.2 copy.50
  382.4 1.3 copy.51
  (61 shorter events, 3.7 us)
Async XLA Ops:
  0.6 5.0 %copy-start = (bf16[128,3072]{1,0:T(8,128)(2,1)S(1)}, bf16[128,3072]{1,0:T(8,128)(2,1)}, u32[]{:S(2)}) copy-start(bf16[128,3072]{1,0:T(8,128)(2,1)} %param.33) | copy-start | bytes 2359300
  0.7 5.3 %copy-start.5 = (bf16[2,1,512,1024]{3,2,1,0:T(8,128)(2,1)S(1)}, bf16[2,1,512,1024]{3,2,1,0:T(8,128)(2,1)}, u32[]{:S(2)}) copy-start(bf16[2,1,512,1024]{3,2,1,0:T(8,128)(2,1)} %param.21) | copy-start | bytes 6291460
  2.4 57.6 %copy-start.20 = (f32[1024]{0:T(1024)}, f32[1024]{0:T(1024)S(1)}, u32[]{:S(2)}) copy-start(f32[1024]{0:T(1024)S(1)} %convert_element_type.55) | copy-start | bytes 12292
  5.7 54.3 %copy-start.13 = (bf16[32,1024]{0,1:T(8,128)(2,1)}, bf16[32,1024]{0,1:T(8,128)(2,1)S(1)}, u32[]{:S(2)}) copy-start(bf16[32,1024]{0,1:T(8,128)(2,1)S(1)} %convolution_convert_fusion.2) | copy-start | bytes 196612
  6.0 55.1 %copy-start.10 = (bf16[32,3072]{1,0:T(8,128)(2,1)}, bf16[32,3072]{1,0:T(8,128)(2,1)S(1)}, u32[]{:S(2)}) copy-start(bf16[32,3072]{1,0:T(8,128)(2,1)S(1)} %convolution_convert_fusion.refs_11_) | copy-start | bytes 589828
  50.4 9.6 %copy-start.7 = (bf16[1024,1024]{1,0:T(8,128)(2,1)S(1)}, bf16[1024,1024]{1,0:T(8,128)(2,1)}, u32[]{:S(2)}) copy-start(bf16[1024,1024]{1,0:T(8,128)(2,1)} %fusion.5.refs_7_) | copy-start | bytes 6291460
  61.1 1.8 copy-start.11
  62.9 8.2 %copy-start.2 = (f32[1024,3072]{1,0:T(8,128)}, f32[1024,3072]{1,0:T(8,128)S(1)}, u32[]{:S(2)}) copy-start(f32[1024,3072]{1,0:T(8,128)S(1)} %convolution_add_fusion.refs_4_) | copy-start | bytes 37748740
  63.0 4.7 %copy-start.18 = (bf16[3,1024]{1,0:T(4,128)(2,1)S(1)}, bf16[3,1024]{1,0:T(4,128)(2,1)}, u32[]{:S(2)}) copy-start(bf16[3,1024]{1,0:T(4,128)(2,1)} %param.29) | copy-start | bytes 18436
  63.0 4.8 %copy-start.16 = (bf16[1024,128]{1,0:T(8,128)(2,1)S(1)}, bf16[1024,128]{1,0:T(8,128)(2,1)}, u32[]{:S(2)}) copy-start(bf16[1024,128]{1,0:T(8,128)(2,1)} %param.34) | copy-start | bytes 786436
  63.0 5.0 %copy-start.17 = (bf16[128,1024]{1,0:T(8,128)(2,1)S(1)}, bf16[128,1024]{1,0:T(8,128)(2,1)}, u32[]{:S(2)}) copy-start(bf16[128,1024]{1,0:T(8,128)(2,1)} %param.35) | copy-start | bytes 786436
  63.0 6.5 %copy-start.21 = (bf16[1024]{0:T(1024)(128)(2,1)S(1)}, bf16[1024]{0:T(1024)(128)(2,1)}, u32[]{:S(2)}) copy-start(bf16[1024]{0:T(1024)(128)(2,1)} %param.31) | copy-start | bytes 6148
  64.4 5.1 %collective-permute-start = (f32[2,2,1024]{2,1,0:T(2,128)S(1)}, f32[2,2,1024]{2,1,0:T(2,128)S(1)}, u32[]{:S(2)}, u32[]{:S(2)}) collective-permute-start(f32[2,2,1024]{2,1,0:T(2,128)S(1)} %slice.40), channel_id=1, source_target_pairs={{0,1},{2,3},{4,5},{6,7},{8,9},{10,11},{12,13},{14,15},{16,17},{18,... | collective-permute-start | bytes 49160 | tf_op jit(solution)/shard_map/ppermute | solution.py:25
  68.0 4.3 %copy-start.14 = (bf16[32,1024]{0,1:T(8,128)(2,1)}, bf16[32,1024]{0,1:T(8,128)(2,1)S(1)}, u32[]{:S(2)}) copy-start(bf16[32,1024]{0,1:T(8,128)(2,1)S(1)} %convolution_convert_fusion.1) | copy-start | bytes 196612
  68.2 6.2 %copy-start.15 = (bf16[32,1024]{1,0:T(8,128)(2,1)}, bf16[32,1024]{1,0:T(8,128)(2,1)S(1)}, u32[]{:S(2)}) copy-start(bf16[32,1024]{1,0:T(8,128)(2,1)S(1)} %convolution_convert_fusion.3.refs_13_) | copy-start | bytes 196612
  69.5 8.9 %copy-start.19 = (f32[1024]{0:T(1024)}, f32[1024]{0:T(1024)S(1)}, u32[]{:S(2)}) copy-start(f32[1024]{0:T(1024)S(1)} %convert_element_type.65) | copy-start | bytes 12292
  71.1 2.1 copy-start.4
  73.2 5.1 %copy-start.6 = (bf16[1024,1024]{1,0:T(8,128)(2,1)}, bf16[1024,1024]{1,0:T(8,128)(2,1)S(1)}, u32[]{:S(2)}) copy-start(bf16[1024,1024]{1,0:T(8,128)(2,1)S(1)} %fusion.7.refs_6_) | copy-start | bytes 6291460
  73.2 2.4 copy-start.9
  74.3 4.0 %copy-start.12 = (bf16[1024,32]{1,0:T(8,128)(2,1)}, bf16[1024,32]{1,0:T(8,128)(2,1)S(1)}, u32[]{:S(2)}) copy-start(bf16[1024,32]{1,0:T(8,128)(2,1)S(1)} %fusion.10.refs_9_) | copy-start | bytes 196612
  78.4 2.0 copy-start.3
  379.2 3.2 copy-start.8
  379.2 4.6 %copy-start.1 = (bf16[128,3072]{1,0:T(8,128)(2,1)S(1)}, bf16[128,3072]{1,0:T(8,128)(2,1)}, u32[]{:S(2)}) copy-start(bf16[128,3072]{1,0:T(8,128)(2,1)} %param.33) | copy-start | bytes 2359300

commit v4 on v3

--- a/solution.py
+++ b/solution.py
@@ -15,14 +15,10 @@
 BF16 = jnp.bfloat16
 F32 = jnp.float32
 VMEM_LIMIT = 62 * 1024 * 1024
-FF_CHUNK = 768
+FF_CHUNK = 512
 ROW_BLOCK = 256
-
-
-def from_behind(block, axis, distance):
-    devices = range(lax.axis_size(axis))
-    route = [(i - distance, i) for i in devices if i - distance in devices]
-    return lax.ppermute(block, axis, route)
+WIDE_BLOCK = 512
+VMEM_LIMIT_FRONT = 63 * 1024 * 1024
 
 
 def dot_nn(left, right):
@@ -77,11 +73,14 @@
             return self.device(lax.rem(self.place + self.count - step, self.count))
         return self.device(lax.rem(self.place + step, self.count))
 
-    def greet(self):
+    def greet(self, seq_size):
         barrier = pltpu.get_barrier_semaphore()
-        for device in (self.to_next, self.to_prev, self.to_core, self.to_seq):
+        devices = [self.to_next, self.to_prev, self.to_core, self.to_seq]
+        if seq_size > 2:
+            devices.append({"seq": lax.rem(self.x + seq_size - 1, seq_size)})
+        for device in devices:
             pl.semaphore_signal(barrier, inc=1, device_id=device, device_id_type=MESH)
-        pl.semaphore_wait(barrier, 4)
+        pl.semaphore_wait(barrier, len(devices))
 
 
 class Unit:
@@ -190,17 +189,6 @@
     ]
 
 
-def in_order(units, lag=2):
-    entries = []
-    for k, unit in enumerate(units):
-        entries.append((k, 0, unit.own))
-        for step in range(1, unit.steps + 1):
-            entries.append((k + step, 1, functools.partial(unit.relay, step)))
-            entries.append((k + step + lag, 2, functools.partial(unit.relay_seq, step)))
-    for entry in sorted(entries, key=lambda entry: entry[:2]):
-        entry[2]()
-
-
 def move_in(moves, sems):
     inward = [pltpu.make_async_copy(a, b, sems.at[0, k]) for k, (a, b, _) in enumerate(moves)]
     outward = [pltpu.make_async_copy(b, c, sems.at[1, k]) for k, (_, b, c) in enumerate(moves)]
@@ -212,8 +200,8 @@
     return outward
 
 
-def row_spot(landing, rows, third, owner, columns=None):
-    return landing.at[pl.ds(owner * rows + third * (rows // 3), rows // 3), :]
+def row_spot(landing, rows, start, size, third, owner):
+    return landing.at[pl.ds(owner * rows + start + third * size, size), :]
 
 
 def column_spot(landing, rows, width, last, third, owner):
@@ -227,137 +215,286 @@
     return landing.at[:, pl.ds(owner * rows, rows), pl.ds(start, size)]
 
 
-def mixer_gather_kernel(fsdp_size, in_own, out_own, in_all, out_all, s0, s1, s2, s3, local_sem, held_in, held_out):
-    ring = Ring(fsdp_size)
-    rows = in_own.shape[0]
-    mine = pl.ds(ring.me * rows, rows)
-    moved = move_in([(in_own, held_in, in_all.at[mine, :]), (out_own, held_out, out_all.at[mine, :])], local_sem)
-    ring.greet()
-    for copy in moved:
-        copy.wait()
-    part = in_all.shape[1] // 3
-    out_x = 3 * out_all.shape[1] // 8
-    sems = (s0, s1, s2, s3)
-    units = [
-        Unit(ring, 0, functools.partial(column_spot, in_all, rows, part, part), sems),
-        Unit(ring, 1, functools.partial(column_spot, out_all, rows, out_x, out_all.shape[1] - 2 * out_x), sems),
-    ]
-    in_order(units)
-    for unit in units:
-        unit.collect()
-    for unit in units:
-        unit.drain()
+def share_out(actions, ticks):
+    cuts = [len(actions) * k // ticks for k in range(ticks + 1)]
+    return [actions[cuts[k] : cuts[k + 1]] for k in range(ticks)]
+
+
+def run_tick(lists, tick):
+    for k, actions in enumerate(lists):
+
+        @pl.when(tick == k)
+        def _(actions=actions):
+            for action in actions:
+                action()
+
+
+def rms_unit(rows):
+    inverse = lax.rsqrt(jnp.mean(rows * rows, axis=-1, keepdims=True) + EPSILON)
+    return inverse, rows * inverse
+
+
+def rms_back(scaled, inverse, unit_rows):
+    return inverse * (scaled - unit_rows * jnp.mean(scaled * unit_rows, axis=-1, keepdims=True))
 
 
 ANYWHERE = pl.BlockSpec(memory_space=pl.ANY)
 IN_VMEM = pl.BlockSpec(memory_space=pltpu.VMEM)
 
 
-def gather_mixer(fsdp_size, in_weight, out_weight):
-    rows = fsdp_size * in_weight.shape[0]
-    own = (in_weight, out_weight)
-    return pl.pallas_call(
-        functools.partial(mixer_gather_kernel, fsdp_size),
-        out_shape=tuple(jax.ShapeDtypeStruct((rows, member.shape[1]), BF16) for member in own),
-        in_specs=[ANYWHERE] * 2,
-        out_specs=(ANYWHERE,) * 2,
-        scratch_shapes=unit_sems(2, fsdp_size // 2)
-        + [pltpu.SemaphoreType.DMA((2, 2))]
-        + [pltpu.VMEM(member.shape, BF16) for member in own],
-        compiler_params=pltpu.CompilerParams(collective_id=0, has_side_effects=True),
-    )(*own)
-
-
-def slot_mask(rows, slots, per_sequence, base=0):
-    row = lax.broadcasted_iota(jnp.int32, (rows, slots), 0)
-    column = lax.broadcasted_iota(jnp.int32, (rows, slots), 1)
-    return (row // per_sequence == column // R).astype(F32)
-
-
-def feed_forward_kernel(fsdp_size, per_sequence, *refs):
+def front_kernel(sizes, per_sequence, *refs):
     (
-        second, cotangent, after, pick, pick_t,
-        gate_first, gate_second, up_first, up_second, down_first, down_second,
-        gate_own, up_own, down_own,
-    ) = refs[:14]
-    block_out, grad_second, grads, gu_all, down_all = refs[14:19]
-    sems, local_sem, load_sem = refs[19:23], refs[23], refs[24]
+        block_in, cotangent, pick, pick_t, taps, gain_first, gain_second,
+        in_first, in_second, out_first, out_second, gate_first, up_first, down_second,
+        gate_second, up_second, down_first, in_own, out_own, gate_own, up_own, down_own,
+    ) = refs[:22]
     (
-        held_gate, held_up, held_down, total, grad_hidden, gate_w, up_w, down_w, hidden_s, gate_s, up_s,
-        first_gu, first_down, second_gu, second_down, low_gu, grad_low_down, low_down, grad_low_gu,
-    ) = refs[25:]
+        grad_second, grads, low_in, low_out, in_first_s, in_second_s, out_first_s, out_second_s,
+        block_out, after_out, mixed_out, conv_out, mixer_out, normed_out, in_all, out_all, gu_all, down_all,
+    ) = refs[22:40]
+    sems, local_sem, load_sem, stage_sem, rim_sem, out_sem = refs[40:44], refs[44], refs[45], refs[46], refs[47], refs[48]
+    held = refs[49:54]
+    (
+        total, wide, gate_w, up_w, down_w, normed, mixer, second, gate_up_first, first_down, second_gu, second_down,
+        low_gu, grad_low_down, low_down, grad_low_gu, partial, rim_out, rim_in,
+    ) = refs[54:]
+    fsdp_size, seq_size = sizes
     ring = Ring(fsdp_size)
     rows, down_rows = gate_own.shape[0], down_own.shape[0]
-    tokens, features = second.shape
+    tokens, features = cotangent.shape
     hidden_size = gate_own.shape[1]
     chunks = hidden_size // FF_CHUNK
+    sequences = tokens // per_sequence
+    block = min(ROW_BLOCK, per_sequence)
+    wide_block = min(WIDE_BLOCK, tokens)
+    blocks, wide_blocks = tokens // block, tokens // wide_block
     slots = pick.shape[1]
-    blocks = tokens // ROW_BLOCK
     mine = pl.ds(ring.me * rows, rows)
     moved = move_in(
         [
-            (down_own, held_down, down_all.at[pl.ds(ring.me * down_rows, down_rows), :]),
-            (gate_own, held_gate, gu_all.at[0, mine, :]),
-            (up_own, held_up, gu_all.at[1, mine, :]),
+            (in_own, held[0], in_all.at[mine, :]),
+            (out_own, held[1], out_all.at[mine, :]),
+            (down_own, held[4], down_all.at[pl.ds(ring.me * down_rows, down_rows), :]),
+            (gate_own, held[2], gu_all.at[0, mine, :]),
+            (up_own, held[3], gu_all.at[1, mine, :]),
         ],
         local_sem,
     )
-    started = pltpu.make_async_copy(after, total, load_sem.at[2, 0])
-    started.start()
-    ring.greet()
+    stages = []
+    for k in range(-(-hidden_size // features)):
+        width = min(features, hidden_size - k * features)
+        part, lanes = pl.ds(k * features, width), pl.ds(k * LANES, LANES)
+        stages += [
+            (gate_second.at[:, part], second.at[lanes, pl.ds(0, width)]),
+            (up_second.at[:, part], normed.at[lanes, pl.ds(0, width)]),
+            (down_first.at[part, :], mixer.at[pl.ds(0, width), lanes]),
+        ]
+    stages = [pltpu.make_async_copy(a, b, stage_sem.at[k]) for k, (a, b) in enumerate(stages)]
+    for copy in stages:
+        copy.start()
+    ring.greet(seq_size)
+
+    part = in_all.shape[1] // 3
+    out_x = 3 * features // 8
+    unit_list = [
+        Unit(ring, 0, functools.partial(column_spot, in_all, rows, part, part), sems),
+        Unit(ring, 1, functools.partial(column_spot, out_all, rows, out_x, features - 2 * out_x), sems),
+    ]
+    pieces = 2 if down_rows % 96 == 0 else 1
+    for k in range(pieces):
+        size = down_rows // pieces // 3
+        unit_list.append(Unit(ring, 2 + k, functools.partial(row_spot, down_all, down_rows, 3 * size * k, size), sems))
+    fixed = len(unit_list)
+    comm_chunks = 2 * chunks // 3
+    comm_size = hidden_size // comm_chunks // 3
+
+    def chunk_unit(k):
+        return Unit(ring, fixed + k, functools.partial(chunk_spot, gu_all, rows, comm_size, k), sems)
+
+    steps = unit_list[0].steps
+    stepped = steps == 4 and wide_blocks == 2
+    starts = {0: 0, 1: 1, 2: 2, 3: 4}
+    entries = []
+
+    def enter(start, unit, last=10**6):
+        plan = [(start, 0, unit.own)]
+        for step in range(1, steps + 1):
+            plan.append((start + step, 1, functools.partial(unit.relay, step)))
+            plan.append((start + step + 1, 2, functools.partial(unit.relay_seq, step)))
+        entries.extend((slot, kind, unit.number, action) for slot, kind, action in plan if slot <= last)
+
+    for k, unit in enumerate(unit_list):
+        enter(starts[k], unit)
+    chunk_start = 2 * fixed - 2
+    if stepped:
+        for k in range(comm_chunks):
+            if 2 * k <= 6:
+                enter(chunk_start + 2 * k, chunk_unit(k), chunk_start + 6)
+    else:
+        enter(chunk_start, chunk_unit(0))
+    entries.sort(key=lambda entry: entry[:3])
+
+    def until(numbers):
+        last = max(k for k, entry in enumerate(entries) if entry[2] in numbers)
+        taken = [entry[3] for entry in entries[: last + 1]]
+        del entries[: last + 1]
+        return taken
+
     for copy in moved:
         copy.wait()
-    down_unit = Unit(ring, 0, functools.partial(row_spot, down_all, down_rows), sems)
-
-    def chunk_unit(k):
-        return Unit(ring, 1 + k, functools.partial(chunk_spot, gu_all, rows, FF_CHUNK // 3, k), sems)
-
-    steps = down_unit.steps
-    down_unit.own()
-    chunk_unit(0).own()
-
-    for k, (first, second_map) in enumerate(((gate_first, gate_second), (up_first, up_second))):
-        first_gu[k] = dot_nn(first[...], pick[...]).astype(BF16)
-        for j in range(chunks):
-            part = dot_nn(pick_t[...], second_map[:, j * FF_CHUNK : (j + 1) * FF_CHUNK])
-            second_gu[k, j] = part.astype(BF16)
+    early = until((0,))
+    early[0]()
+    early[1]()
+
+    def rows_of(r, size=block):
+        return pl.ds(pl.multiple_of(r * size, size), size)
+
+    def masked(r, values, size=block):
+        row = r * size + lax.broadcasted_iota(jnp.int32, (size, slots), 0)
+        column = lax.broadcasted_iota(jnp.int32, (size, slots), 1)
+        return jnp.where(row // per_sequence == column // R, ADAPTER_SCALE * values, 0.0).astype(BF16)
+
+    for copy in stages:
+        copy.wait()
+    for k in range(-(-hidden_size // features)):
+        width = min(features, hidden_size - k * features)
+        at, lanes = slice(k * features, k * features + width), slice(k * LANES, (k + 1) * LANES)
+        second_gu[0, :, at] = dot_nn(pick_t[...], second[lanes, :width]).astype(BF16)
+        second_gu[1, :, at] = dot_nn(pick_t[...], normed[lanes, :width]).astype(BF16)
+        first_down[at, :] = dot_nn(mixer[:width, lanes], pick[...]).astype(BF16)
     second_down[...] = dot_nn(pick_t[...], down_second[...]).astype(BF16)
-    for j in range(chunks):
-        first_down[j] = dot_nn(down_first[j * FF_CHUNK : (j + 1) * FF_CHUNK, :], pick[...]).astype(BF16)
-    mask = slot_mask(tokens, slots, per_sequence)
-    for k in range(2):
-        low = (dot_nn(second[...], first_gu[k]) * mask).astype(BF16)
-        low_gu[k] = low * ADAPTER_SCALE
-    grad_low_down[...] = (ADAPTER_SCALE * dot_nt(cotangent[...], second_down[...]) * mask).astype(BF16)
-    grad_second[...] = jnp.zeros_like(grad_second)
+    in_second_s[...] = dot_nn(pick_t[...], in_second[...]).astype(BF16)
+    out_second_s[...] = dot_nn(pick_t[...], out_second[...]).astype(BF16)
+    in_first_s[...] = dot_nn(in_first[...], pick[...]).astype(BF16)
+    out_first_s[...] = dot_nn(out_first[...], pick[...]).astype(BF16)
+    gate_up_first[0] = dot_nn(gate_first[...], pick[...]).astype(BF16)
+    gate_up_first[1] = dot_nn(up_first[...], pick[...]).astype(BF16)
+
+    @pl.loop(0, blocks)
+    def _(r):
+        at = rows_of(r)
+        normed_rows = (rms_unit(block_in[at, :].astype(F32))[1] * gain_first[...]).astype(BF16)
+        normed[at, :] = normed_rows
+        low_in[at, :] = masked(r, dot_nn(normed_rows, in_first_s[...]))
+        grad_low_down[at, :] = masked(r, dot_nt(cotangent[at, :], second_down[...]))
+        grad_second[at, :] = jnp.zeros((block, features), F32)
+
     low_down[...] = jnp.zeros_like(low_down)
     grad_low_gu[...] = jnp.zeros_like(grad_low_gu)
-
-    for step in range(1, steps + 1):
-        down_unit.relay(step)
-    for step in range(1, steps + 1):
-        down_unit.relay_seq(step)
-    down_unit.collect()
+    for action in early[2:]:
+        action()
+    unit_list[0].collect()
+
+    half = FF_CHUNK
+    middle, last_part, conv_part = (slice(k * features, (k + 1) * features) for k in (1, 2, 3))
+    in_loads = []
+    for k in range(2):
+        for part_number, buffer in ((0, gate_w), (1, up_w)):
+            columns = pl.ds(part_number * features + k * half, half)
+            in_loads.append(pltpu.make_async_copy(in_all.at[:, columns], buffer.at[k], load_sem.at[k, part_number]))
+        place = in_all.at[pl.ds(k * half, half), pl.ds(2 * features, features)]
+        in_loads.append(pltpu.make_async_copy(place, down_w.at[k], load_sem.at[k, 2]))
+    for copy in in_loads:
+        copy.start()
+    for copy in in_loads:
+        copy.wait()
+    lists = share_out(until((1,)), blocks)
+
+    @pl.loop(0, blocks)
+    def _(r):
+        run_tick(lists, r)
+        at = rows_of(r)
+        values, low = normed[at, :], low_in[at, :]
+        for part_number, buffer in ((0, gate_w), (1, up_w)):
+            for k in range(2):
+                start = part_number * features + k * half
+                columns = slice(start, start + half)
+                wide[at, columns] = dot_nn(values, buffer[k]) + dot_nn(low, in_second_s[:, columns])
+        wide[at, last_part] = (
+            dot_nn(values[:, :half], down_w[0])
+            + dot_nn(values[:, half:], down_w[1])
+            + dot_nn(low, in_second_s[:, last_part])
+        )
+
+    unit_list[1].collect()
+    out_loads = [
+        pltpu.make_async_copy(out_all.at[:, pl.ds(k * half, half)], gate_w.at[k], load_sem.at[k, 0]) for k in range(2)
+    ]
+    for copy in out_loads:
+        copy.start()
+    for k in range(sequences):
+        at = slice((k + 1) * per_sequence - 8, (k + 1) * per_sequence)
+        rim_out[k] = wide[at, :features] * wide[at, last_part]
+    rim = pltpu.make_async_remote_copy(
+        src_ref=rim_out,
+        dst_ref=rim_in,
+        send_sem=rim_sem.at[0],
+        recv_sem=rim_sem.at[1],
+        device_id={"seq": lax.rem(ring.x + 1, seq_size)},
+        device_id_type=MESH,
+    )
+    rim.start()
+    mixed_store = pltpu.make_async_copy(wide.at[:, pl.ds(0, 3 * features)], mixed_out, out_sem.at[0])
+    mixed_store.start()
+    normed_store = pltpu.make_async_copy(normed.at[pl.ds(0, tokens), :], normed_out, out_sem.at[1])
+    normed_store.start()
+    for copy in out_loads:
+        copy.wait()
+    rim.wait_recv()
+    inner = (ring.x > 0).astype(F32)
+    lists = share_out(until(range(2, fixed)), blocks)
+
+    @pl.loop(0, blocks)
+    def _(r):
+        run_tick(lists, r)
+        at = rows_of(r)
+        gated = wide[at, :features] * wide[at, last_part]
+        before_at = pl.ds(pl.multiple_of(jnp.maximum(r * block - 8, 0), 8), 8)
+        before = wide[before_at, :features] * wide[before_at, last_part]
+        first = lax.rem(r * block, per_sequence) == 0
+        before = jnp.where(first, rim_in[(r * block) // per_sequence] * inner, before)
+        extended = jnp.concatenate([before, gated], axis=0)
+        convolved = (
+            taps[0:1, :] * extended[6 : block + 6] + taps[1:2, :] * extended[7 : block + 7] + taps[2:3, :] * gated
+        )
+        wide[at, conv_part] = convolved
+        mixed = (wide[at, middle] * convolved).astype(BF16)
+        mixer[at, :] = mixed
+        low = masked(r, dot_nn(mixed, out_first_s[...]))
+        low_out[at, :] = low
+        branch = jnp.concatenate([dot_nn(mixed, gate_w[0]), dot_nn(mixed, gate_w[1])], axis=1)
+        after = block_in[at, :].astype(F32) + (branch + dot_nn(low, out_second_s[...]))
+        total[at, :] = after
+        second_rows = (rms_unit(after)[1] * gain_second[...]).astype(BF16)
+        second[at, :] = second_rows
+        for k in range(2):
+            low_gu[k, at, :] = masked(r, dot_nn(second_rows, gate_up_first[k]))
+
+    stores = [
+        pltpu.make_async_copy(wide.at[:, pl.ds(3 * features, features)], conv_out, out_sem.at[2]),
+        pltpu.make_async_copy(mixer.at[pl.ds(0, tokens), :], mixer_out, out_sem.at[3]),
+        pltpu.make_async_copy(total, after_out, out_sem.at[4]),
+    ]
+    for copy in stores:
+        copy.start()
+    for unit in unit_list[2:]:
+        unit.collect()
 
     def down_load(j, s):
-        place = pl.ds(pl.multiple_of(j * FF_CHUNK, FF_CHUNK), FF_CHUNK)
-        return pltpu.make_async_copy(down_all.at[place, :], down_w.at[s], load_sem.at[s, 0])
+        return pltpu.make_async_copy(down_all.at[rows_of(j, FF_CHUNK), :], down_w.at[s], load_sem.at[s, 2])
 
     def gu_loads(j, s):
-        place = pl.ds(pl.multiple_of(j * FF_CHUNK, FF_CHUNK), FF_CHUNK)
+        place = rows_of(j, FF_CHUNK)
         return (
-            pltpu.make_async_copy(gu_all.at[0, :, place], gate_w.at[s], load_sem.at[s, 1]),
-            pltpu.make_async_copy(gu_all.at[1, :, place], up_w.at[s], load_sem.at[s, 2]),
+            pltpu.make_async_copy(gu_all.at[0, :, place], gate_w.at[s], load_sem.at[s, 0]),
+            pltpu.make_async_copy(gu_all.at[1, :, place], up_w.at[s], load_sem.at[s, 1]),
         )
 
-    per_tick = -(-steps // blocks)
-
-    def ticks(unit_action, r):
-        for k in range(per_tick):
-            step = r * per_tick + k + 1
-            when(step <= steps, functools.partial(unit_action, step))
-
     down_load(0, 0).start()
+    mixed_store.wait()
+    for copy in stores:
+        copy.wait()
+    lists = share_out([entry[3] for entry in entries], chunks)
 
     @pl.loop(0, chunks)
     def _(j):
@@ -368,157 +505,218 @@
             down_load(j + 1, 1 - s).start()
 
         down_load(j, s).wait()
-
-        @pl.loop(0, blocks)
+        run_tick(lists, j)
+        columns = rows_of(j, FF_CHUNK)
+
+        @pl.loop(0, wide_blocks)
         def _(r):
-            at = pl.ds(pl.multiple_of(r * ROW_BLOCK, ROW_BLOCK), ROW_BLOCK)
-
-            @pl.when(j == 0)
-            def _():
-                ticks(chunk_unit(0).relay, r)
-
-            @pl.when((j == 1) & (r == 0))
-            def _():
-                chunk_unit(1).own()
-
-            @pl.when(j == 2)
-            def _():
-                ticks(chunk_unit(0).relay_seq, r)
-
-            @pl.when(j == 3)
-            def _():
-                ticks(chunk_unit(1).relay, r)
-
-            @pl.when((j == 4) & (r == 0))
-            def _():
-                chunk_unit(2).own()
-
-            grad_hidden[j, at, :] = dot_nt(cotangent[at, :], down_w[s]) + dot_nt(
-                grad_low_down[at, :], first_down[j]
+            at = rows_of(r, wide_block)
+            wide[at, columns] = dot_nt(cotangent[at, :], down_w[s]) + dot_nt(
+                grad_low_down[at, :], first_down[columns, :]
             )
 
-    started.wait()
     chunk_unit(0).collect()
-    for copy in gu_loads(0, 0):
-        copy.start()
-    down_load(0, 0).start()
-
-    @pl.loop(0, chunks)
-    def _(j):
-        s = lax.rem(j, 2)
+
+    def begin(j, s):
         for copy in (down_load(j, s),) + gu_loads(j, s):
-            copy.wait()
-
-        @pl.loop(0, blocks)
-        def _(r):
-            at = pl.ds(pl.multiple_of(r * ROW_BLOCK, ROW_BLOCK), ROW_BLOCK)
-
-            @pl.when((r == 0) & (j + 3 < chunks))
-            def _():
-                chunk_unit(j + 3).own()
-
-            @pl.when(j + 2 < chunks)
-            def _():
-                ticks(chunk_unit(j + 2).relay, r)
-
-            @pl.when(j + 1 < chunks)
-            def _():
-                spread = -(-steps // max(blocks - 1, 1))
-                for k in range(spread):
-                    step = r * spread + k + 1
-                    when(step <= steps, functools.partial(chunk_unit(j + 1).relay_seq, step))
-
-                @pl.when(r == blocks - 1)
-                def _():
-                    chunk_unit(j + 1).collect()
-                    for copy in (down_load(j + 1, 1 - s),) + gu_loads(j + 1, 1 - s):
-                        copy.start()
-
-            rows_in = second[at, :]
-            gate = dot_nn(rows_in, gate_w[s]) + dot_nn(low_gu[0, at, :], second_gu[0, j])
-            up = dot_nn(rows_in, up_w[s]) + dot_nn(low_gu[1, at, :], second_gu[1, j])
-            back = grad_hidden[j, at, :]
-            sigmoid = 1.0 / (1.0 + jnp.exp(-gate))
-            active = gate * sigmoid
-            hidden = (active * up).astype(BF16)
-            grad_gate = (back * up * sigmoid * (1.0 + gate * (1.0 - sigmoid))).astype(BF16)
-            grad_up = (back * active).astype(BF16)
-            hidden_s[at, :] = hidden
-            gate_s[at, :] = grad_gate
-            up_s[at, :] = grad_up
-            total[at, :] += dot_nn(hidden, down_w[s])
-            grad_second[at, :] += dot_nt(grad_gate, gate_w[s]) + dot_nt(grad_up, up_w[s])
-            low_down[at, :] += dot_nn(hidden, first_down[j])
-            grad_low_gu[0, at, :] += dot_nt(grad_gate, second_gu[0, j])
-            grad_low_gu[1, at, :] += dot_nt(grad_up, second_gu[1, j])
-
-        base = j * FF_CHUNK
-        for offset, left, right in (
-            (0, grad_low_down[...], hidden_s),
-            (hidden_size, low_gu[0], gate_s),
-            (2 * hidden_size, low_gu[1], up_s),
-        ):
-            columns = pl.ds(pl.multiple_of(offset + base, LANES), FF_CHUNK)
-            grads[:, columns] = dot_tn(left, right[...]).astype(BF16)
-
-    half_low_down = (ADAPTER_SCALE * low_down[...] * mask).astype(BF16)
-    block_out[...] = (total[...] + dot_nn(half_low_down, second_down[...])).astype(BF16)
+            copy.start()
+
+    begin(0, 0)
+
+    def guarded(k, action):
+        when(k < comm_chunks, lambda: action(chunk_unit(k)))
+
+    def whole_unit(k, with_own):
+        unit = chunk_unit(k)
+        if with_own:
+            unit.own()
+        for step in range(1, steps + 1):
+            unit.relay(step)
+        for step in range(1, steps + 1):
+            unit.relay_seq(step)
+        unit.collect()
+
+    def group_ticks(i, s):
+        n = 2 * i
+
+        def go(k, name, *step):
+            return lambda: guarded(n + k, lambda unit: getattr(unit, name)(*step))
+
+        def take(k, chunk):
+            def action():
+                chunk_unit(n + k).collect()
+                begin(3 * i + chunk, lax.rem(s + chunk, 2))
+
+            return action
+
+        def only(chunk):
+            return lambda: begin(3 * i + chunk, lax.rem(s + chunk, 2))
+
+        more = i + 1 < chunks // 3
+        if not stepped:
+            return {
+                (0, 0): [lambda: whole_unit(n + 1, True), only(1)],
+                (1, 0): [only(2)],
+                (2, 0): [lambda: when(more, lambda: (whole_unit(n + 2, True), only(3)())[0])],
+            }
+        return {
+            (0, 0): [go(2, "relay", 3), go(3, "relay", 1), go(1, "relay_seq", 4), go(2, "relay_seq", 2)],
+            (0, 1): [take(1, 1), go(4, "own"), go(2, "relay", 4), go(3, "relay", 2), go(2, "relay_seq", 3), go(3, "relay_seq", 1)],
+            (1, 0): [go(3, "relay", 3), go(4, "relay", 1), go(2, "relay_seq", 4), go(3, "relay_seq", 2)],
+            (1, 1): [only(2), go(5, "own"), go(3, "relay", 4), go(4, "relay", 2)],
+            (2, 0): [go(3, "relay_seq", 3), go(4, "relay_seq", 1)],
+            (2, 1): [lambda: when(more, take(2, 3))],
+        }
+
+    @pl.loop(0, chunks // 3)
+    def _(i):
+        for c in range(3):
+            j = 3 * i + c
+            s = lax.rem(j, 2)
+            columns = rows_of(j, FF_CHUNK)
+            for copy in (down_load(j, s),) + gu_loads(j, s):
+                copy.wait()
+            ticks = group_ticks(i, lax.rem(3 * i, 2))
+            partial[...] = jnp.zeros_like(partial)
+
+            @pl.loop(0, wide_blocks)
+            def _(r, c=c, j=j, s=s, columns=columns, ticks=ticks):
+                for (wanted, tick), actions in ticks.items():
+                    if wanted == c:
+
+                        @pl.when(r == tick)
+                        def _(actions=actions):
+                            for action in actions:
+                                action()
+
+                at = rows_of(r, wide_block)
+                values = second[at, :]
+                lows = (grad_low_down[at, :], low_gu[0, at, :], low_gu[1, at, :])
+                gate = dot_nn(values, gate_w[s]) + dot_nn(lows[1], second_gu[0, :, columns])
+                up = dot_nn(values, up_w[s]) + dot_nn(lows[2], second_gu[1, :, columns])
+                back = wide[at, columns]
+                sigmoid = 1.0 / (1.0 + jnp.exp(-gate))
+                active = gate * sigmoid
+                hidden = (active * up).astype(BF16)
+                grad_gate = (back * up * (sigmoid + active * (1.0 - sigmoid))).astype(BF16)
+                grad_up = (back * active).astype(BF16)
+                total[at, :] += dot_nn(hidden, down_w[s])
+                grad_second[at, :] += dot_nt(grad_gate, gate_w[s]) + dot_nt(grad_up, up_w[s])
+                low_down[at, :] += dot_nn(hidden, first_down[columns, :])
+                grad_low_gu[0, at, :] += dot_nt(grad_gate, second_gu[0, :, columns])
+                grad_low_gu[1, at, :] += dot_nt(grad_up, second_gu[1, :, columns])
+                for k, right in enumerate((hidden, grad_gate, grad_up)):
+                    partial[k] += dot_tn(lows[k], right)
+
+            for k in range(3):
+                place = pl.ds(pl.multiple_of(k * hidden_size + j * FF_CHUNK, FF_CHUNK), FF_CHUNK)
+                grads[:, place] = partial[k].astype(BF16)
+
+    normed_store.wait()
     base = 3 * hidden_size
-    grads[:, base + 2 * features : base + 3 * features] = dot_tn(half_low_down, cotangent[...]).astype(BF16)
+
+    @pl.loop(0, blocks)
+    def _(r):
+        at = rows_of(r)
+        low = masked(r, low_down[at, :])
+        grad_low_down[at, :] = low
+        normed[at, :] = (total[at, :] + dot_nn(low, second_down[...])).astype(BF16)
+        for k in range(2):
+            back_low = masked(r, grad_low_gu[k, at, :])
+            low_gu[k, at, :] = back_low
+            grad_second[at, :] += dot_nt(back_low, gate_up_first[k])
+
+    block_store = pltpu.make_async_copy(normed.at[pl.ds(0, tokens), :], block_out, out_sem.at[1])
+    block_store.start()
+    grads[:, base + 2 * features : base + 3 * features] = dot_tn(grad_low_down[...], cotangent[...]).astype(BF16)
     for k in range(2):
-        back_low = (ADAPTER_SCALE * grad_low_gu[k] * mask).astype(BF16)
         columns = slice(base + k * features, base + (k + 1) * features)
-        grads[:, columns] = dot_tn(back_low, second[...]).astype(BF16)
-        grad_second[...] += dot_nt(back_low, first_gu[k])
-
-    down_unit.drain()
-
-    @pl.loop(0, chunks)
+        grads[:, columns] = dot_tn(low_gu[k], second[:tokens, :]).astype(BF16)
+
+    for unit in unit_list:
+        unit.drain()
+
+    @pl.loop(0, comm_chunks)
     def _(k):
         chunk_unit(k).drain()
 
-
-def feed_forward(fsdp_size, per_sequence, grads_width, second, cotangent, after, pick, pick_t, adapters, own):
-    tokens, features = second.shape
-    hidden_size = own[0].shape[1]
+    rim.wait_send()
+    block_store.wait()
+
+
+def front(sizes, per_sequence, grads_width, operands):
+    fsdp_size, seq_size = sizes
+    block_in, cotangent, pick = operands[:3]
+    own = operands[-5:]
+    tokens, features = cotangent.shape
+    hidden_size = own[2].shape[1]
     slots = pick.shape[1]
-    chunks = hidden_size // FF_CHUNK
+    sequences = tokens // per_sequence
+    units = 4 + 2 * (hidden_size // FF_CHUNK) // 3
+    tall = max(tokens, features)
+    stages = 3 * -(-hidden_size // features)
+
+    def shape(*dims, kind=BF16):
+        return jax.ShapeDtypeStruct(dims, kind)
+
     return pl.pallas_call(
-        functools.partial(feed_forward_kernel, fsdp_size, per_sequence),
+        functools.partial(front_kernel, sizes, per_sequence),
         out_shape=(
-            jax.ShapeDtypeStruct((tokens, features), BF16),
-            jax.ShapeDtypeStruct((tokens, features), F32),
-            jax.ShapeDtypeStruct((slots, grads_width), BF16),
-            jax.ShapeDtypeStruct((2, features, hidden_size), BF16),
-            jax.ShapeDtypeStruct((hidden_size, features), BF16),
+            shape(tokens, features, kind=F32),
+            shape(slots, grads_width),
+            shape(tokens, slots),
+            shape(tokens, slots),
+            shape(features, slots),
+            shape(slots, 3 * features),
+            shape(features, slots),
+            shape(slots, features),
+            shape(tokens, features),
+            shape(tokens, features, kind=F32),
+            shape(tokens, 3 * features, kind=F32),
+            shape(tokens, features, kind=F32),
+            shape(tokens, features),
+            shape(tokens, features),
+            shape(features, 3 * features),
+            shape(features, features),
+            shape(2, features, hidden_size),
+            shape(hidden_size, features),
         ),
-        in_specs=[IN_VMEM, IN_VMEM, ANYWHERE] + [IN_VMEM] * 8 + [ANYWHERE] * 3,
-        out_specs=(IN_VMEM, IN_VMEM, IN_VMEM, ANYWHERE, ANYWHERE),
-        scratch_shapes=unit_sems(1 + chunks, fsdp_size // 2)
-        + [pltpu.SemaphoreType.DMA((2, 3)), pltpu.SemaphoreType.DMA((3, 3))]
+        in_specs=[IN_VMEM] * 14 + [ANYWHERE] * 8,
+        out_specs=(IN_VMEM,) * 8 + (ANYWHERE,) * 10,
+        scratch_shapes=unit_sems(units, fsdp_size // 2)
+        + [
+            pltpu.SemaphoreType.DMA((2, 5)),
+            pltpu.SemaphoreType.DMA((2, 3)),
+            pltpu.SemaphoreType.DMA((stages,)),
+            pltpu.SemaphoreType.DMA((2,)),
+            pltpu.SemaphoreType.DMA((5,)),
+        ]
         + [pltpu.VMEM(member.shape, BF16) for member in own]
         + [
             pltpu.VMEM((tokens, features), F32),
-            pltpu.VMEM((chunks, tokens, FF_CHUNK), F32),
+            pltpu.VMEM((tokens, hidden_size), F32),
             pltpu.VMEM((2, features, FF_CHUNK), BF16),
             pltpu.VMEM((2, features, FF_CHUNK), BF16),
             pltpu.VMEM((2, FF_CHUNK, features), BF16),
-            pltpu.VMEM((tokens, FF_CHUNK), BF16),
-            pltpu.VMEM((tokens, FF_CHUNK), BF16),
-            pltpu.VMEM((tokens, FF_CHUNK), BF16),
+            pltpu.VMEM((tall, features), BF16),
+            pltpu.VMEM((tall, features), BF16),
+            pltpu.VMEM((tall, features), BF16),
             pltpu.VMEM((2, features, slots), BF16),
-            pltpu.VMEM((chunks, FF_CHUNK, slots), BF16),
-            pltpu.VMEM((2, chunks, slots, FF_CHUNK), BF16),
+            pltpu.VMEM((hidden_size, slots), BF16),
+            pltpu.VMEM((2, slots, hidden_size), BF16),
             pltpu.VMEM((slots, features), BF16),
             pltpu.VMEM((2, tokens, slots), BF16),
             pltpu.VMEM((tokens, slots), BF16),
             pltpu.VMEM((tokens, slots), F32),
             pltpu.VMEM((2, tokens, slots), F32),
+            pltpu.VMEM((3, slots, FF_CHUNK), F32),
+            pltpu.VMEM((sequences, 8, features), F32),
+            pltpu.VMEM((sequences, 8, features), F32),
         ],
         compiler_params=pltpu.CompilerParams(
-            collective_id=1, has_side_effects=True, vmem_limit_bytes=VMEM_LIMIT
+            collective_id=0, has_side_effects=True, vmem_limit_bytes=VMEM_LIMIT_FRONT
         ),
-    )(second, cotangent, after, pick, pick_t, *adapters, *own)
+    )(*operands)
 
 
 class Shares:
@@ -701,7 +899,6 @@
     early.start()
     for copy in loads[:3]:
         copy.wait()
-    mask = slot_mask(block, slots, per_sequence)
 
     def rows_of(r):
         return pl.ds(pl.multiple_of(r * block, block), block)
@@ -936,11 +1133,6 @@
     )(early.reshape(-1, LANES, LANES), late.reshape(-1, LANES, LANES))
 
 
-def rms_parts(values):
-    inverse = lax.rsqrt(jnp.mean(values * values, axis=-1, keepdims=True) + EPSILON)
-    return (inverse, values * inverse)
-
-
 def per_device(
     block_input,
     output_grad,
@@ -972,59 +1164,45 @@
     hidden_size = gate_weight.shape[1]
     shares = Shares(fsdp_size * seq_size, features, hidden_size)
     kernel = conv_weight.astype(F32)
-    gain_first = first_gain.astype(F32)
-    gain_second = second_gain.astype(F32)
+    gain_first = first_gain.astype(F32)[None, :]
+    gain_second = second_gain.astype(F32)[None, :]
     wanted = jnp.repeat(adapter_ids.reshape(sequences) * R, R) + jnp.tile(jnp.arange(R), sequences)
     pick = (lax.broadcasted_iota(jnp.int32, (LANES, slots), 0) == wanted[None, :]).astype(BF16)
     pick_t = (lax.broadcasted_iota(jnp.int32, (slots, LANES), 1) == wanted[:, None]).astype(BF16)
-    mask = slot_mask(tokens, slots, local_len)
-    in_first, out_first = (dot_nn(m, pick).astype(BF16) for m in (infirst_adapter, outfirst_adapter))
-    in_second, out_second = (dot_nn(pick_t, m).astype(BF16) for m in (insecond_adapter, outsecond_adapter))
-
-    weight_in, weight_out = gather_mixer(fsdp_size, in_weight, out_weight)
-    inputs = block_input.reshape(tokens, features).astype(F32)
     cotangent = output_grad.reshape(tokens, features)
-    inverse_first, unit_first = rms_parts(inputs)
-    normed = (unit_first * gain_first).astype(BF16)
-    low_in = (dot_nn(normed, in_first) * mask * ADAPTER_SCALE).astype(BF16)
-    mixed_in = dot_nn(normed, weight_in) + dot_nn(low_in, in_second)
-    first_part = mixed_in[:, :features]
-    middle_part = mixed_in[:, features : 2 * features]
-    last_part = mixed_in[:, 2 * features :]
-    gated_values = (first_part * last_part).reshape(sequences, local_len, features)
-    rim_rows = from_behind(gated_values[:, local_len - 2 :, :], "seq", 1)
-    extended = jnp.concatenate([rim_rows, gated_values], axis=1)
-    conv_out = (
-        kernel[0] * extended[:, :local_len]
-        + kernel[1] * extended[:, 1 : local_len + 1]
-        + kernel[2] * extended[:, 2:]
-    ).reshape(tokens, features)
-    mixer_out = (middle_part * conv_out).astype(BF16)
-    low_out = (dot_nn(mixer_out, out_first) * mask * ADAPTER_SCALE).astype(BF16)
-    after_mixer = inputs + (dot_nn(mixer_out, weight_out) + dot_nn(low_out, out_second))
-    inverse_second, unit_second = rms_parts(after_mixer)
-    second = (unit_second * gain_second).astype(BF16)
-
-    block_output, grad_second, grads_late, _, _ = feed_forward(
-        fsdp_size,
+    block_in = block_input.reshape(tokens, features)
+    (
+        grad_second, grads_early, low_in, low_out, in_first, in_second, out_first, out_second,
+        block_output, after_mixer, mixed_in, conv_out, mixer_out, normed, weight_in, weight_out, _, _,
+    ) = front(
+        (fsdp_size, seq_size),
         local_len,
         shares.early_width,
-        second,
-        cotangent,
-        after_mixer,
-        pick,
-        pick_t,
         (
+            block_in,
+            cotangent,
+            pick,
+            pick_t,
+            kernel,
+            gain_first,
+            gain_second,
+            infirst_adapter,
+            insecond_adapter,
+            outfirst_adapter,
+            outsecond_adapter,
             gatefirst_adapter,
+            upfirst_adapter,
+            downsecond_adapter,
             gatesecond_adapter,
-            upfirst_adapter,
             upsecond_adapter,
             downfirst_adapter,
-            downsecond_adapter,
+            in_weight,
+            out_weight,
+            gate_weight,
+            up_weight,
+            down_weight,
         ),
-        (gate_weight, up_weight, down_weight),
     )
-
     grad_input, early, late = mixer_back(
         (fsdp_size, seq_size),
         local_len,
@@ -1033,7 +1211,7 @@
             grad_second,
             after_mixer,
             cotangent,
-            block_input.reshape(tokens, features),
+            block_in,
             mixed_in,
             conv_out,
             mixer_out,
@@ -1046,11 +1224,11 @@
             out_second,
             pick_t,
             kernel,
-            gain_first[None, :],
-            gain_second[None, :],
+            gain_first,
+            gain_second,
             weight_in,
             weight_out,
-            grads_late,
+            grads_early,
         ),
     )
     shape = block_input.shape

time: 392 us -> 313 us (0.80); the launches traced: 384 us -> 312 us
  Pallas kernels: 340 us -> 301 us
  matrix products: 18.7 us -> 0 us
  other arithmetic: 13.4 us -> 5.88 us
    pallas_call x2 -> x1, Pallas kernels: 248 us -> 208 us  [front(): pl.pallas_call(functools.partial(front_kernel, sizes, per_sequence), out_...]
    dot_general x10 -> x0, matrix products: 18.7 us -> none  [dot_nn(): return jnp.dot(left, right, preferred_element_type=F32)]
    convert_element_type x5 -> x0, other arithmetic: 5.39 us -> none  [the longest x1 1.86 us: per_device(): normed = (unit_first * gain_first).astype(BF16)]
    unnamed x47 -> x4, local copies, waits for them, and re-layouts: 8.23 us -> 4.55 us
  transfers between devices with their start and end apart: 1 -> 0, of which waited for: 0 -> 0; matrix products, arithmetic and copies ran while one was open for 1% -> 0% of each run, Pallas kernels for 0% -> 0%
where the time goes in v4:
time: 313 us; the launch traced here: 312 us
  Pallas kernels  301 us (96%)
  other arithmetic  5.88 us (2%)
  local copies, waits for them, and re-layouts  4.64 us (1%)
    pallas_call x1, Pallas kernels, front(): pl.pallas_call(functools.partial(front_kernel, sizes, per_sequence), out_...  208 us
    pallas_call x1, Pallas kernels, mixer_back(): pl.pallas_call(functools.partial(mixer_back_kernel, sizes, per_sequence,...  84 us
    pallas_call x1, Pallas kernels, spread(): pl.pallas_call(functools.partial(spread_kernel, layout), out_shape=tuple(...  8.54 us

profile of v4, /device:TPU:0, one launch (start us, length us, event | category | flops | bytes accessed | tf_op | source)
XLA Modules:
  0.0 312.2 jit_solution(510941329872432077)
XLA Ops:
  0.6 0.7 multiply_bitcast_fusion
  1.3 0.1 iota_add_fusion
  1.4 0.1 add.15
  1.5 1.3 broadcast_in_dim.20
  2.7 1.3 broadcast_in_dim.21
  4.0 0.7 fusion.1.refs_3_.refs_14_
  4.7 1.3 convert_element_type.13.refs_4_.refs_15_
  6.0 0.6 fusion.refs_2_
  6.6 208.5 %shard_map.292 = (f32[1024,1024]{1,0:T(8,128)}, bf16[32,16896]{1,0:T(8,128)(2,1)}, bf16[1024,32]{1,0:T(8,128)(2,1)}, bf16[1024,32]{1,0:T(8,128)(2,1)}, bf16[1024...) custom-call(bf16[1024,1024]{1,0:T(8,128)(2,1)} %bitcast.14, ...), custom_call_target="tpu_custom_call" | custom-call | tf_op jit(solution)/shard_map/pallas_call | solution.py:662
  215.1 84.0 %shard_map.293 = (bf16[1024,1024]{1,0:T(8,128)(2,1)}, bf16[16,2,4,128,128]{4,3,2,1,0:T(8,128)(2,1)}, bf16[16,2,2,128,128]{4,3,2,1,0:T(8,128)(2,1)}) custom-call(f32[1024,1024]{1,0:T(8,128)} %get-tuple-element.42.refs_0_, f32[1024,1024]{1,0:T(8,128)} %get-tuple-element.43.refs_1_, bf16[1024,1024]{1,0:T(8,128)(2,1)} %bitcast.17, bf16[1024,1024]{1,0:T(8,128)(2,1)} %bitcast.15, ...), custom_call_target="tpu_custom_call" | custom-call | tf_op jit(solution)/shard_map/pallas_call | solution.py:1053
  299.1 8.5 %shard_map.294 = (f32[1024,128]{1,0:T(8,128)}, f32[128,3072]{1,0:T(8,128)}, f32[1024,128]{1,0:T(8,128)}, f32[128,1024]{1,0:T(8,128)}, f32[1024,128]{1,0:T(8,128)...) custom-call(bf16[128,128,128]{2,1,0:T(8,128)(2,1)} %bitcast.18, ...), custom_call_target="tpu_custom_call" | custom-call | tf_op jit(solution)/shard_map/pallas_call | solution.py:1127
  307.7 0.0 copy-start
  307.7 3.2 %copy.37 = bf16[2,1,512,1024]{3,2,1,0:T(8,128)(2,1)} copy(bf16[2,1,512,1024]{3,2,1,0:T(8,128)(2,1)} %bitcast.20) | data formatting | bytes 4194304
  310.9 0.0 copy-done
  310.9 1.3 copy.38
Async XLA Ops:
  307.7 3.2 %copy-start = (bf16[1024,1024]{1,0:T(8,128)(2,1)S(1)}, bf16[1024,1024]{1,0:T(8,128)(2,1)}, u32[]{:S(2)}) copy-start(bf16[1024,1024]{1,0:T(8,128)(2,1)} %get-tuple-element.57) | copy-start | bytes 6291460

commit v5 on v4

v5 whole, which is shorter than its diff:
```python
import functools

import jax
import jax.numpy as jnp
from jax import lax
from jax.experimental import pallas as pl
from jax.experimental.pallas import tpu as pltpu
from jax.sharding import PartitionSpec as P

R = 16
LANES = 128
EPSILON = 1e-05
ADAPTER_SCALE = 0.5
MESH = pl.DeviceIdType.MESH
BF16 = jnp.bfloat16
F32 = jnp.float32
VMEM_LIMIT = 62 * 1024 * 1024
FF_CHUNK = 512
ROW_BLOCK = 256
WIDE_BLOCK = 512
VMEM_LIMIT_FRONT = 63 * 1024 * 1024


def dot_nn(left, right):
    return jnp.dot(left, right, preferred_element_type=F32)


def dot_nt(left, right):
    return lax.dot_general(left, right, (((1,), (1,)), ((), ())), preferred_element_type=F32)


def dot_tn(left, right):
    return lax.dot_general(left, right, (((0,), (0,)), ((), ())), preferred_element_type=F32)


def when(condition, action):
    if isinstance(condition, bool):
        if condition:
            action()
    else:
        pl.when(condition)(action)


class Ring:
    def __init__(self, fsdp_size):
        self.count = fsdp_size // 2
        self.me = lax.axis_index("fsdp")
        self.core = lax.rem(self.me, 2)
        chip = self.me // 2
        self.grid = fsdp_size == 16
        if self.grid:
            z, y = chip // 2, lax.rem(chip, 2)
            self.place = y * z + (1 - y) * (7 - z)
        else:
            self.place = chip
        x = lax.axis_index("seq")
        self.x = x
        self.role = lax.rem(x, 2)
        self.to_next = {"fsdp": self.device(lax.rem(self.place + 1, self.count))}
        self.to_prev = {"fsdp": self.device(lax.rem(self.place + self.count - 1, self.count))}
        self.to_core = {"fsdp": self.me + 1 - 2 * self.core}
        self.to_seq = {"seq": x + 1 - 2 * self.role}

    def device(self, place):
        if self.grid:
            y = 1 - place // 4
            z = y * place + (1 - y) * (7 - place)
            return (z * 2 + y) * 2 + self.core
        return place * 2 + self.core

    def at_step(self, direction, step):
        if direction == 0:
            return self.device(lax.rem(self.place + self.count - step, self.count))
        return self.device(lax.rem(self.place + step, self.count))

    def target(self, k, seq_size, devices):
        d = lax.rem(self.me * seq_size + self.x + k, devices)
        return d, {"fsdp": d // seq_size, "seq": lax.rem(d, seq_size)}

    def greet(self, seq_size, devices):
        barrier = pltpu.get_barrier_semaphore()

        @pl.loop(1, devices)
        def _(k):
            device = self.target(k, seq_size, devices)[1]
            pl.semaphore_signal(barrier, inc=1, device_id=device, device_id_type=MESH)

        pl.semaphore_wait(barrier, devices - 1)


class Exchange:
    def __init__(self, ring, seq_size, devices, source, got, sems):
        self.ring, self.seq_size, self.devices = ring, seq_size, devices
        self.source, self.got, self.sems = source, got, sems
        self.me = ring.me * seq_size + ring.x

    def own(self):
        return pltpu.make_async_copy(self.source(self.me), self.got.at[self.me], self.sems.at[2])

    def start(self):
        self.own().start()

        @pl.loop(1, self.devices)
        def _(k):
            d, device = self.ring.target(k, self.seq_size, self.devices)
            pltpu.make_async_remote_copy(
                src_ref=self.source(d),
                dst_ref=self.got.at[self.me],
                send_sem=self.sems.at[0],
                recv_sem=self.sems.at[1],
                device_id=device,
                device_id_type=MESH,
            ).start()

    def all_pieces(self):
        others = self.got.at[pl.ds(0, self.devices - 1)]
        return pltpu.make_async_remote_copy(
            src_ref=others,
            dst_ref=others,
            send_sem=self.sems.at[0],
            recv_sem=self.sems.at[1],
            device_id=self.ring.to_next,
            device_id_type=MESH,
        )

    def arrived(self):
        self.own().wait()
        self.all_pieces().wait_recv()

    def drain(self):
        self.all_pieces().wait_send()


class Unit:
    def __init__(self, ring, number, spot, sems):
        self.ring, self.number, self.spot = ring, number, spot
        self.send, self.ring_sem, self.seq_sem, self.core_sem = sems
        half = ring.count // 2
        self.reaches = ((half, ring.count - 1 - half), (ring.count - 1 - half, half))
        self.steps = half
        self.others = ring.count - 1

    def copy(self, spot, slot, sem, device):
        return pltpu.make_async_remote_copy(
            src_ref=spot,
            dst_ref=spot,
            send_sem=self.send.at[self.number, slot],
            recv_sem=sem,
            device_id=device,
            device_id_type=MESH,
        )

    def arrived(self, spot, sem):
        self.copy(spot, 0, sem, self.ring.to_next).wait_recv()

    def own(self):
        ring, n = self.ring, self.number
        for slot, third in ((0, ring.role), (1, 2)):
            spot = self.spot(third, ring.me)
            self.copy(spot, 2 * slot, self.ring_sem.at[n, slot, 0], ring.to_next).start()
            self.copy(spot, 2 * slot + 1, self.ring_sem.at[n, slot, self.others - 1], ring.to_prev).start()
        for k, third in enumerate((ring.role, 1 - ring.role, 2)):
            self.copy(self.spot(third, ring.me), 4 + k, self.core_sem.at[n, third, 0], ring.to_core).start()

    def relay(self, step):
        ring, n, others = self.ring, self.number, self.others
        for slot, third in ((0, ring.role), (1, 2)):
            for direction in (0, 1):
                reach = self.reaches[slot][direction]
                lane = step - 1 if direction == 0 else others - step
                spot = self.spot(third, ring.at_step(direction, step))

                def forward(slot=slot, direction=direction, lane=lane, spot=spot):
                    onward = self.ring_sem.at[n, slot, lane + 1 - 2 * direction]
                    target = (ring.to_next, ring.to_prev)[direction]
                    self.copy(spot, 7 + slot * others + lane, onward, target).start()

                def take(slot=slot, third=third, reach=reach, lane=lane, spot=spot, forward=forward):
                    self.arrived(spot, self.ring_sem.at[n, slot, lane])
                    when(step < reach, forward)
                    if slot == 0:
                        self.copy(spot, 7 + 2 * others + lane, self.seq_sem.at[n, lane], ring.to_seq).start()
                    core = self.core_sem.at[n, third, 1 + lane]
                    self.copy(spot, 7 + (3 + slot) * others + lane, core, ring.to_core).start()

                when(step <= reach, take)

    def relay_seq(self, step):
        ring, n, others = self.ring, self.number, self.others
        third = 1 - ring.role
        for direction in (0, 1):
            reach = self.reaches[0][direction]
            lane = step - 1 if direction == 0 else others - step
            spot = self.spot(third, ring.at_step(direction, step))

            def take(lane=lane, spot=spot):
                self.arrived(spot, self.seq_sem.at[n, lane])
                core = self.core_sem.at[n, third, 1 + lane]
                self.copy(spot, 7 + 5 * others + lane, core, ring.to_core).start()

            when(step <= reach, take)

    def collect(self):
        for third in range(3):
            for lane in range(self.others + 1):
                self.arrived(self.spot(third, self.ring.me), self.core_sem.at[self.number, third, lane])

    def drain(self):
        ring, others = self.ring, self.others

        def done(third, slot):
            self.copy(self.spot(third, ring.me), slot, self.seq_sem.at[self.number, 0], ring.to_next).wait_send()

        for slot, third in ((0, 0), (1, 2)):
            done(third, 2 * slot)
            done(third, 2 * slot + 1)
            for direction in (0, 1):
                reach = self.reaches[slot][direction]
                for step in range(1, reach + 1):
                    lane = step - 1 if direction == 0 else others - step
                    if step < reach:
                        done(third, 7 + slot * others + lane)
                    done(third, 7 + (3 + slot) * others + lane)
        for lane in range(others):
            done(0, 7 + 2 * others + lane)
            done(0, 7 + 5 * others + lane)
        for k, third in enumerate((0, 0, 2)):
            done(third, 4 + k)


def unit_sems(units, count):
    return [
        pltpu.SemaphoreType.DMA((units, 7 + 6 * (count - 1))),
        pltpu.SemaphoreType.DMA((units, 2, count - 1)),
        pltpu.SemaphoreType.DMA((units, count - 1)),
        pltpu.SemaphoreType.DMA((units, 3, count)),
    ]


def move_in(moves, sems):
    inward = [pltpu.make_async_copy(a, b, sems.at[0, k]) for k, (a, b, _) in enumerate(moves)]
    outward = [pltpu.make_async_copy(b, c, sems.at[1, k]) for k, (_, b, c) in enumerate(moves)]
    for copy in inward:
        copy.start()
    for first, second in zip(inward, outward):
        first.wait()
        second.start()
    return outward


def row_spot(landing, rows, start, size, third, owner):
    return landing.at[pl.ds(owner * rows + start + third * size, size), :]


def column_spot(landing, rows, width, last, third, owner):
    size = last if isinstance(third, int) and third == 2 else width
    start = third * width if isinstance(third, int) else pl.multiple_of(third * width, LANES)
    return landing.at[pl.ds(owner * rows, rows), pl.ds(start, size)]


def down_pieces(down_rows):
    return 3 if down_rows % 288 == 0 else 1


def in_spot(landing, rows, part, half, third, owner):
    start = pl.multiple_of(third * part + half * (part // 2), LANES)
    return landing.at[pl.ds(owner * rows, rows), pl.ds(start, part // 2)]


def chunk_spot(landing, rows, size, chunk, third, owner):
    start = pl.multiple_of((chunk * 3 + third) * size, LANES)
    return landing.at[:, pl.ds(owner * rows, rows), pl.ds(start, size)]


class Plan:
    LINK, CORE, DELAY, COST = 37e3, 200e3, 1.7, 0.25
    WINDOWS = (4, 8, 1.5, 6, 1.5, 4, 1, 8, 1, 3, 2, 2)

    def __init__(self, units, sizes):
        self.units, self.sizes = units, sizes
        self.now = 0.0
        self.free = {"next": 0.0, "prev": 0.0, "seq": 0.0, "core": 0.0}
        self.steps = units[0].steps
        self.owned = 0
        self.arrival, self.core, self.left, self.collected = {}, {}, {}, set()
        self.list = []

    def send(self, link, size):
        if size:
            rate = self.CORE if link == "core" else self.LINK
            self.free[link] = max(self.free[link], self.now) + size / rate
        return self.free[link] + self.DELAY

    def run_own(self):
        u = self.owned
        self.owned += 1
        shared, common = self.sizes[u]
        self.list.append(self.units[u].own)
        self.now += self.COST
        size = shared + common
        self.arrival[(u, "ring", 1)] = max(self.send("next", size), self.send("prev", size))
        self.core[u] = self.send("core", 2 * shared + common)
        self.left[u] = 2 * self.steps

    def run(self, key):
        u, kind, step = key
        del self.arrival[key]
        shared, common = self.sizes[u]
        unit = self.units[u]
        self.left[u] -= 1
        self.now += self.COST
        if kind == "seq":
            self.list.append(functools.partial(unit.relay_seq, step))
            lanes = sum(step <= reach for reach in unit.reaches[0])
            self.core[u] = max(self.core[u], self.send("core", lanes * shared))
            return
        self.list.append(functools.partial(unit.relay, step))
        across = inward = 0
        onward = []
        for size, reaches, is_shared in ((shared, unit.reaches[0], True), (common, unit.reaches[1], False)):
            for link, reach in zip(("next", "prev"), reaches):
                if step <= reach:
                    inward += size
                    across += size if is_shared else 0
                if step < reach:
                    onward.append(self.send(link, size))
        if onward:
            self.arrival[(u, "ring", step + 1)] = max(onward)
        self.arrival[(u, "seq", step)] = self.send("seq", across)
        self.core[u] = max(self.core[u], self.send("core", inward))

    def ready(self):
        return [key for key, at in sorted(self.arrival.items()) if at <= self.now]

    def pump(self):
        while True:
            keys = self.ready()
            if keys:
                self.run(keys[0])
            elif (
                self.owned < len(self.units)
                and max(self.free["next"], self.free["prev"]) - self.now < self.WINDOWS[self.owned % 12]
            ):
                self.run_own()
            else:
                return

    def can_collect(self, u):
        return u < self.owned and self.left[u] == 0 and self.core[u] <= self.now

    def collect(self, u):
        if u not in self.collected:
            self.collected.add(u)
            self.list.append(self.units[u].collect)
            self.now += self.COST

    def need(self, numbers):
        for u in numbers:
            if u in self.collected:
                continue
            while not self.can_collect(u):
                self.pump()
                if self.can_collect(u):
                    break
                if u < self.owned and self.left[u] == 0:
                    self.now = max(self.now, self.core[u])
                elif self.arrival:
                    self.now = max(self.now, min(self.arrival.values()))
                else:
                    self.run_own()
            self.collect(u)

    def take(self):
        taken, self.list = self.list, []
        return taken

    def tick(self, duration):
        self.pump()
        taken = self.take()
        self.now += duration
        return taken


def run_tick(lists, tick):
    for k, actions in enumerate(lists):
        if not actions:
            continue

        @pl.when(tick == k)
        def _(actions=actions):
            for action in actions:
                action()


def rms_unit(rows):
    inverse = lax.rsqrt(jnp.mean(rows * rows, axis=-1, keepdims=True) + EPSILON)
    return inverse, rows * inverse


def rms_back(scaled, inverse, unit_rows):
    return inverse * (scaled - unit_rows * jnp.mean(scaled * unit_rows, axis=-1, keepdims=True))


ANYWHERE = pl.BlockSpec(memory_space=pl.ANY)
IN_VMEM = pl.BlockSpec(memory_space=pltpu.VMEM)


class Shares:
    def __init__(self, devices, features, hidden_size):
        self.devices = devices
        self.wide, self.narrow = hidden_size // LANES, features // LANES
        self.chunk = FF_CHUNK // LANES
        self.per_chunk = 3 * self.chunk
        third = 3 * self.per_chunk
        names = ("down_first", "gate_second", "up_second")

        def of_third(k):
            return [
                (name, (3 * k + c) * self.chunk + i) for c in range(3) for name in names for i in range(self.chunk)
            ]

        def all_of(name, count):
            return [(name, i) for i in range(count)]

        self.used = min(third, devices)
        self.pitch = third
        sets = [of_third(0), of_third(1)]
        self.spare = [tiles[self.used :] for tiles in sets]
        sets = [tiles[: self.used] for tiles in sets]
        narrow = self.narrow
        rest = of_third(2) + all_of("gate_first", narrow) + all_of("up_first", narrow)
        rest += all_of("down_second", narrow) + self.spare[0] + self.spare[1]
        self.rest_all = len(rest)
        self.per = max(1, len(rest) // devices)
        self.rest_used = min(len(rest), self.per * devices)
        self.left = len(rest) - self.rest_used
        sets.append(rest[: self.rest_used])
        sets.append(rest[self.rest_used :] + all_of("out_first", narrow) + all_of("out_second", narrow))
        sets.append(all_of("in_first", narrow) + all_of("in_second", 3 * narrow))
        self.sets = sets
        self.rest_start = 2 * self.pitch
        self.grads_width = (self.rest_start + self.rest_all) * LANES

    def is_first(self, number, tile):
        flags = [name.endswith("first") for name, _ in self.sets[number]]
        found, start = tile < 0, 0
        for k in range(1, len(flags) + 1):
            if k == len(flags) or flags[k] != flags[start]:
                if flags[start]:
                    found = found | ((tile >= start) & (tile < k))
                start = k
        return found

    def places(self):
        found = {}
        for number, tiles in enumerate(self.sets):
            for k, tile in enumerate(tiles):
                if number == 2:
                    found[tile] = (0, (2 + self.per) * (k // self.per) + 2 + k % self.per)
                else:
                    found[tile] = (0, (2 + self.per) * k + number) if number < 2 else (1, 2 * k + number - 3)
        return found


def column_tiles(source, start, count, used, d, devices):
    if used // count < devices:
        d = lax.rem(d, used // count)
    return source.at[:, pl.ds(pl.multiple_of((start + d * count) * LANES, LANES), count * LANES)]


class Sum:
    def __init__(self, ring, seq_size, number, landing, is_first, got, result, sems, unit_sems_refs):
        self.ring, self.seq_size, self.landing = ring, seq_size, landing
        self.is_first, self.got, self.result = is_first, got, result
        self.seq_sem, self.local_sem = sems
        self.place = landing.at[ring.me, ring.x]
        self.unit = Unit(ring, number, self.spot, unit_sems_refs)

    def spot(self, third, owner):
        size = 32 if isinstance(third, int) and third == 2 else 48
        return self.landing.at[owner, :, :, pl.ds(third * 48, size), :]

    def add(self, chosen):
        tiles = self.result.shape[0]
        for t in range(tiles):
            tile = dot_tn(chosen, self.got(t))
            self.result[t] = jnp.where(self.is_first(t), tile.T, tile).astype(BF16)
        store = pltpu.make_async_copy(self.result, self.place, self.local_sem.at[0])
        store.start()
        store.wait()
        for k in range(1, self.seq_size):
            self.across(k).start()

    def across(self, k):
        return pltpu.make_async_remote_copy(
            src_ref=self.place,
            dst_ref=self.place,
            send_sem=self.seq_sem.at[0, k],
            recv_sem=self.seq_sem.at[1, k],
            device_id={"seq": lax.rem(self.ring.x + k, self.seq_size)},
            device_id_type=MESH,
        )

    def crossed(self):
        for k in range(1, self.seq_size):
            self.across(k).wait_recv()

    def groups(self):
        unit = self.unit
        found = [[self.crossed, unit.own], [functools.partial(unit.relay, 1)]]
        for step in range(2, unit.steps + 1):
            found.append([functools.partial(unit.relay, step), functools.partial(unit.relay_seq, step - 1)])
        return found + [[functools.partial(unit.relay_seq, unit.steps)]]

    def drain(self):
        self.unit.drain()
        for k in range(1, self.seq_size):
            self.across(k).wait_send()


def share_out(groups, ticks):
    cuts = [len(groups) * k // ticks for k in range(ticks + 1)]
    return [sum(groups[cuts[k] : cuts[k + 1]], []) for k in range(ticks)]


def front_kernel(sizes, per_sequence, shares, *refs):
    (
        block_in, cotangent, ids, taps_in, gain_first_in, gain_second_in,
        in_first, in_second, out_first, out_second, gate_first, up_first, down_second,
        gate_second, up_second, down_first, in_own, out_own, gate_own, up_own, down_own,
    ) = refs[:21]
    (
        grad_second, grads, low_in, low_out, in_first_s, in_second_s, out_first_s, out_second_s, pick_t,
        block_out, after_out, mixed_out, conv_out, mixer_out, normed_out, in_all, out_all, gu_all, down_all,
        grad_mixer_out, got_front, got_rest, got_out, picks,
    ) = refs[21:45]
    sems, local_sem, load_sem, stage_sem, rim_sem, out_sem = refs[45:49], refs[49], refs[50], refs[51], refs[52], refs[53]
    exchange_sems = refs[54:59]
    held = refs[59:64]
    pick, taps, gain_first, gain_second, out_grads, out_tiles = refs[-6:]
    (
        total, wide, gate_w, up_w, down_w, normed, mixer, second, gate_up_first, first_down, second_gu, second_down,
        low_gu, grad_low_down, low_down, grad_low_gu, partial, rim_out, rim_in,
    ) = refs[64:-6]
    fsdp_size, seq_size = sizes
    ring = Ring(fsdp_size)
    rows, down_rows = gate_own.shape[0], down_own.shape[0]
    tokens, features = cotangent.shape
    hidden_size = gate_own.shape[1]
    chunks = hidden_size // FF_CHUNK
    sequences = tokens // per_sequence
    block = min(ROW_BLOCK, per_sequence)
    wide_block = min(WIDE_BLOCK, tokens)
    blocks, wide_blocks = tokens // block, tokens // wide_block
    slots = low_in.shape[1]
    mine = pl.ds(ring.me * rows, rows)
    moved = move_in(
        [
            (in_own, held[0], in_all.at[mine, :]),
            (out_own, held[1], out_all.at[mine, :]),
            (down_own, held[4], down_all.at[pl.ds(ring.me * down_rows, down_rows), :]),
            (gate_own, held[2], gu_all.at[0, mine, :]),
            (up_own, held[3], gu_all.at[1, mine, :]),
        ],
        local_sem,
    )
    stages = []
    for k in range(-(-hidden_size // features)):
        width = min(features, hidden_size - k * features)
        part, lanes = pl.ds(k * features, width), pl.ds(k * LANES, LANES)
        stages += [
            (gate_second.at[:, part], second.at[lanes, pl.ds(0, width)]),
            (up_second.at[:, part], normed.at[lanes, pl.ds(0, width)]),
            (down_first.at[part, :], mixer.at[pl.ds(0, width), lanes]),
        ]
    stages = [pltpu.make_async_copy(a, b, stage_sem.at[k]) for k, (a, b) in enumerate(stages)]
    for copy in stages:
        copy.start()
    devices = fsdp_size * seq_size
    ring.greet(seq_size, devices)

    part = in_all.shape[1] // 3
    out_x = 3 * features // 8
    unit_list, sizes_of = [], []

    def add_unit(spot, shared, common):
        unit_list.append(Unit(ring, len(unit_list), spot, sems))
        sizes_of.append((2 * shared, 2 * common))

    for k in range(2):
        add_unit(functools.partial(in_spot, in_all, rows, part, k), rows * part // 2, rows * part // 2)
    last_out = features - 2 * out_x
    add_unit(functools.partial(column_spot, out_all, rows, out_x, last_out), rows * out_x, rows * last_out)
    pieces = down_pieces(down_rows)
    for k in range(pieces):
        size = down_rows // pieces // 3
        add_unit(functools.partial(row_spot, down_all, down_rows, 3 * size * k, size), size * features, size * features)
    fixed = len(unit_list)
    comm_chunks = 2 * chunks // 3
    comm_size = hidden_size // comm_chunks // 3
    for k in range(comm_chunks):
        add_unit(functools.partial(chunk_spot, gu_all, rows, comm_size, k), 2 * rows * comm_size, 2 * rows * comm_size)
    plan = Plan(unit_list, sizes_of)

    def run_all(actions):
        for action in actions:
            action()

    for copy in moved:
        copy.wait()
    run_all(plan.tick(5.0))
    sequence_row = lax.broadcasted_iota(jnp.int32, (slots, LANES), 0)
    sequence_column = lax.broadcasted_iota(jnp.int32, (LANES, slots), 1)
    wanted_row, wanted_column = lax.rem(sequence_row, R), lax.rem(sequence_column, R)
    for k in range(sequences):
        base = ids[k] * R
        wanted_row += jnp.where(sequence_row // R == k, base, 0)
        wanted_column += jnp.where(sequence_column // R == k, base, 0)
    pick_t[...] = (wanted_row == lax.broadcasted_iota(jnp.int32, (slots, LANES), 1)).astype(F32).astype(BF16)
    pick[...] = (wanted_column == lax.broadcasted_iota(jnp.int32, (LANES, slots), 0)).astype(F32).astype(BF16)
    taps[...] = taps_in[...].astype(F32)
    gain_first[...] = gain_first_in[...].astype(F32)
    gain_second[...] = gain_second_in[...].astype(F32)

    def rows_of(r, size=block):
        return pl.ds(pl.multiple_of(r * size, size), size)

    def masked(r, values, size=block):
        row = r * size + lax.broadcasted_iota(jnp.int32, (size, slots), 0)
        column = lax.broadcasted_iota(jnp.int32, (size, slots), 1)
        return jnp.where(row // per_sequence == column // R, ADAPTER_SCALE * values, 0.0).astype(BF16)

    for copy in stages:
        copy.wait()
    for k in range(-(-hidden_size // features)):
        width = min(features, hidden_size - k * features)
        at, lanes = slice(k * features, k * features + width), slice(k * LANES, (k + 1) * LANES)
        second_gu[0, :, at] = dot_nn(pick_t[...], second[lanes, :width]).astype(BF16)
        second_gu[1, :, at] = dot_nn(pick_t[...], normed[lanes, :width]).astype(BF16)
        first_down[at, :] = dot_nn(mixer[:width, lanes], pick[...]).astype(BF16)
    second_down[...] = dot_nn(pick_t[...], down_second[...]).astype(BF16)
    in_second_s[...] = dot_nn(pick_t[...], in_second[...]).astype(BF16)
    out_second_s[...] = dot_nn(pick_t[...], out_second[...]).astype(BF16)
    in_first_s[...] = dot_nn(in_first[...], pick[...]).astype(BF16)
    out_first_s[...] = dot_nn(out_first[...], pick[...]).astype(BF16)
    gate_up_first[0] = dot_nn(gate_first[...], pick[...]).astype(BF16)
    gate_up_first[1] = dot_nn(up_first[...], pick[...]).astype(BF16)
    lists = [plan.tick(0.9) for _ in range(blocks)]

    @pl.loop(0, blocks)
    def _(r):
        run_tick(lists, r)
        at = rows_of(r)
        normed_rows = (rms_unit(block_in[at, :].astype(F32))[1] * gain_first[...]).astype(BF16)
        normed[at, :] = normed_rows
        low_in[at, :] = masked(r, dot_nn(normed_rows, in_first_s[...]))
        grad_low_down[at, :] = masked(r, dot_nt(cotangent[at, :], second_down[...]))
        grad_second[at, :] = jnp.zeros((block, features), F32)

    low_down[...] = jnp.zeros_like(low_down)
    grad_low_gu[...] = jnp.zeros_like(grad_low_gu)
    plan.need((0, 1))
    run_all(plan.take())

    half = FF_CHUNK
    middle, last_part, conv_part = (slice(k * features, (k + 1) * features) for k in (1, 2, 3))
    in_loads = []
    for k in range(2):
        for part_number, buffer in ((0, gate_w), (1, up_w)):
            columns = pl.ds(part_number * features + k * half, half)
            in_loads.append(pltpu.make_async_copy(in_all.at[:, columns], buffer.at[k], load_sem.at[k, part_number]))
        place = in_all.at[pl.ds(k * half, half), pl.ds(2 * features, features)]
        in_loads.append(pltpu.make_async_copy(place, down_w.at[k], load_sem.at[k, 2]))
    for copy in in_loads:
        copy.start()
    run_all(plan.tick(2.0))
    for copy in in_loads:
        copy.wait()
    lists = [plan.tick(1.6) for _ in range(blocks)]

    @pl.loop(0, blocks)
    def _(r):
        run_tick(lists, r)
        at = rows_of(r)
        values, low = normed[at, :], low_in[at, :]
        for part_number, buffer in ((0, gate_w), (1, up_w)):
            for k in range(2):
                start = part_number * features + k * half
                columns = slice(start, start + half)
                wide[at, columns] = dot_nn(values, buffer[k]) + dot_nn(low, in_second_s[:, columns])
        wide[at, last_part] = (
            dot_nn(values[:, :half], down_w[0])
            + dot_nn(values[:, half:], down_w[1])
            + dot_nn(low, in_second_s[:, last_part])
        )

    plan.need((2,))
    run_all(plan.take())
    out_loads = [
        pltpu.make_async_copy(out_all.at[:, pl.ds(k * half, half)], gate_w.at[k], load_sem.at[k, 0]) for k in range(2)
    ]
    for copy in out_loads:
        copy.start()
    for k in range(sequences):
        at = slice((k + 1) * per_sequence - 8, (k + 1) * per_sequence)
        rim_out[k] = wide[at, :features] * wide[at, last_part]
    rim = pltpu.make_async_remote_copy(
        src_ref=rim_out,
        dst_ref=rim_in,
        send_sem=rim_sem.at[0],
        recv_sem=rim_sem.at[1],
        device_id={"seq": lax.rem(ring.x + 1, seq_size)},
        device_id_type=MESH,
    )
    rim.start()
    mixed_store = pltpu.make_async_copy(wide.at[:, pl.ds(0, 3 * features)], mixed_out, out_sem.at[0])
    mixed_store.start()
    normed_store = pltpu.make_async_copy(normed.at[pl.ds(0, tokens), :], normed_out, out_sem.at[1])
    normed_store.start()
    run_all(plan.tick(2.0))
    for copy in out_loads:
        copy.wait()
    rim.wait_recv()
    inner = (ring.x > 0).astype(F32)
    lists = [plan.tick(2.2) for _ in range(blocks)]

    @pl.loop(0, blocks)
    def _(r):
        run_tick(lists, r)
        at = rows_of(r)
        gated = wide[at, :features] * wide[at, last_part]
        before_at = pl.ds(pl.multiple_of(jnp.maximum(r * block - 8, 0), 8), 8)
        before = wide[before_at, :features] * wide[before_at, last_part]
        first = lax.rem(r * block, per_sequence) == 0
        before = jnp.where(first, rim_in[(r * block) // per_sequence] * inner, before)
        extended = jnp.concatenate([before, gated], axis=0)
        convolved = (
            taps[0:1, :] * extended[6 : block + 6] + taps[1:2, :] * extended[7 : block + 7] + taps[2:3, :] * gated
        )
        wide[at, conv_part] = convolved
        mixed = (wide[at, middle] * convolved).astype(BF16)
        mixer[at, :] = mixed
        low = masked(r, dot_nn(mixed, out_first_s[...]))
        low_out[at, :] = low
        branch = jnp.concatenate([dot_nn(mixed, gate_w[0]), dot_nn(mixed, gate_w[1])], axis=1)
        after = block_in[at, :].astype(F32) + (branch + dot_nn(low, out_second_s[...]))
        total[at, :] = after
        second_rows = (rms_unit(after)[1] * gain_second[...]).astype(BF16)
        second[at, :] = second_rows
        for k in range(2):
            low_gu[k, at, :] = masked(r, dot_nn(second_rows, gate_up_first[k]))

    stores = [
        pltpu.make_async_copy(wide.at[:, pl.ds(3 * features, features)], conv_out, out_sem.at[2]),
        pltpu.make_async_copy(mixer.at[pl.ds(0, tokens), :], mixer_out, out_sem.at[3]),
        pltpu.make_async_copy(total, after_out, out_sem.at[4]),
    ]
    for copy in stores:
        copy.start()
    plan.need(range(3, fixed))
    run_all(plan.take())

    def down_load(j, s):
        return pltpu.make_async_copy(down_all.at[rows_of(j, FF_CHUNK), :], down_w.at[s], load_sem.at[s, 2])

    def gu_loads(j, s):
        place = rows_of(j, FF_CHUNK)
        return (
            pltpu.make_async_copy(gu_all.at[0, :, place], gate_w.at[s], load_sem.at[s, 0]),
            pltpu.make_async_copy(gu_all.at[1, :, place], up_w.at[s], load_sem.at[s, 1]),
        )

    down_load(0, 0).start()
    mixed_store.wait()
    for copy in stores:
        copy.wait()
    lists = [plan.tick(1.7) for _ in range(chunks)]

    @pl.loop(0, chunks)
    def _(j):
        s = lax.rem(j, 2)

        @pl.when(j + 1 < chunks)
        def _():
            down_load(j + 1, 1 - s).start()

        down_load(j, s).wait()
        run_tick(lists, j)
        columns = rows_of(j, FF_CHUNK)

        @pl.loop(0, wide_blocks)
        def _(r):
            at = rows_of(r, wide_block)
            wide[at, columns] = dot_nt(cotangent[at, :], down_w[s]) + dot_nt(
                grad_low_down[at, :], first_down[columns, :]
            )

    def begin(j):
        for copy in (down_load(j, j % 2),) + gu_loads(j, j % 2):
            copy.start()

    def units_of(j):
        first, last = j * FF_CHUNK // (3 * comm_size), (j * FF_CHUNK + FF_CHUNK - 1) // (3 * comm_size)
        return range(fixed + first, fixed + last + 1)

    plan.need(units_of(0))
    plan.list.append(functools.partial(begin, 0))
    run_all(plan.tick(1.0))

    def tile_columns(start):
        return lambda d: column_tiles(grads, start, 1, shares.used, d, devices)

    sources = [tile_columns(k * shares.pitch) for k in range(2)]
    sources.append(
        lambda d: column_tiles(grads, shares.rest_start, shares.per, shares.rest_used, d, devices)
    )
    sources.append(lambda d: column_tiles(out_tiles, 0, 1, shares.left + 2 * shares.narrow, d, devices))
    sources.append(lambda d: pick_t)
    places = (got_front.at[0], got_front.at[1], got_rest, got_out, picks)
    exchanges = [
        Exchange(ring, seq_size, devices, source, place, exchange_sems[k])
        for k, (source, place) in enumerate(zip(sources, places))
    ]
    spare_slot = chunks % 2
    back_loads = [
        pltpu.make_async_copy(out_all.at[:, pl.ds(k * half, half)], buffer.at[spare_slot], load_sem.at[2, k])
        for k, buffer in enumerate((gate_w, up_w))
    ]
    back_loads.append(pltpu.make_async_copy(after_out, wide.at[:, pl.ds(0, features)], load_sem.at[2, 2]))

    def load_back():
        for copy in back_loads:
            copy.start()

    lists, begun = [], 0
    for tick in range(chunks * wide_blocks):
        j = tick // wide_blocks
        plan.pump()
        if begun == j and j + 1 < chunks:
            possible = all(u in plan.collected or plan.can_collect(u) for u in units_of(j + 1))
            if possible or (tick + 1) % wide_blocks == 0:
                plan.need(units_of(j + 1))
                plan.list.append(functools.partial(begin, j + 1))
                begun += 1
        if tick == (chunks - 2) * wide_blocks:
            plan.list += [exchanges[0].start, exchanges[4].start]
        if tick == (chunks - 1) * wide_blocks:
            plan.list += [load_back, exchanges[1].start]
        lists.append(plan.tick(3.9))

    @pl.loop(0, chunks * wide_blocks)
    def _(tick):
        j, r = tick // wide_blocks, lax.rem(tick, wide_blocks)
        s = lax.rem(j, 2)
        columns = rows_of(j, FF_CHUNK)

        @pl.when(r == 0)
        def _():
            for copy in (down_load(j, s),) + gu_loads(j, s):
                copy.wait()
            partial[...] = jnp.zeros_like(partial)

        run_tick(lists, tick)
        at = rows_of(r, wide_block)
        values = second[at, :]
        lows = (grad_low_down[at, :], low_gu[0, at, :], low_gu[1, at, :])
        gate = dot_nn(values, gate_w[s]) + dot_nn(lows[1], second_gu[0, :, columns])
        up = dot_nn(values, up_w[s]) + dot_nn(lows[2], second_gu[1, :, columns])
        back = wide[at, columns]
        sigmoid = 1.0 / (1.0 + jnp.exp(-gate))
        active = gate * sigmoid
        hidden = (active * up).astype(BF16)
        grad_gate = (back * up * (sigmoid + active * (1.0 - sigmoid))).astype(BF16)
        grad_up = (back * active).astype(BF16)
        total[at, :] += dot_nn(hidden, down_w[s])
        grad_second[at, :] += dot_nt(grad_gate, gate_w[s]) + dot_nt(grad_up, up_w[s])
        low_down[at, :] += dot_nn(hidden, first_down[columns, :])
        grad_low_gu[0, at, :] += dot_nt(grad_gate, second_gu[0, :, columns])
        grad_low_gu[1, at, :] += dot_nt(grad_up, second_gu[1, :, columns])
        for k, right in enumerate((hidden, grad_gate, grad_up)):
            partial[k] += dot_tn(lows[k], right)

        @pl.when(r == wide_blocks - 1)
        def _():
            for k in range(3):
                start = (j // 3) * shares.pitch + lax.rem(j, 3) * shares.per_chunk + k * shares.chunk
                place = pl.ds(pl.multiple_of(start * LANES, LANES), FF_CHUNK)
                grads[:, place] = partial[k].astype(BF16)

    normed_store.wait()
    rest_tiles = shares.rest_start + 3 * shares.per_chunk
    base = rest_tiles * LANES

    @pl.loop(0, blocks)
    def _(r):
        at = rows_of(r)
        low = masked(r, low_down[at, :])
        grad_low_down[at, :] = low
        normed[at, :] = (total[at, :] + dot_nn(low, second_down[...])).astype(BF16)
        for k in range(2):
            back_low = masked(r, grad_low_gu[k, at, :])
            low_gu[k, at, :] = back_low
            grad_second[at, :] += dot_nt(back_low, gate_up_first[k])

    block_store = pltpu.make_async_copy(normed.at[pl.ds(0, tokens), :], block_out, out_sem.at[1])
    block_store.start()
    grads[:, base + 2 * features : base + 3 * features] = dot_tn(grad_low_down[...], cotangent[...]).astype(BF16)
    for k in range(2):
        columns = slice(base + k * features, base + (k + 1) * features)
        grads[:, columns] = dot_tn(low_gu[k], second[:tokens, :]).astype(BF16)
    start = base + 3 * features
    for k in range(2):
        width = len(shares.spare[k]) * LANES
        if width:
            spare = (k * shares.pitch + shares.used) * LANES
            grads[:, start : start + width] = grads[:, spare : spare + width]
            start += width
    exchanges[2].start()

    for copy in back_loads:
        copy.wait()
    out_grads[...] = jnp.zeros_like(out_grads)

    @pl.loop(0, blocks)
    def _(r):
        at = rows_of(r)
        inverse, unit_rows = rms_unit(wide[at, :features])
        gradient = cotangent[at, :].astype(F32) + rms_back(
            grad_second[at, :] * gain_second[...], inverse, unit_rows
        )
        grad_second[at, :] = gradient
        rounded = gradient.astype(BF16)
        back_low = masked(r, dot_nt(rounded, out_second_s[...]))
        total[at, :] = (
            dot_nt(rounded[:, :half], gate_w[spare_slot])
            + dot_nt(rounded[:, half:], up_w[spare_slot])
            + dot_nt(back_low, out_first_s[...])
        )
        out_grads[0] += dot_tn(back_low, mixer[at, :])
        out_grads[1] += dot_tn(low_out[at, :], rounded)

    mixer_store = pltpu.make_async_copy(total, grad_mixer_out, out_sem.at[0])
    mixer_store.start()
    if shares.left:
        start = (shares.rest_start + shares.rest_used) * LANES
        out_tiles[:, : shares.left * LANES] = grads[:, start : start + shares.left * LANES]
    for k in range(2):
        start = shares.left * LANES + k * features
        out_tiles[:, start : start + features] = out_grads[k].astype(BF16)
    exchanges[3].start()
    for unit in unit_list[:fixed]:
        unit.drain()

    @pl.loop(0, comm_chunks)
    def _(k):
        Unit(ring, fixed + k, functools.partial(chunk_spot, gu_all, rows, comm_size, k), sems).drain()

    rim.wait_send()
    block_store.wait()
    mixer_store.wait()
    for member in exchanges:
        member.arrived()
    for member in exchanges:
        member.drain()


def front(sizes, per_sequence, shares, operands):
    fsdp_size, seq_size = sizes
    cotangent, ids = operands[1:3]
    own = operands[-5:]
    tokens, features = cotangent.shape
    hidden_size = own[2].shape[1]
    sequences = ids.shape[0]
    slots = sequences * R
    units = 3 + down_pieces(own[4].shape[0]) + 2 * (hidden_size // FF_CHUNK) // 3
    tall = max(tokens, features)
    stages = 3 * -(-hidden_size // features)

    def shape(*dims, kind=BF16):
        return jax.ShapeDtypeStruct(dims, kind)

    return pl.pallas_call(
        functools.partial(front_kernel, sizes, per_sequence, shares),
        out_shape=(
            shape(tokens, features, kind=F32),
            shape(slots, shares.grads_width),
            shape(tokens, slots),
            shape(tokens, slots),
            shape(features, slots),
            shape(slots, 3 * features),
            shape(features, slots),
            shape(slots, features),
            shape(slots, LANES),
            shape(tokens, features),
            shape(tokens, features, kind=F32),
            shape(tokens, 3 * features, kind=F32),
            shape(tokens, features, kind=F32),
            shape(tokens, features),
            shape(tokens, features),
            shape(features, 3 * features),
            shape(features, features),
            shape(2, features, hidden_size),
            shape(hidden_size, features),
            shape(tokens, features, kind=F32),
            shape(2, shares.devices, slots, LANES),
            shape(shares.devices, slots, shares.per * LANES),
            shape(shares.devices, slots, LANES),
            shape(shares.devices, slots, LANES),
        ),
        in_specs=[IN_VMEM] * 2 + [pl.BlockSpec(memory_space=pltpu.SMEM)] + [IN_VMEM] * 10 + [ANYWHERE] * 8,
        out_specs=(IN_VMEM,) * 9 + (ANYWHERE,) * 15,
        scratch_shapes=unit_sems(units, fsdp_size // 2)
        + [
            pltpu.SemaphoreType.DMA((2, 5)),
            pltpu.SemaphoreType.DMA((3, 3)),
            pltpu.SemaphoreType.DMA((stages,)),
            pltpu.SemaphoreType.DMA((2,)),
            pltpu.SemaphoreType.DMA((5,)),
        ]
        + [pltpu.SemaphoreType.DMA((3,))] * 5
        + [pltpu.VMEM(member.shape, BF16) for member in own]
        + [
            pltpu.VMEM((tokens, features), F32),
            pltpu.VMEM((tokens, hidden_size), F32),
            pltpu.VMEM((2, features, FF_CHUNK), BF16),
            pltpu.VMEM((2, features, FF_CHUNK), BF16),
            pltpu.VMEM((2, FF_CHUNK, features), BF16),
            pltpu.VMEM((tall, features), BF16),
            pltpu.VMEM((tall, features), BF16),
            pltpu.VMEM((tall, features), BF16),
            pltpu.VMEM((2, features, slots), BF16),
            pltpu.VMEM((hidden_size, slots), BF16),
            pltpu.VMEM((2, slots, hidden_size), BF16),
            pltpu.VMEM((slots, features), BF16),
            pltpu.VMEM((2, tokens, slots), BF16),
            pltpu.VMEM((tokens, slots), BF16),
            pltpu.VMEM((tokens, slots), F32),
            pltpu.VMEM((2, tokens, slots), F32),
            pltpu.VMEM((3, slots, FF_CHUNK), F32),
            pltpu.VMEM((sequences, 8, features), F32),
            pltpu.VMEM((sequences, 8, features), F32),
            pltpu.VMEM((LANES, slots), BF16),
            pltpu.VMEM((3, features), F32),
            pltpu.VMEM((1, features), F32),
            pltpu.VMEM((1, features), F32),
            pltpu.VMEM((2, slots, features), F32),
            pltpu.VMEM((slots, (shares.left + 2 * shares.narrow) * LANES), BF16),
        ],
        compiler_params=pltpu.CompilerParams(
            collective_id=0, has_side_effects=True, vmem_limit_bytes=VMEM_LIMIT_FRONT
        ),
    )(*operands)


def mixer_back_kernel(sizes, per_sequence, shares, *refs):
    (
        grad_after_in, grad_mixer_in, block_in_in, mixed, conv, normed_in, weight_in, low_in, in_first, in_second,
        taps_in, gain_first_in, got_front, got_rest, got_out, picks,
    ) = refs[:16]
    grad_input = refs[16]
    landings = refs[17:19]
    units_refs = refs[19:23]
    exchange_sem, seq_sems, local_sems = refs[23], refs[24:26], refs[26:28]
    rim_sem, load_sem = refs[28:30]
    got_in, results = refs[30], refs[31:33]
    (
        rim_out, rim_in, grad_after, mixed_s, conv_s, in_w, grad_mixer, grad_mixed,
        low_in_back, in_tiles, block_in, normed, taps, gain_first,
    ) = refs[33:]
    fsdp_size, seq_size = sizes
    devices = fsdp_size * seq_size
    ring = Ring(fsdp_size)
    me = ring.me * seq_size + ring.x
    tokens, features = grad_mixer.shape
    slots = low_in.shape[1]
    sequences = tokens // per_sequence
    block = min(ROW_BLOCK, per_sequence)
    loads = [
        pltpu.make_async_copy(a, b, load_sem.at[k])
        for k, (a, b) in enumerate(
            (
                (grad_mixer_in, grad_mixer),
                (mixed, mixed_s),
                (conv, conv_s),
                (normed_in, normed),
                (weight_in, in_w),
                (block_in_in, block_in),
                (grad_after_in, grad_after),
            )
        )
    ]
    for copy in loads[:3]:
        copy.start()
    ring.greet(seq_size, devices)
    in_exchange = Exchange(
        ring, seq_size, devices, lambda d: column_tiles(in_tiles, 0, 1, 4 * shares.narrow, d, devices), got_in,
        exchange_sem,
    )
    total_slots = devices * slots
    per = shares.per

    def front_got(t):
        if t < 2:
            return got_front[t].reshape(total_slots, LANES)
        return got_rest[:, :, (t - 2) * LANES : (t - 1) * LANES].reshape(total_slots, LANES)

    def front_first(t):
        return shares.is_first(t, me) if t < 2 else shares.is_first(2, me * per + t - 2)

    def back_got(t):
        return (got_out, got_in)[t][...].reshape(total_slots, LANES)

    sums = [
        Sum(ring, seq_size, k, landings[k], is_first, got, results[k], (seq_sems[k], local_sems[k]), units_refs)
        for k, (got, is_first) in enumerate(
            ((front_got, front_first), (back_got, lambda t: shares.is_first(3 + t, me)))
        )
    ]
    chosen = picks[...].reshape(total_slots, LANES)
    sums[0].add(chosen)
    taps[...] = taps_in[...].astype(F32)
    gain_first[...] = gain_first_in[...].astype(F32)
    parts = tokens // block
    groups = sums[0].groups()
    while len(groups) < 2 * parts - 1:
        groups.append([])

    def rows_of(r):
        return pl.ds(pl.multiple_of(r * block, block), block)

    def masked(r, values):
        row = r * block + lax.broadcasted_iota(jnp.int32, (block, slots), 0)
        column = lax.broadcasted_iota(jnp.int32, (block, slots), 1)
        return jnp.where(row // per_sequence == column // R, ADAPTER_SCALE * values, 0.0).astype(BF16)

    for copy in loads[:3]:
        copy.wait()
    for copy in loads[3:]:
        copy.start()
    middle = slice(features, 2 * features)
    for k in range(sequences):
        at = slice(k * per_sequence, k * per_sequence + 8)
        rim_out[k] = grad_mixer[at, :] * mixed_s[at, middle]
    rim = pltpu.make_async_remote_copy(
        src_ref=rim_out,
        dst_ref=rim_in,
        send_sem=rim_sem.at[0],
        recv_sem=rim_sem.at[1],
        device_id={"seq": lax.rem(ring.x + seq_size - 1, seq_size)},
        device_id_type=MESH,
    )
    rim.start()
    rim.wait_recv()
    inner = (ring.x < seq_size - 1).astype(F32)

    first_lists = share_out(groups[: parts - 1], parts - 1)

    @pl.loop(0, parts)
    def _(r):
        run_tick([[]] + first_lists, r)
        at = rows_of(r)
        back = grad_mixer[at, :]
        through = back * mixed_s[at, middle]
        after_at = pl.ds(pl.multiple_of(jnp.minimum((r + 1) * block, tokens - 8), 8), 8)
        beyond = grad_mixer[after_at, :] * mixed_s[after_at, middle]
        last = lax.rem((r + 1) * block, per_sequence) == 0
        beyond = jnp.where(last, rim_in[(r * block) // per_sequence] * inner, beyond)
        extended = jnp.concatenate([through, beyond], axis=0)
        gated = (
            taps[2:3, :] * through + taps[1:2, :] * extended[1 : block + 1] + taps[0:1, :] * extended[2 : block + 2]
        )
        grad_mixed[at, :features] = (gated * mixed_s[at, 2 * features :]).astype(BF16)
        grad_mixed[at, middle] = (back * conv_s[at, :]).astype(BF16)
        grad_mixed[at, 2 * features :] = (gated * mixed_s[at, :features]).astype(BF16)
        low_in_back[at, :] = masked(r, dot_nt(grad_mixed[at, :], in_second[...]))

    for copy in loads[3:]:
        copy.wait()
    in_tiles[:, features : 4 * features] = dot_tn(low_in[...], grad_mixed[...]).astype(BF16)
    in_tiles[:, :features] = dot_tn(low_in_back[...], normed[...]).astype(BF16)
    in_exchange.start()

    def finish(r):
        at = rows_of(r)
        rows = block_in[at, :].astype(F32)
        inverse = lax.rsqrt(jnp.mean(rows * rows, axis=-1, keepdims=True) + EPSILON)
        unit_rows = rows * inverse
        gradient = dot_nt(grad_mixed[at, :], in_w[...]) + dot_nt(low_in_back[at, :], in_first[...])
        scaled = gradient * gain_first[...]
        grad_input[at, :] = (
            grad_after[at, :]
            + inverse * (scaled - unit_rows * jnp.mean(scaled * unit_rows, axis=-1, keepdims=True))
        ).astype(BF16)

    def add_last():
        in_exchange.arrived()
        sums[1].add(chosen)

    rest = share_out(groups[parts - 1 :], parts)
    rest[-1] = rest[-1] + [add_last]

    @pl.loop(0, parts)
    def _(r):
        run_tick(rest, r)
        finish(r)

    for actions in sums[1].groups():
        for action in actions:
            action()
    for member in sums:
        member.unit.collect()
    for member in sums:
        member.drain()
    in_exchange.drain()
    rim.wait_send()


def mixer_back(sizes, per_sequence, shares, operands):
    fsdp_size, seq_size = sizes
    devices = fsdp_size * seq_size
    tokens, features = operands[0].shape
    slots = operands[7].shape[1]
    sequences = tokens // per_sequence
    tiles = (2 + shares.per, 2)
    return pl.pallas_call(
        functools.partial(mixer_back_kernel, sizes, per_sequence, shares),
        out_shape=(jax.ShapeDtypeStruct((tokens, features), BF16),)
        + tuple(jax.ShapeDtypeStruct((fsdp_size, seq_size, count, LANES, LANES), BF16) for count in tiles),
        in_specs=[ANYWHERE] * 7 + [IN_VMEM] * 9,
        out_specs=(IN_VMEM,) + (ANYWHERE,) * 2,
        scratch_shapes=unit_sems(2, fsdp_size // 2)
        + [pltpu.SemaphoreType.DMA((3,))]
        + [pltpu.SemaphoreType.DMA((2, seq_size))] * 2
        + [pltpu.SemaphoreType.DMA((1,))] * 2
        + [
            pltpu.SemaphoreType.DMA((2,)),
            pltpu.SemaphoreType.DMA((7,)),
            pltpu.VMEM((devices, slots, LANES), BF16),
        ]
        + [pltpu.VMEM((count, LANES, LANES), BF16) for count in tiles]
        + [
            pltpu.VMEM((sequences, 8, features), F32),
            pltpu.VMEM((sequences, 8, features), F32),
            pltpu.VMEM((tokens, features), F32),
            pltpu.VMEM((tokens, 3 * features), F32),
            pltpu.VMEM((tokens, features), F32),
            pltpu.VMEM((features, 3 * features), BF16),
            pltpu.VMEM((tokens, features), F32),
            pltpu.VMEM((tokens, 3 * features), BF16),
            pltpu.VMEM((tokens, slots), BF16),
            pltpu.VMEM((slots, 4 * shares.narrow * LANES), BF16),
            pltpu.VMEM((tokens, features), BF16),
            pltpu.VMEM((tokens, features), BF16),
            pltpu.VMEM((3, features), F32),
            pltpu.VMEM((1, features), F32),
        ],
        compiler_params=pltpu.CompilerParams(
            collective_id=2, has_side_effects=True, vmem_limit_bytes=VMEM_LIMIT_FRONT
        ),
    )(*operands)


def spread_kernel(layout, *refs):
    sources, outs = refs[:2], refs[2:]
    for out, (first, runs) in zip(outs, layout):
        for source, start, stride, offset, count in runs:

            @pl.loop(0, count)
            def _(k, source=sources[source], start=start, stride=stride, offset=offset, out=out, first=first):
                at = pl.ds(pl.multiple_of((offset + k) * LANES, LANES), LANES)
                tile = source[start + k * stride].astype(F32)
                if first:
                    out[at, :] = tile
                else:
                    out[:, at] = tile


def spread(shares, landings):
    wide, narrow = shares.wide, shares.narrow
    places = shares.places()
    layout, shapes = [], []
    for name, count in (
        ("in_first", narrow),
        ("in_second", 3 * narrow),
        ("out_first", narrow),
        ("out_second", narrow),
        ("gate_first", narrow),
        ("gate_second", wide),
        ("up_first", narrow),
        ("up_second", wide),
        ("down_first", wide),
        ("down_second", narrow),
    ):
        runs, k = [], 0
        while k < count:
            source, start = places[(name, k)]
            stride, length = 1, 1
            if k + 1 < count and places[(name, k + 1)][0] == source:
                stride = places[(name, k + 1)][1] - start
            while k + length < count and places[(name, k + length)] == (source, start + length * stride):
                length += 1
            runs.append((source, start, stride, k, length))
            k += length
        first = name.endswith("first")
        layout.append((first, tuple(runs)))
        shapes.append(jax.ShapeDtypeStruct((count * LANES, LANES) if first else (LANES, count * LANES), F32))
    return pl.pallas_call(
        functools.partial(spread_kernel, tuple(layout)),
        out_shape=tuple(shapes),
        in_specs=[IN_VMEM] * 2,
        out_specs=(IN_VMEM,) * len(shapes),
        compiler_params=pltpu.CompilerParams(vmem_limit_bytes=VMEM_LIMIT),
    )(*(landing.reshape(-1, LANES, LANES) for landing in landings))


def per_device(
    block_input,
    output_grad,
    adapter_ids,
    in_weight,
    out_weight,
    gate_weight,
    up_weight,
    down_weight,
    conv_weight,
    first_gain,
    second_gain,
    infirst_adapter,
    insecond_adapter,
    outfirst_adapter,
    outsecond_adapter,
    gatefirst_adapter,
    gatesecond_adapter,
    upfirst_adapter,
    upsecond_adapter,
    downfirst_adapter,
    downsecond_adapter,
):
    batches, seq_count, local_len, features = block_input.shape
    sequences = batches * seq_count
    tokens = sequences * local_len
    fsdp_size, seq_size = lax.axis_size("fsdp"), lax.axis_size("seq")
    hidden_size = gate_weight.shape[1]
    shares = Shares(fsdp_size * seq_size, features, hidden_size)
    gain_first, gain_second = first_gain[None, :], second_gain[None, :]
    cotangent = output_grad.reshape(tokens, features)
    block_in = block_input.reshape(tokens, features)
    (
        grad_after, _, low_in, _, in_first, in_second, _, _, _,
        block_output, _, mixed_in, conv_out, _, normed, weight_in, _, _, _,
        grad_mixer, got_front, got_rest, got_out, picks,
    ) = front(
        (fsdp_size, seq_size),
        local_len,
        shares,
        (
            block_in,
            cotangent,
            adapter_ids.reshape(sequences),
            conv_weight,
            gain_first,
            gain_second,
            infirst_adapter,
            insecond_adapter,
            outfirst_adapter,
            outsecond_adapter,
            gatefirst_adapter,
            upfirst_adapter,
            downsecond_adapter,
            gatesecond_adapter,
            upsecond_adapter,
            downfirst_adapter,
            in_weight,
            out_weight,
            gate_weight,
            up_weight,
            down_weight,
        ),
    )
    grad_input, *landings = mixer_back(
        (fsdp_size, seq_size),
        local_len,
        shares,
        (
            grad_after,
            grad_mixer,
            block_in,
            mixed_in,
            conv_out,
            normed,
            weight_in,
            low_in,
            in_first,
            in_second,
            conv_weight,
            gain_first,
            got_front,
            got_rest,
            got_out,
            picks,
        ),
    )
    shape = block_input.shape
    return (block_output.reshape(shape), grad_input.reshape(shape)) + tuple(spread(shares, landings))


def solution(mesh):
    return jax.shard_map(
        per_device,
        mesh=mesh,
        in_specs=(
            P(None, "fsdp", "seq", None),
            P(None, "fsdp", "seq", None),
            P(None, "fsdp"),
            P("fsdp", None),
            P("fsdp", None),
            P("fsdp", None),
            P("fsdp", None),
            P("fsdp", None),
            P(),
            P(),
            P(),
            P(),
            P(),
            P(),
            P(),
            P(),
            P(),
            P(),
            P(),
            P(),
            P(),
        ),
        out_specs=(
            P(None, "fsdp", "seq", None),
            P(None, "fsdp", "seq", None),
            P(),
            P(),
            P(),
            P(),
            P(),
            P(),
            P(),
            P(),
            P(),
            P(),
        ),
        check_vma=False,
    )
```

time: 313 us -> 302 us (0.965)
  Pallas kernels: 301 us -> 294 us
  other arithmetic: 5.88 us -> 0 us
    pallas_call x1, Pallas kernels: 84 us -> 67.9 us  [mixer_back(): pl.pallas_call(functools.partial(mixer_back_kernel, sizes, per_sequence,...]
    pallas_call x2, Pallas kernels: 217 us -> 226 us  [the longest x1 218 us: front(): pl.pallas_call(functools.partial(front_kernel, sizes, per_sequence, share...]
where the time goes in v5:
time: 302 us
  Pallas kernels  294 us (97%)
  local copies, waits for them, and re-layouts  7.11 us (2%)
    pallas_call x1, Pallas kernels, front(): pl.pallas_call(functools.partial(front_kernel, sizes, per_sequence, share...  218 us
    pallas_call x1, Pallas kernels, mixer_back(): pl.pallas_call(functools.partial(mixer_back_kernel, sizes, per_sequence,...  67.9 us
    pallas_call x1, Pallas kernels, spread(): pl.pallas_call(functools.partial(spread_kernel, tuple(layout)), out_shape...  8.54 us

profile of v5, /device:TPU:0, one launch (start us, length us, event | category | flops | bytes accessed | tf_op | source)
XLA Modules:
  0.0 302.1 jit_solution(5658323944916614720)
XLA Ops:
  0.6 1.3 broadcast_in_dim.6.refs_4_.refs_11_
  1.9 1.3 broadcast_in_dim.7.refs_5_
  3.2 217.9 %shard_map.292 = (f32[1024,1024]{1,0:T(8,128)}, bf16[32,17920]{1,0:T(8,128)(2,1)}, bf16[1024,32]{1,0:T(8,128)(2,1)}, bf16[1024,32]{1,0:T(8,128)(2,1)}, bf16[1024...) custom-call(bf16[1024,1024]{1,0:T(8,128)(2,1)} %bitcast.11, ...), custom_call_target="tpu_custom_call" | custom-call | tf_op jit(solution)/shard_map/pallas_call | solution.py:982
  221.1 67.9 %shard_map.293 = (bf16[1024,1024]{1,0:T(8,128)(2,1)}, bf16[16,2,4,128,128]{4,3,2,1,0:T(8,128)(2,1)}, bf16[16,2,2,128,128]{4,3,2,1,0:T(8,128)(2,1)}) custom-call(f32[1024,1024]{1,0:T(8,128)} %get-tuple-element.40.refs_0_, f32[1024,1024]{1,0:T(8,128)} %get-tuple-element.41.refs_1_, bf16[1024,1024]{1,0:T(8,128)(2,1)} %bitcast.12, ...), custom_call_target="tpu_custom_call" | custom-call | tf_op jit(solution)/shard_map/pallas_call | solution.py:1225
  289.0 8.5 %shard_map.294 = (f32[1024,128]{1,0:T(8,128)}, f32[128,3072]{1,0:T(8,128)}, f32[1024,128]{1,0:T(8,128)}, f32[128,1024]{1,0:T(8,128)}, f32[1024,128]{1,0:T(8,128)...) custom-call(bf16[128,128,128]{2,1,0:T(8,128)(2,1)} %bitcast.13, ...), custom_call_target="tpu_custom_call" | custom-call | tf_op jit(solution)/shard_map/pallas_call | solution.py:1307
  297.5 0.0 copy-start
  297.5 3.2 %copy.37 = bf16[2,1,512,1024]{3,2,1,0:T(8,128)(2,1)} copy(bf16[2,1,512,1024]{3,2,1,0:T(8,128)(2,1)} %bitcast.16) | data formatting | bytes 4194304
  300.7 0.0 copy-done
  300.7 1.3 copy.38
Async XLA Ops:
  297.5 3.2 %copy-start = (bf16[1024,1024]{1,0:T(8,128)(2,1)S(1)}, bf16[1024,1024]{1,0:T(8,128)(2,1)}, u32[]{:S(2)}) copy-start(bf16[1024,1024]{1,0:T(8,128)(2,1)} %get-tuple-element.53) | copy-start | bytes 6291460

commit v6 on v5

--- a/solution.py
+++ b/solution.py
@@ -260,6 +260,12 @@
 
 def down_pieces(down_rows):
     return 3 if down_rows % 288 == 0 else 1
+
+
+def unroll_gain(out, rows):
+    values = rows[...].astype(F32)
+    for k in range(values.shape[0]):
+        out[:, k * LANES : (k + 1) * LANES] = values[k : k + 1, :]
 
 
 def in_spot(landing, rows, part, half, third, owner):
@@ -458,7 +464,7 @@
                 if number == 2:
                     found[tile] = (0, (2 + self.per) * (k // self.per) + 2 + k % self.per)
                 else:
-                    found[tile] = (0, (2 + self.per) * k + number) if number < 2 else (1, 2 * k + number - 3)
+                    found[tile] = (0, (2 + self.per) * k + number) if number < 2 else (number - 2, k)
         return found
 
 
@@ -525,23 +531,23 @@
 
 def front_kernel(sizes, per_sequence, shares, *refs):
     (
-        block_in, cotangent, ids, taps_in, gain_first_in, gain_second_in,
+        block_any, cotangent_any, ids, taps_in, gain_first_in, gain_second_in,
         in_first, in_second, out_first, out_second, gate_first, up_first, down_second,
         gate_second, up_second, down_first, in_own, out_own, gate_own, up_own, down_own,
     ) = refs[:21]
     (
         grad_second, grads, low_in, low_out, in_first_s, in_second_s, out_first_s, out_second_s, pick_t,
         block_out, after_out, mixed_out, conv_out, mixer_out, normed_out, in_all, out_all, gu_all, down_all,
-        grad_mixer_out, got_front, got_rest, got_out, picks,
+        grad_mixer_out, got_front, got_rest, out_tiles, picks,
     ) = refs[21:45]
     sems, local_sem, load_sem, stage_sem, rim_sem, out_sem = refs[45:49], refs[49], refs[50], refs[51], refs[52], refs[53]
-    exchange_sems = refs[54:59]
-    held = refs[59:64]
-    pick, taps, gain_first, gain_second, out_grads, out_tiles = refs[-6:]
+    exchange_sems = refs[54:58]
+    held = refs[58:63]
+    pick, taps, gain_first, gain_second, out_grads, block_in, cotangent, input_sem = refs[-8:]
     (
         total, wide, gate_w, up_w, down_w, normed, mixer, second, gate_up_first, first_down, second_gu, second_down,
         low_gu, grad_low_down, low_down, grad_low_gu, partial, rim_out, rim_in,
-    ) = refs[64:-6]
+    ) = refs[63:-8]
     fsdp_size, seq_size = sizes
     ring = Ring(fsdp_size)
     rows, down_rows = gate_own.shape[0], down_own.shape[0]
@@ -574,6 +580,8 @@
             (down_first.at[part, :], mixer.at[pl.ds(0, width), lanes]),
         ]
     stages = [pltpu.make_async_copy(a, b, stage_sem.at[k]) for k, (a, b) in enumerate(stages)]
+    stages.append(pltpu.make_async_copy(block_any, block_in, input_sem.at[0]))
+    stages.append(pltpu.make_async_copy(cotangent_any, cotangent, input_sem.at[1]))
     for copy in stages:
         copy.start()
     devices = fsdp_size * seq_size
@@ -613,14 +621,14 @@
     sequence_column = lax.broadcasted_iota(jnp.int32, (LANES, slots), 1)
     wanted_row, wanted_column = lax.rem(sequence_row, R), lax.rem(sequence_column, R)
     for k in range(sequences):
-        base = ids[k] * R
+        base = ids[k // ids.shape[1], k % ids.shape[1]] * R
         wanted_row += jnp.where(sequence_row // R == k, base, 0)
         wanted_column += jnp.where(sequence_column // R == k, base, 0)
     pick_t[...] = (wanted_row == lax.broadcasted_iota(jnp.int32, (slots, LANES), 1)).astype(F32).astype(BF16)
     pick[...] = (wanted_column == lax.broadcasted_iota(jnp.int32, (LANES, slots), 0)).astype(F32).astype(BF16)
     taps[...] = taps_in[...].astype(F32)
-    gain_first[...] = gain_first_in[...].astype(F32)
-    gain_second[...] = gain_second_in[...].astype(F32)
+    unroll_gain(gain_first, gain_first_in)
+    unroll_gain(gain_second, gain_second_in)
 
     def rows_of(r, size=block):
         return pl.ds(pl.multiple_of(r * size, size), size)
@@ -814,9 +822,8 @@
     sources.append(
         lambda d: column_tiles(grads, shares.rest_start, shares.per, shares.rest_used, d, devices)
     )
-    sources.append(lambda d: column_tiles(out_tiles, 0, 1, shares.left + 2 * shares.narrow, d, devices))
     sources.append(lambda d: pick_t)
-    places = (got_front.at[0], got_front.at[1], got_rest, got_out, picks)
+    places = (got_front.at[0], got_front.at[1], got_rest, picks)
     exchanges = [
         Exchange(ring, seq_size, devices, source, place, exchange_sems[k])
         for k, (source, place) in enumerate(zip(sources, places))
@@ -843,7 +850,7 @@
                 plan.list.append(functools.partial(begin, j + 1))
                 begun += 1
         if tick == (chunks - 2) * wide_blocks:
-            plan.list += [exchanges[0].start, exchanges[4].start]
+            plan.list += [exchanges[0].start, exchanges[3].start]
         if tick == (chunks - 1) * wide_blocks:
             plan.list += [load_back, exchanges[1].start]
         lists.append(plan.tick(3.9))
@@ -947,7 +954,6 @@
     for k in range(2):
         start = shares.left * LANES + k * features
         out_tiles[:, start : start + features] = out_grads[k].astype(BF16)
-    exchanges[3].start()
     for unit in unit_list[:fixed]:
         unit.drain()
 
@@ -970,7 +976,7 @@
     own = operands[-5:]
     tokens, features = cotangent.shape
     hidden_size = own[2].shape[1]
-    sequences = ids.shape[0]
+    sequences = ids.shape[0] * ids.shape[1]
     slots = sequences * R
     units = 3 + down_pieces(own[4].shape[0]) + 2 * (hidden_size // FF_CHUNK) // 3
     tall = max(tokens, features)
@@ -1004,11 +1010,11 @@
             shape(tokens, features, kind=F32),
             shape(2, shares.devices, slots, LANES),
             shape(shares.devices, slots, shares.per * LANES),
-            shape(shares.devices, slots, LANES),
+            shape(slots, (shares.left + 2 * shares.narrow) * LANES),
             shape(shares.devices, slots, LANES),
         ),
-        in_specs=[IN_VMEM] * 2 + [pl.BlockSpec(memory_space=pltpu.SMEM)] + [IN_VMEM] * 10 + [ANYWHERE] * 8,
-        out_specs=(IN_VMEM,) * 9 + (ANYWHERE,) * 15,
+        in_specs=[ANYWHERE] * 2 + [pl.BlockSpec(memory_space=pltpu.SMEM)] + [IN_VMEM] * 10 + [ANYWHERE] * 8,
+        out_specs=(IN_VMEM,) * 9 + (ANYWHERE,) * 13 + (IN_VMEM, ANYWHERE),
         scratch_shapes=unit_sems(units, fsdp_size // 2)
         + [
             pltpu.SemaphoreType.DMA((2, 5)),
@@ -1017,7 +1023,7 @@
             pltpu.SemaphoreType.DMA((2,)),
             pltpu.SemaphoreType.DMA((5,)),
         ]
-        + [pltpu.SemaphoreType.DMA((3,))] * 5
+        + [pltpu.SemaphoreType.DMA((3,))] * 4
         + [pltpu.VMEM(member.shape, BF16) for member in own]
         + [
             pltpu.VMEM((tokens, features), F32),
@@ -1044,7 +1050,9 @@
             pltpu.VMEM((1, features), F32),
             pltpu.VMEM((1, features), F32),
             pltpu.VMEM((2, slots, features), F32),
-            pltpu.VMEM((slots, (shares.left + 2 * shares.narrow) * LANES), BF16),
+            pltpu.VMEM((tokens, features), BF16),
+            pltpu.VMEM((tokens, features), BF16),
+            pltpu.SemaphoreType.DMA((2,)),
         ],
         compiler_params=pltpu.CompilerParams(
             collective_id=0, has_side_effects=True, vmem_limit_bytes=VMEM_LIMIT_FRONT
@@ -1055,18 +1063,18 @@
 def mixer_back_kernel(sizes, per_sequence, shares, *refs):
     (
         grad_after_in, grad_mixer_in, block_in_in, mixed, conv, normed_in, weight_in, low_in, in_first, in_second,
-        taps_in, gain_first_in, got_front, got_rest, got_out, picks,
+        taps_in, gain_first_in, got_front, got_rest, out_tiles, picks,
     ) = refs[:16]
     grad_input = refs[16]
-    landings = refs[17:19]
-    units_refs = refs[19:23]
-    exchange_sem, seq_sems, local_sems = refs[23], refs[24:26], refs[26:28]
-    rim_sem, load_sem = refs[28:30]
-    got_in, results = refs[30], refs[31:33]
+    landings = refs[17:20]
+    units_refs = refs[20:24]
+    exchange_sems, seq_sems, local_sems = refs[24:26], refs[26:29], refs[29:32]
+    rim_sem, load_sem = refs[32:34]
+    got_out, got_in, results = refs[34], refs[35], refs[36:39]
     (
         rim_out, rim_in, grad_after, mixed_s, conv_s, in_w, grad_mixer, grad_mixed,
         low_in_back, in_tiles, block_in, normed, taps, gain_first,
-    ) = refs[33:]
+    ) = refs[39:]
     fsdp_size, seq_size = sizes
     devices = fsdp_size * seq_size
     ring = Ring(fsdp_size)
@@ -1092,10 +1100,15 @@
     for copy in loads[:3]:
         copy.start()
     ring.greet(seq_size, devices)
-    in_exchange = Exchange(
-        ring, seq_size, devices, lambda d: column_tiles(in_tiles, 0, 1, 4 * shares.narrow, d, devices), got_in,
-        exchange_sem,
+    out_exchange, in_exchange = (
+        Exchange(
+            ring, seq_size, devices,
+            functools.partial(lambda source, d: column_tiles(source, 0, 1, source.shape[1] // LANES, d, devices), source),
+            got, exchange_sems[k],
+        )
+        for k, (source, got) in enumerate(((out_tiles, got_out), (in_tiles, got_in)))
     )
+    out_exchange.start()
     total_slots = devices * slots
     per = shares.per
 
@@ -1107,23 +1120,31 @@
     def front_first(t):
         return shares.is_first(t, me) if t < 2 else shares.is_first(2, me * per + t - 2)
 
-    def back_got(t):
-        return (got_out, got_in)[t][...].reshape(total_slots, LANES)
+    def one_got(got):
+        return lambda t: got[...].reshape(total_slots, LANES)
 
     sums = [
         Sum(ring, seq_size, k, landings[k], is_first, got, results[k], (seq_sems[k], local_sems[k]), units_refs)
         for k, (got, is_first) in enumerate(
-            ((front_got, front_first), (back_got, lambda t: shares.is_first(3 + t, me)))
+            (
+                (front_got, front_first),
+                (one_got(got_out), lambda t: shares.is_first(3, me)),
+                (one_got(got_in), lambda t: shares.is_first(4, me)),
+            )
         )
     ]
     chosen = picks[...].reshape(total_slots, LANES)
     sums[0].add(chosen)
     taps[...] = taps_in[...].astype(F32)
-    gain_first[...] = gain_first_in[...].astype(F32)
+    unroll_gain(gain_first, gain_first_in)
     parts = tokens // block
-    groups = sums[0].groups()
-    while len(groups) < 2 * parts - 1:
-        groups.append([])
+
+    def add_out():
+        out_exchange.arrived()
+        sums[1].add(chosen)
+
+    begin_all, *front_steps = sums[0].groups()
+    out_steps, in_steps = sums[1].groups(), sums[2].groups()
 
     def rows_of(r):
         return pl.ds(pl.multiple_of(r * block, block), block)
@@ -1153,11 +1174,9 @@
     rim.wait_recv()
     inner = (ring.x < seq_size - 1).astype(F32)
 
-    first_lists = share_out(groups[: parts - 1], parts - 1)
-
     @pl.loop(0, parts)
     def _(r):
-        run_tick([[]] + first_lists, r)
+        run_tick([[]] * (parts - 1) + [begin_all], r)
         at = rows_of(r)
         back = grad_mixer[at, :]
         through = back * mixed_s[at, middle]
@@ -1194,23 +1213,31 @@
 
     def add_last():
         in_exchange.arrived()
-        sums[1].add(chosen)
-
-    rest = share_out(groups[parts - 1 :], parts)
-    rest[-1] = rest[-1] + [add_last]
+        sums[2].add(chosen)
+
+    def step_of(steps, k):
+        return steps[k] if 0 <= k < len(steps) else []
+
+    rest = []
+    for k in range(len(front_steps) + len(in_steps) + parts):
+        actions = [add_last] if k == parts - 2 else []
+        actions += step_of(in_steps, k - parts + 1) + step_of(front_steps, k)
+        actions += [add_out] if k == 0 else []
+        rest.append(actions + step_of(out_steps, k - 1))
 
     @pl.loop(0, parts)
     def _(r):
-        run_tick(rest, r)
+        run_tick(rest[:parts], r)
         finish(r)
 
-    for actions in sums[1].groups():
+    for actions in rest[parts:]:
         for action in actions:
             action()
     for member in sums:
         member.unit.collect()
     for member in sums:
         member.drain()
+    out_exchange.drain()
     in_exchange.drain()
     rim.wait_send()
 
@@ -1221,20 +1248,21 @@
     tokens, features = operands[0].shape
     slots = operands[7].shape[1]
     sequences = tokens // per_sequence
-    tiles = (2 + shares.per, 2)
+    tiles = (2 + shares.per, 1, 1)
     return pl.pallas_call(
         functools.partial(mixer_back_kernel, sizes, per_sequence, shares),
         out_shape=(jax.ShapeDtypeStruct((tokens, features), BF16),)
         + tuple(jax.ShapeDtypeStruct((fsdp_size, seq_size, count, LANES, LANES), BF16) for count in tiles),
         in_specs=[ANYWHERE] * 7 + [IN_VMEM] * 9,
-        out_specs=(IN_VMEM,) + (ANYWHERE,) * 2,
-        scratch_shapes=unit_sems(2, fsdp_size // 2)
-        + [pltpu.SemaphoreType.DMA((3,))]
-        + [pltpu.SemaphoreType.DMA((2, seq_size))] * 2
-        + [pltpu.SemaphoreType.DMA((1,))] * 2
+        out_specs=(IN_VMEM,) + (ANYWHERE,) * 3,
+        scratch_shapes=unit_sems(3, fsdp_size // 2)
+        + [pltpu.SemaphoreType.DMA((3,))] * 2
+        + [pltpu.SemaphoreType.DMA((2, seq_size))] * 3
+        + [pltpu.SemaphoreType.DMA((1,))] * 3
         + [
             pltpu.SemaphoreType.DMA((2,)),
             pltpu.SemaphoreType.DMA((7,)),
+            pltpu.VMEM((devices, slots, LANES), BF16),
             pltpu.VMEM((devices, slots, LANES), BF16),
         ]
         + [pltpu.VMEM((count, LANES, LANES), BF16) for count in tiles]
@@ -1261,21 +1289,39 @@
 
 
 def spread_kernel(layout, *refs):
-    sources, outs = refs[:2], refs[2:]
-    for out, (first, runs) in zip(outs, layout):
-        for source, start, stride, offset, count in runs:
-
-            @pl.loop(0, count)
-            def _(k, source=sources[source], start=start, stride=stride, offset=offset, out=out, first=first):
-                at = pl.ds(pl.multiple_of((offset + k) * LANES, LANES), LANES)
-                tile = source[start + k * stride].astype(F32)
+    count = len(layout)
+    landings, kept, outs, kept_outs = refs[:3], refs[3:5], refs[5 : 5 + count], refs[5 + count : 7 + count]
+    sources, held = refs[7 + count : 10 + count], refs[10 + count : 12 + count]
+    staged, load_sem, out_sem = refs[12 + count : 12 + 2 * count], refs[-2], refs[-1]
+    loads = [pltpu.make_async_copy(a, b, load_sem.at[k]) for k, (a, b) in enumerate(zip(landings + kept, sources + held))]
+    for copy in loads:
+        copy.start()
+    stores = [pltpu.make_async_copy(a, b, out_sem.at[count + k]) for k, (a, b) in enumerate(zip(held, kept_outs))]
+    for copy in loads[:3]:
+        copy.wait()
+    for k, (out, (first, runs)) in enumerate(zip(staged, layout)):
+        for source, start, stride, offset, length in runs:
+
+            @pl.loop(0, length)
+            def _(j, source=sources[source], start=start, stride=stride, offset=offset, out=out, first=first):
+                at = pl.ds(pl.multiple_of((offset + j) * LANES, LANES), LANES)
+                tile = source[start + j * stride].astype(F32)
                 if first:
                     out[at, :] = tile
                 else:
                     out[:, at] = tile
 
-
-def spread(shares, landings):
+        stores.append(pltpu.make_async_copy(out, outs[k], out_sem.at[k]))
+        stores[-1].start()
+        if k == 1:
+            for j in range(2):
+                loads[3 + j].wait()
+                stores[j].start()
+    for copy in stores:
+        copy.wait()
+
+
+def spread(shares, landings, kept):
     wide, narrow = shares.wide, shares.narrow
     places = shares.places()
     layout, shapes = [], []
@@ -1304,13 +1350,17 @@
         first = name.endswith("first")
         layout.append((first, tuple(runs)))
         shapes.append(jax.ShapeDtypeStruct((count * LANES, LANES) if first else (LANES, count * LANES), F32))
+    landings = [landing.reshape(-1, LANES, LANES) for landing in landings]
+    kept_shapes = [jax.ShapeDtypeStruct(member.shape, member.dtype) for member in kept]
     return pl.pallas_call(
         functools.partial(spread_kernel, tuple(layout)),
-        out_shape=tuple(shapes),
-        in_specs=[IN_VMEM] * 2,
-        out_specs=(IN_VMEM,) * len(shapes),
+        out_shape=tuple(shapes + kept_shapes),
+        in_specs=[ANYWHERE] * 5,
+        out_specs=(ANYWHERE,) * (len(shapes) + 2),
+        scratch_shapes=[pltpu.VMEM(member.shape, member.dtype) for member in (*landings, *kept, *shapes)]
+        + [pltpu.SemaphoreType.DMA((5,)), pltpu.SemaphoreType.DMA((len(shapes) + 2,))],
         compiler_params=pltpu.CompilerParams(vmem_limit_bytes=VMEM_LIMIT),
-    )(*(landing.reshape(-1, LANES, LANES) for landing in landings))
+    )(*landings, *kept)
 
 
 def per_device(
@@ -1342,13 +1392,13 @@
     fsdp_size, seq_size = lax.axis_size("fsdp"), lax.axis_size("seq")
     hidden_size = gate_weight.shape[1]
     shares = Shares(fsdp_size * seq_size, features, hidden_size)
-    gain_first, gain_second = first_gain[None, :], second_gain[None, :]
+    gain_first, gain_second = (gain.reshape(-1, LANES) for gain in (first_gain, second_gain))
     cotangent = output_grad.reshape(tokens, features)
     block_in = block_input.reshape(tokens, features)
     (
         grad_after, _, low_in, _, in_first, in_second, _, _, _,
         block_output, _, mixed_in, conv_out, _, normed, weight_in, _, _, _,
-        grad_mixer, got_front, got_rest, got_out, picks,
+        grad_mixer, got_front, got_rest, out_tiles, picks,
     ) = front(
         (fsdp_size, seq_size),
         local_len,
@@ -1356,7 +1406,7 @@
         (
             block_in,
             cotangent,
-            adapter_ids.reshape(sequences),
+            adapter_ids,
             conv_weight,
             gain_first,
             gain_second,
@@ -1396,12 +1446,13 @@
             gain_first,
             got_front,
             got_rest,
-            got_out,
+            out_tiles,
             picks,
         ),
     )
+    *gradients, block_output, grad_input = spread(shares, landings, (block_output, grad_input))
     shape = block_input.shape
-    return (block_output.reshape(shape), grad_input.reshape(shape)) + tuple(spread(shares, landings))
+    return (block_output.reshape(shape), grad_input.reshape(shape)) + tuple(gradients)
 
 
 def solution(mesh):

time: 302 us -> 287 us (0.950)
  Pallas kernels: 294 us -> 284 us
  local copies, waits for them, and re-layouts: 7.11 us -> 1.3 us
    pallas_call x1, Pallas kernels: 218 us -> 209 us  [front(): pl.pallas_call(functools.partial(front_kernel, sizes, per_sequence, share...]
    unnamed x4 -> x1, local copies, waits for them, and re-layouts: 4.55 us -> 1.3 us
where the time goes in v6:
time: 287 us; the launch traced here: 286 us
  Pallas kernels  284 us (99%)
    pallas_call x1, Pallas kernels, front(): pl.pallas_call(functools.partial(front_kernel, sizes, per_sequence, share...  209 us
    pallas_call x1, Pallas kernels, mixer_back(): pl.pallas_call(functools.partial(mixer_back_kernel, sizes, per_sequence,...  66 us
    pallas_call x1, Pallas kernels, spread(): pl.pallas_call(functools.partial(spread_kernel, tuple(layout)), out_shape...  8.92 us

profile of v6, /device:TPU:0, one launch (start us, length us, event | category | flops | bytes accessed | tf_op | source)
XLA Modules:
  0.0 285.7 jit_solution(13947657806220420181)
XLA Ops:
  0.6 1.3 copy.33.refs_2_
  1.9 208.6 %shard_map.292 = (f32[1024,1024]{1,0:T(8,128)}, bf16[32,17920]{1,0:T(8,128)(2,1)}, bf16[1024,32]{1,0:T(8,128)(2,1)}, bf16[1024,32]{1,0:T(8,128)(2,1)}, bf16[1024...) custom-call(bf16[1024,1024]{1,0:T(8,128)(2,1)} %bitcast.13, ...), custom_call_target="tpu_custom_call" | custom-call | tf_op jit(solution)/shard_map/pallas_call | solution.py:988
  210.6 66.0 %shard_map.293 = (bf16[1024,1024]{1,0:T(8,128)(2,1)}, bf16[16,2,4,128,128]{4,3,2,1,0:T(8,128)(2,1)}, bf16[16,2,1,128,128]{4,3,2,1,0:T(8,128)(2,1)}, bf16[16,2,1,128,128]{4,3,2,1,0:T(8,128)(2,1)}) custom-call(f32[1024,1024]{1,0:T(8,128)} %get-tuple-element.42.refs_0_, f32[1024,1024]{1,0:T(8,128)} %get-tuple-element.43.refs_1_, bf16[1024,1024]{1,0:T(8,128)(2,1)} %bitcast.14, ...), custom_call_target="tpu_custom_call" | custom-call | tf_op jit(solution)/shard_map/pallas_call | solution.py:1252
  276.6 8.9 %shard_map.294 = (f32[1024,128]{1,0:T(8,128)}, f32[128,3072]{1,0:T(8,128)}, f32[1024,128]{1,0:T(8,128)}, f32[128,1024]{1,0:T(8,128)}, f32[1024,128]{1,0:T(8,128)...) custom-call(bf16[128,128,128]{2,1,0:T(8,128)(2,1)} %bitcast.15, ...), custom_call_target="tpu_custom_call" | custom-call | tf_op jit(solution)/shard_map/pallas_call | solution.py:1355

commit v7 on v6

--- a/solution.py
+++ b/solution.py
@@ -279,8 +279,8 @@
 
 
 class Plan:
-    LINK, CORE, DELAY, COST = 37e3, 200e3, 1.7, 0.25
-    WINDOWS = (4, 8, 1.5, 6, 1.5, 4, 1, 8, 1, 3, 2, 2)
+    LINK, CORE, DELAY, COST = 41e3, 200e3, 2.0, 0.15
+    WINDOWS = (2, 10, 5, 2, 1.5, 10, 2, 4, 1.5, 1.5, 1.5, 8)
 
     def __init__(self, units, sizes):
         self.units, self.sizes = units, sizes
@@ -462,7 +462,7 @@
         for number, tiles in enumerate(self.sets):
             for k, tile in enumerate(tiles):
                 if number == 2:
-                    found[tile] = (0, (2 + self.per) * (k // self.per) + 2 + k % self.per)
+                    found[tile] = (0, (2 + self.per) * (k % self.devices) + 2 + k // self.devices)
                 else:
                     found[tile] = (0, (2 + self.per) * k + number) if number < 2 else (number - 2, k)
         return found
@@ -489,7 +489,7 @@
     def add(self, chosen):
         tiles = self.result.shape[0]
         for t in range(tiles):
-            tile = dot_tn(chosen, self.got(t))
+            tile = dot_nn(chosen, self.got(t))
             self.result[t] = jnp.where(self.is_first(t), tile.T, tile).astype(BF16)
         store = pltpu.make_async_copy(self.result, self.place, self.local_sem.at[0])
         store.start()
@@ -541,13 +541,13 @@
         grad_mixer_out, got_front, got_rest, out_tiles, picks,
     ) = refs[21:45]
     sems, local_sem, load_sem, stage_sem, rim_sem, out_sem = refs[45:49], refs[49], refs[50], refs[51], refs[52], refs[53]
-    exchange_sems = refs[54:58]
-    held = refs[58:63]
+    exchange_sems = refs[54 : 57 + shares.per]
+    held = refs[57 + shares.per : 62 + shares.per]
     pick, taps, gain_first, gain_second, out_grads, block_in, cotangent, input_sem = refs[-8:]
     (
         total, wide, gate_w, up_w, down_w, normed, mixer, second, gate_up_first, first_down, second_gu, second_down,
         low_gu, grad_low_down, low_down, grad_low_gu, partial, rim_out, rim_in,
-    ) = refs[63:-8]
+    ) = refs[62 + shares.per : -8]
     fsdp_size, seq_size = sizes
     ring = Ring(fsdp_size)
     rows, down_rows = gate_own.shape[0], down_own.shape[0]
@@ -819,11 +819,17 @@
         return lambda d: column_tiles(grads, start, 1, shares.used, d, devices)
 
     sources = [tile_columns(k * shares.pitch) for k in range(2)]
-    sources.append(
-        lambda d: column_tiles(grads, shares.rest_start, shares.per, shares.rest_used, d, devices)
-    )
+    for k in range(shares.per):
+        sources.append(
+            functools.partial(
+                lambda k, d: column_tiles(
+                    grads, shares.rest_start + k * devices, 1, min(devices, shares.rest_used), d, devices
+                ),
+                k,
+            )
+        )
     sources.append(lambda d: pick_t)
-    places = (got_front.at[0], got_front.at[1], got_rest, picks)
+    places = [got_front.at[0], got_front.at[1]] + [got_rest.at[k] for k in range(shares.per)] + [picks]
     exchanges = [
         Exchange(ring, seq_size, devices, source, place, exchange_sems[k])
         for k, (source, place) in enumerate(zip(sources, places))
@@ -850,7 +856,7 @@
                 plan.list.append(functools.partial(begin, j + 1))
                 begun += 1
         if tick == (chunks - 2) * wide_blocks:
-            plan.list += [exchanges[0].start, exchanges[3].start]
+            plan.list += [exchanges[0].start, exchanges[-1].start]
         if tick == (chunks - 1) * wide_blocks:
             plan.list += [load_back, exchanges[1].start]
         lists.append(plan.tick(3.9))
@@ -895,6 +901,9 @@
                 grads[:, place] = partial[k].astype(BF16)
 
     normed_store.wait()
+    ready = 1 if shares.per > 1 and devices <= 3 * shares.per_chunk else 0
+    for member in exchanges[2 : 2 + ready]:
+        member.start()
     rest_tiles = shares.rest_start + 3 * shares.per_chunk
     base = rest_tiles * LANES
 
@@ -922,7 +931,8 @@
             spare = (k * shares.pitch + shares.used) * LANES
             grads[:, start : start + width] = grads[:, spare : spare + width]
             start += width
-    exchanges[2].start()
+    for member in exchanges[2 + ready : 2 + shares.per]:
+        member.start()
 
     for copy in back_loads:
         copy.wait()
@@ -1009,7 +1019,7 @@
             shape(hidden_size, features),
             shape(tokens, features, kind=F32),
             shape(2, shares.devices, slots, LANES),
-            shape(shares.devices, slots, shares.per * LANES),
+            shape(shares.per, shares.devices, slots, LANES),
             shape(slots, (shares.left + 2 * shares.narrow) * LANES),
             shape(shares.devices, slots, LANES),
         ),
@@ -1023,7 +1033,7 @@
             pltpu.SemaphoreType.DMA((2,)),
             pltpu.SemaphoreType.DMA((5,)),
         ]
-        + [pltpu.SemaphoreType.DMA((3,))] * 4
+        + [pltpu.SemaphoreType.DMA((3,))] * (3 + shares.per)
         + [pltpu.VMEM(member.shape, BF16) for member in own]
         + [
             pltpu.VMEM((tokens, features), F32),
@@ -1073,7 +1083,7 @@
     got_out, got_in, results = refs[34], refs[35], refs[36:39]
     (
         rim_out, rim_in, grad_after, mixed_s, conv_s, in_w, grad_mixer, grad_mixed,
-        low_in_back, in_tiles, block_in, normed, taps, gain_first,
+        low_in_back, in_tiles, block_in, normed, taps, gain_first, chosen_t,
     ) = refs[39:]
     fsdp_size, seq_size = sizes
     devices = fsdp_size * seq_size
@@ -1110,15 +1120,14 @@
     )
     out_exchange.start()
     total_slots = devices * slots
-    per = shares.per
 
     def front_got(t):
         if t < 2:
             return got_front[t].reshape(total_slots, LANES)
-        return got_rest[:, :, (t - 2) * LANES : (t - 1) * LANES].reshape(total_slots, LANES)
+        return got_rest[t - 2].reshape(total_slots, LANES)
 
     def front_first(t):
-        return shares.is_first(t, me) if t < 2 else shares.is_first(2, me * per + t - 2)
+        return shares.is_first(t, me) if t < 2 else shares.is_first(2, me + (t - 2) * devices)
 
     def one_got(got):
         return lambda t: got[...].reshape(total_slots, LANES)
@@ -1133,7 +1142,8 @@
             )
         )
     ]
-    chosen = picks[...].reshape(total_slots, LANES)
+    chosen_t[...] = picks[...].reshape(total_slots, LANES).astype(F32).T.astype(BF16)
+    chosen = chosen_t[...]
     sums[0].add(chosen)
     taps[...] = taps_in[...].astype(F32)
     unroll_gain(gain_first, gain_first_in)
@@ -1141,7 +1151,7 @@
 
     def add_out():
         out_exchange.arrived()
-        sums[1].add(chosen)
+        sums[1].add(chosen_t[...])
 
     begin_all, *front_steps = sums[0].groups()
     out_steps, in_steps = sums[1].groups(), sums[2].groups()
@@ -1213,7 +1223,7 @@
 
     def add_last():
         in_exchange.arrived()
-        sums[2].add(chosen)
+        sums[2].add(chosen_t[...])
 
     def step_of(steps, k):
         return steps[k] if 0 <= k < len(steps) else []
@@ -1281,6 +1291,7 @@
             pltpu.VMEM((tokens, features), BF16),
             pltpu.VMEM((3, features), F32),
             pltpu.VMEM((1, features), F32),
+            pltpu.VMEM((LANES, devices * slots), BF16),
         ],
         compiler_params=pltpu.CompilerParams(
             collective_id=2, has_side_effects=True, vmem_limit_bytes=VMEM_LIMIT_FRONT

time: 287 us -> 282 us (0.983)
  Pallas kernels: 284 us -> 279 us
    pallas_call x1, Pallas kernels: 66 us -> 61.6 us  [mixer_back(): pl.pallas_call(functools.partial(mixer_back_kernel, sizes, per_sequence,...]
where the time goes in v7:
time: 282 us; the launch traced here: 281 us
  Pallas kernels  279 us (99%)
    pallas_call x1, Pallas kernels, front(): pl.pallas_call(functools.partial(front_kernel, sizes, per_sequence, share...  208 us
    pallas_call x1, Pallas kernels, mixer_back(): pl.pallas_call(functools.partial(mixer_back_kernel, sizes, per_sequence,...  61.6 us
    pallas_call x1, Pallas kernels, spread(): pl.pallas_call(functools.partial(spread_kernel, tuple(layout)), out_shape...  8.92 us

profile of v7, /device:TPU:0, one launch (start us, length us, event | category | flops | bytes accessed | tf_op | source)
XLA Modules:
  0.0 280.7 jit_solution(17894493173889510048)
XLA Ops:
  0.6 1.3 copy.33.refs_2_
  1.9 208.1 %shard_map.292 = (f32[1024,1024]{1,0:T(8,128)}, bf16[32,17920]{1,0:T(8,128)(2,1)}, bf16[1024,32]{1,0:T(8,128)(2,1)}, bf16[1024,32]{1,0:T(8,128)(2,1)}, bf16[1024...) custom-call(bf16[1024,1024]{1,0:T(8,128)(2,1)} %bitcast.13, ...), custom_call_target="tpu_custom_call" | custom-call | tf_op jit(solution)/shard_map/pallas_call | solution.py:998
  210.0 61.6 %shard_map.293 = (bf16[1024,1024]{1,0:T(8,128)(2,1)}, bf16[16,2,4,128,128]{4,3,2,1,0:T(8,128)(2,1)}, bf16[16,2,1,128,128]{4,3,2,1,0:T(8,128)(2,1)}, bf16[16,2,1,128,128]{4,3,2,1,0:T(8,128)(2,1)}) custom-call(f32[1024,1024]{1,0:T(8,128)} %get-tuple-element.42.refs_0_, f32[1024,1024]{1,0:T(8,128)} %get-tuple-element.43.refs_1_, bf16[1024,1024]{1,0:T(8,128)(2,1)} %bitcast.14, ...), custom_call_target="tpu_custom_call" | custom-call | tf_op jit(solution)/shard_map/pallas_call | solution.py:1262
  271.6 8.9 %shard_map.294 = (f32[1024,128]{1,0:T(8,128)}, f32[128,3072]{1,0:T(8,128)}, f32[1024,128]{1,0:T(8,128)}, f32[128,1024]{1,0:T(8,128)}, f32[1024,128]{1,0:T(8,128)...) custom-call(bf16[128,128,128]{2,1,0:T(8,128)(2,1)} %bitcast.15, ...), custom_call_target="tpu_custom_call" | custom-call | tf_op jit(solution)/shard_map/pallas_call | solution.py:1366

commit v8 on v7

--- a/solution.py
+++ b/solution.py
@@ -621,7 +621,7 @@
     sequence_column = lax.broadcasted_iota(jnp.int32, (LANES, slots), 1)
     wanted_row, wanted_column = lax.rem(sequence_row, R), lax.rem(sequence_column, R)
     for k in range(sequences):
-        base = ids[k // ids.shape[1], k % ids.shape[1]] * R
+        base = ids[k % ids.shape[0], k // ids.shape[0]] * R
         wanted_row += jnp.where(sequence_row // R == k, base, 0)
         wanted_column += jnp.where(sequence_column // R == k, base, 0)
     pick_t[...] = (wanted_row == lax.broadcasted_iota(jnp.int32, (slots, LANES), 1)).astype(F32).astype(BF16)
@@ -1417,7 +1417,7 @@
         (
             block_in,
             cotangent,
-            adapter_ids,
+            adapter_ids.T,
             conv_weight,
             gain_first,
             gain_second,

time: 282 us -> 281 us (level)
  no operation moved by 1% of the time
where the time goes in v8:
time: 281 us; the launch traced here: 279 us
  Pallas kernels  279 us (99%)
    pallas_call x1, Pallas kernels, front(): pl.pallas_call(functools.partial(front_kernel, sizes, per_sequence, share...  208 us
    pallas_call x1, Pallas kernels, mixer_back(): pl.pallas_call(functools.partial(mixer_back_kernel, sizes, per_sequence,...  61.6 us
    pallas_call x1, Pallas kernels, spread(): pl.pallas_call(functools.partial(spread_kernel, tuple(layout)), out_shape...  8.92 us

profile of v8, /device:TPU:0, one launch (start us, length us, event | category | flops | bytes accessed | tf_op | source)
XLA Modules:
  0.0 279.5 jit_solution(8125276201385437359)
XLA Ops:
  0.7 208.1 %shard_map.292 = (f32[1024,1024]{1,0:T(8,128)}, bf16[32,17920]{1,0:T(8,128)(2,1)}, bf16[1024,32]{1,0:T(8,128)(2,1)}, bf16[1024,32]{1,0:T(8,128)(2,1)}, bf16[1024...) custom-call(bf16[1024,1024]{1,0:T(8,128)(2,1)} %bitcast.14, ...), custom_call_target="tpu_custom_call" | custom-call | tf_op jit(solution)/shard_map/pallas_call | solution.py:998
  208.8 61.6 %shard_map.293 = (bf16[1024,1024]{1,0:T(8,128)(2,1)}, bf16[16,2,4,128,128]{4,3,2,1,0:T(8,128)(2,1)}, bf16[16,2,1,128,128]{4,3,2,1,0:T(8,128)(2,1)}, bf16[16,2,1,128,128]{4,3,2,1,0:T(8,128)(2,1)}) custom-call(f32[1024,1024]{1,0:T(8,128)} %get-tuple-element.42.refs_0_, f32[1024,1024]{1,0:T(8,128)} %get-tuple-element.43.refs_1_, bf16[1024,1024]{1,0:T(8,128)(2,1)} %bitcast.15, ...), custom_call_target="tpu_custom_call" | custom-call | tf_op jit(solution)/shard_map/pallas_call | solution.py:1262
  270.4 8.9 %shard_map.294 = (f32[1024,128]{1,0:T(8,128)}, f32[128,3072]{1,0:T(8,128)}, f32[1024,128]{1,0:T(8,128)}, f32[128,1024]{1,0:T(8,128)}, f32[1024,128]{1,0:T(8,128)...) custom-call(bf16[128,128,128]{2,1,0:T(8,128)(2,1)} %bitcast.16, ...), custom_call_target="tpu_custom_call" | custom-call | tf_op jit(solution)/shard_map/pallas_call | solution.py:1366
